TPU v7x, 128 devices: a whole 4x4x4 slice. The times are simulated.
128 devices in a mesh: dp: 16 (over x, y_hi, core), mp: 8 (over y_lo, z).
Axes of the slice: x: 4, y: 4 (y_hi: 2, y_lo: 2; y = y_hi * 2 + y_lo), z: 4, core: 2. Of those that a mesh axis runs over, the one named last changes fastest.
Arguments:
- clean_image: bfloat16 [8, 588, 128], P('mp'), may hold values from -6 to 6
- noise_draw: bfloat16 [8, 16, 588, 128], P('mp', 'dp'), may hold values from -6 to 6
- embed_weight: bfloat16 [588, 6144], P(None, 'dp'), may hold values from -0.25 to 0.25
- position_table: bfloat16 [128, 6144], replicated, may hold values from -3 to 3
- norm_gain: float32 [6144], replicated, may hold values from 0.1 to 1.9
- qkv_weight: bfloat16 [6144, 3, 3072], P(None, None, 'mp'), may hold values from -0.078125 to 0.078125
- query_gain: float32 [128], replicated, may hold values from 0.1 to 1.9
- key_gain: float32 [128], replicated, may hold values from 0.1 to 1.9
- out_weight: bfloat16 [3072, 6144], P('mp'), may hold values from -0.375 to 0.375
Outputs:
- features: bfloat16 [128, 16, 8, 6144], P(None, 'dp', 'mp')
- smoothed: float32 [128, 8, 6144], P(None, 'mp', 'dp')
All inputs are finite; a program needn't handle non-finite values.
Results may differ from a plain program's by a relative error of at most 0.017.
Values may be sent and summed in bfloat16 or wider, within the bound.
No kernel may reach another device: no remote copies, remote signals or barrier semaphores. Data moves between devices by JAX's collectives and lax.ppermute only.
A program may use at most 128 MiB of HBM per device.

v0:
```python
import jax
import jax.numpy as jnp
from jax import lax
from jax.experimental import pallas as pl
from jax.experimental.pallas import tpu as pltpu
from jax.sharding import Mesh
from jax.sharding import PartitionSpec as P


HEAD_DIM = 128
epsilon = 1e-06
bf16 = jnp.bfloat16
f32 = jnp.float32

AXES = ("x", "yh", "core", "yl", "z")
GROUP = ("x", "core")
DP = ("x", "yh", "core")
MP = ("yl", "z")
PIECES = 8
PIX_ROWS = 80
POS_ROWS = 16
ROWS = PIX_ROWS + POS_ROWS


def device_id(xc, yh, m):
    return (((xc // 2) * 2 + yh) * 2 + xc % 2) * 8 + m


def everyone():
    return [(xc, yh, m) for xc in range(8) for yh in range(2) for m in range(8)]


def send(array, target):
    pairs = [(device_id(*s), device_id(*target(*s))) for s in everyone()]
    return lax.ppermute(array, AXES, pairs)


def pixel_pieces(rows):
    k, n = rows.shape
    return jnp.pad(rows, ((0, PIECES * PIX_ROWS - k), (0, 0))).reshape(PIECES, PIX_ROWS, n)


def extended(pixel_rows, pos_rows):
    n = pixel_rows.shape[1]
    both = [pixel_pieces(pixel_rows), pos_rows.reshape(PIECES, POS_ROWS, n)]
    return jnp.concatenate(both, axis=1).reshape(PIECES * ROWS, n)


def dot(left, right, dims):
    return lax.dot_general(left, right, (dims, ((), ())), preferred_element_type=f32)


def join_kernel(piece_ref, pixel_ref, pos_all_ref, pos_ref, gain_ref, qkv_ref, out_ref, mean_ref, acc_ref):
    step = pl.program_id(0)
    shares, _, cols = pixel_ref.shape
    width = shares * cols

    @pl.when(step == 0)
    def _():
        total = jnp.zeros((PIX_ROWS, HEAD_DIM), f32)
        for k in range(shares):
            for j in range(cols // HEAD_DIM):
                total += pixel_ref[k, :, j * HEAD_DIM : (j + 1) * HEAD_DIM].astype(f32)
        total_pos = jnp.sum(pos_all_ref[...].astype(f32), axis=1, keepdims=True)
        total = jnp.sum(total, axis=1, keepdims=True)
        mean_ref[:PIX_ROWS] = jnp.broadcast_to(total * (1.0 / width), (PIX_ROWS, HEAD_DIM))
        mean_ref[PIX_ROWS:] = jnp.broadcast_to(total_pos * (1.0 / width), (POS_ROWS, HEAD_DIM))
        acc_ref[...] = jnp.zeros_like(acc_ref)

    per_step = qkv_ref.shape[1] // cols
    pixels = jnp.concatenate([pixel_ref[per_step * step + k] for k in range(per_step)], axis=1)
    rows = jnp.concatenate([pixels.astype(f32), pos_ref[...].astype(f32)], axis=0)
    centred = ((rows - mean_ref[:, :1]) * gain_ref[...]).astype(bf16)
    qkv = jnp.concatenate([qkv_ref[t] for t in range(3)], axis=1)
    acc_ref[...] += dot(centred, qkv, ((1,), (0,)))

    @pl.when(step == pl.num_programs(0) - 1)
    def _():
        out_ref[...] = acc_ref[...].astype(bf16)


def join_weights(piece, pixel_rows, position_table, gain, qkv):
    shares, _, cols = pixel_rows.shape
    width, group_cols = qkv.shape[1:]
    per_step = 2
    return pl.pallas_call(
        join_kernel,
        out_shape=jax.ShapeDtypeStruct((ROWS, 3 * group_cols), bf16),
        grid_spec=pltpu.PrefetchScalarGridSpec(
            num_scalar_prefetch=1,
            grid=(shares // per_step,),
            in_specs=[
                pl.BlockSpec((shares, PIX_ROWS, cols), lambda i, p: (0, 0, 0)),
                pl.BlockSpec((POS_ROWS, width), lambda i, p: (p[0], 0)),
                pl.BlockSpec((POS_ROWS, per_step * cols), lambda i, p: (p[0], i)),
                pl.BlockSpec((1, per_step * cols), lambda i, p: (0, i)),
                pl.BlockSpec((3, per_step * cols, group_cols), lambda i, p: (0, i, 0)),
            ],
            out_specs=pl.BlockSpec((ROWS, 3 * group_cols), lambda i, p: (0, 0)),
            scratch_shapes=[
                pltpu.VMEM((ROWS, HEAD_DIM), f32),
                pltpu.VMEM((ROWS, 3 * group_cols), f32),
            ],
        ),
        cost_estimate=pl.CostEstimate(
            flops=6 * width * ROWS * group_cols,
            transcendentals=0,
            bytes_accessed=6 * width * group_cols,
        ),
        name="join_weights",
    )(piece, pixel_rows, position_table, position_table, gain, qkv)


def head_norm(raw, scale, gain):
    average = jnp.mean(raw, axis=-1, keepdims=True)
    centred = raw - average
    variance = jnp.mean(centred * centred, axis=-1, keepdims=True)
    return (centred * (scale * lax.rsqrt(variance * scale * scale + epsilon)) * gain).astype(bf16)


def attention_kernel(
    lhs_ref, query_w_ref, key_w_ref, value_w_ref, scale_ref, query_gain_ref, key_gain_ref, out_ref, proj_ref
):
    copies, patches, rows = lhs_ref.shape
    weights = jnp.concatenate([query_w_ref[...], key_w_ref[...], value_w_ref[...]], axis=1)
    proj_ref[...] = dot(lhs_ref[...].reshape(copies * patches, rows), weights, ((1,), (0,)))
    diagonal = lax.broadcasted_iota(jnp.int32, (patches, patches), 0) == lax.broadcasted_iota(
        jnp.int32, (patches, patches), 1
    )
    for c in range(copies):
        here = slice(c * patches, (c + 1) * patches)
        scale_row = jnp.broadcast_to(scale_ref[c : c + 1, :], (patches, patches))
        scale = jnp.sum(jnp.where(diagonal, scale_row, 0.0), axis=1, keepdims=True)
        query = head_norm(proj_ref[here, :HEAD_DIM], scale, query_gain_ref[...])
        key_vec = head_norm(proj_ref[here, HEAD_DIM : 2 * HEAD_DIM], scale, key_gain_ref[...])
        value = (proj_ref[here, 2 * HEAD_DIM :] * scale).astype(bf16)
        exp_scores = jnp.exp(dot(query, key_vec, ((1,), (1,))) * HEAD_DIM ** (-0.5))
        probs = (exp_scores / jnp.sum(exp_scores, axis=-1, keepdims=True)).astype(bf16)
        out_ref[c] = dot(probs, value, ((1,), (0,))).astype(bf16)


def attend(lhs, joined, scale, query_gain, key_gain):
    copies, patches, rows = lhs.shape
    group_cols = joined.shape[1] // 3
    heads = group_cols // HEAD_DIM
    return pl.pallas_call(
        attention_kernel,
        out_shape=jax.ShapeDtypeStruct((copies, patches, group_cols), bf16),
        grid=(heads,),
        in_specs=[
            pl.BlockSpec((copies, patches, rows), lambda h: (0, 0, 0)),
            pl.BlockSpec((rows, HEAD_DIM), lambda h: (0, h)),
            pl.BlockSpec((rows, HEAD_DIM), lambda h: (0, heads + h)),
            pl.BlockSpec((rows, HEAD_DIM), lambda h: (0, 2 * heads + h)),
            pl.BlockSpec((copies, patches), lambda h: (0, 0)),
            pl.BlockSpec((1, HEAD_DIM), lambda h: (0, 0)),
            pl.BlockSpec((1, HEAD_DIM), lambda h: (0, 0)),
        ],
        out_specs=pl.BlockSpec((copies, patches, HEAD_DIM), lambda h: (0, 0, h)),
        scratch_shapes=[pltpu.VMEM((copies * patches, 3 * HEAD_DIM), f32)],
        cost_estimate=pl.CostEstimate(
            flops=4 * copies * rows * patches * group_cols * 3,
            transcendentals=copies * patches * group_cols,
            bytes_accessed=20 * copies * patches * group_cols,
        ),
        name="attend",
    )(lhs, joined, joined, joined, scale, query_gain[None], key_gain[None])


def assemble_kernel(in_ref, out_ref):
    cores, halves, _, cols = in_ref.shape
    for yb in range(halves):
        for c in range(cores):
            start = (yb * cores + c) * cols
            out_ref[:, start : start + cols] = in_ref[c, yb]


def assemble(moved):
    shares, halves, patches, cols = moved.shape
    return pl.pallas_call(
        assemble_kernel,
        out_shape=jax.ShapeDtypeStruct((patches, shares * halves * cols), bf16),
        grid=(shares // 2,),
        in_specs=[pl.BlockSpec((2, halves, patches, cols), lambda i: (i, 0, 0, 0))],
        out_specs=pl.BlockSpec((patches, 2 * halves * cols), lambda i: (0, i)),
        name="assemble",
    )(moved)


def block(
    clean_image,
    noise_draw,
    embed_weight,
    position_table,
    norm_gain,
    qkv_weight,
    query_gain,
    key_gain,
    out_weight,
):
    xi, yhi, ci = (lax.axis_index(a) for a in ("x", "yh", "core"))
    patches, width = position_table.shape
    cols = embed_weight.shape[1]
    shares = width // cols

    def my_columns(array):
        start = (xi * 4 + ci) * cols
        return [
            lax.dynamic_slice_in_dim(array, start + yb * 2 * cols, cols, axis=1) for yb in range(2)
        ]

    noisy = (clean_image[0].astype(f32) + 0.5 * noise_draw[0, 0].astype(f32)).astype(bf16)
    lhs_own = extended(noisy, jnp.eye(patches, dtype=bf16)).T
    lhs = lax.all_gather(lhs_own, GROUP)

    mine = pixel_pieces(embed_weight).reshape(4, 1, 2, PIX_ROWS, cols)
    mine = jnp.broadcast_to(mine, (4, 2, 2, PIX_ROWS, cols)).reshape(shares, PIX_ROWS, cols)
    pixel_rows = lax.all_to_all(mine, DP, 0, 0, tiled=True)
    out_mine = jnp.stack(my_columns(out_weight))
    out_mine = jnp.broadcast_to(out_mine[None], (8, *out_mine.shape))
    out_mine, pixel_rows, own_weight = lax.optimization_barrier((out_mine, pixel_rows, embed_weight))
    piece = join_weights(
        (2 * xi + ci).astype(jnp.int32).reshape(1),
        pixel_rows,
        position_table,
        norm_gain[None],
        jnp.transpose(qkv_weight, (1, 0, 2)),
    )
    piece = send(piece, lambda xc, yh, m: (m, yh, xc))
    joined = jnp.broadcast_to(piece[None], (8, *piece.shape))
    joined = lax.all_to_all(joined, MP, 0, 0, tiled=True).reshape(8 * ROWS, -1)

    other_weight = lax.ppermute(own_weight, "yh", [(0, 1), (1, 0)])
    first = jnp.where(yhi == 0, embed_weight, other_weight)
    second = jnp.where(yhi == 0, other_weight, embed_weight)
    weight_two = extended(
        jnp.concatenate([first, second], axis=1),
        jnp.concatenate(my_columns(position_table), axis=1),
    )
    embedded = jnp.einsum("cpk,kd->cpd", lhs, weight_two, preferred_element_type=f32)

    average = jnp.mean(embedded, axis=-1)
    spread = jnp.mean(jnp.square(embedded - average[..., None]), axis=-1)
    stat = jnp.stack([average, spread])
    stats = [stat]
    for k in range(1, 8):
        stats.append(send(stat, lambda xc, yh, m, k=k: (xc ^ k, yh, m)))
    average = sum(each[0] for each in stats) * 0.125
    spread = sum(each[1] + jnp.square(each[0] - average) for each in stats) * 0.125
    scale = lax.rsqrt(spread + epsilon)

    out_mine, joined = lax.optimization_barrier((out_mine, joined))
    out_all = lax.all_to_all(out_mine, MP, 0, 0, tiled=True)

    head_out = attend(lhs, joined, scale, query_gain, key_gain)
    head_out = head_out.reshape(8 * patches, -1)
    head_all = lax.all_gather(head_out, GROUP)
    halves = []
    for yb in range(2):
        attention = jnp.einsum("gtc,gcd->td", head_all, out_all[:, yb], preferred_element_type=f32)
        halves.append(
            embedded[:, :, yb * cols : (yb + 1) * cols] + attention.reshape(8, patches, cols)
        )
    output = jnp.stack(halves, axis=1)

    summed = jnp.sum(output, axis=0) * (1.0 / 16)
    kept = jnp.where(yhi == 0, summed[0], summed[1])
    sent = jnp.where(yhi == 0, summed[1], summed[0])
    smoothed = (kept + lax.ppermute(sent, "yh", [(0, 1), (1, 0)]))[:, None, :]

    moved = lax.all_to_all(output.astype(bf16), GROUP, 0, 0, tiled=True)
    features = assemble(moved).reshape(patches, 1, 1, width)
    return features, smoothed


def solution(mesh):
    fine = Mesh(mesh.devices.reshape(4, 2, 2, 2, 4), AXES)
    placed = (
        P(MP, None, None),
        P(MP, DP, None, None),
        P(None, DP),
        P(),
        P(),
        P(None, None, MP),
        P(),
        P(),
        P(MP, None),
    )
    return jax.shard_map(
        block,
        mesh=fine,
        in_specs=placed,
        out_specs=(P(None, DP, MP, None), P(None, MP, DP)),
        check_vma=False,
    )
```

profile of v0, /device:TPU:1, one launch (start us, length us, event | category | flops | bytes accessed | tf_op | source)
XLA Modules:
  0.0 222.3 jit_solution(16407481444769123102)
XLA Ops:
  7.2 0.0 all-gather.6.cloned.1.call-start
  7.2 0.1 fusion.10
  7.3 1.0 fusion.9
  8.4 0.7 pad_maximum_fusion.3
  9.1 1.1 pad.13
  10.2 1.0 broadcast_in_dim.34
  11.2 8.4 %all-to-all-start = ((bf16[16,80,384]{2,1,0:T(8,128)(2,1)}), bf16[16,80,384]{2,1,0:T(8,128)(2,1)S(1)}, u32[]{:S(2)}, u32[]{:S(2)}) async-start(bf16[16,80,384]{2,1,0:T(8,128)(2,1)} %bitcast.9), calls=%async_computation | async-start | bytes 1966080 | tf_op jit(solution)/shard_map/all_to_all | solution.py:218
  19.6 1.1 dynamic-slice_bitcast_fusion.1
  20.7 0.1 pad_maximum_fusion.2
  20.8 17.1 %all-to-all-done.pixel_ref = bf16[16,80,384]{2,1,0:T(8,128)(2,1)S(1)} async-done(((bf16[16,80,384]{2,1,0:T(8,128)(2,1)}), bf16[16,80,384]{2,1,0:T(8,128)(2,1)S(1)}, u32[]{:S(2)}, u32[]{:S(2)}) %all-to-all-start) | async-done | bytes 983072 | tf_op jit(solution)/shard_map/all_to_all | solution.py:218
  38.0 2.9 %broadcast_in_dim.32 = bf16[8,2,384,384]{3,2,1,0:T(8,128)(2,1)} broadcast(bf16[2,384,384]{2,1,0:T(8,128)(2,1)S(1)} %pad_maximum_fusion.2), dimensions={1,2,3} | broadcast | bytes 5308416 | tf_op jit(solution)/shard_map/broadcast_in_dim | solution.py:220
  40.8 2.8 %collective-permute-start = (bf16[588,384]{1,0:T(8,128)(2,1)S(1)}, bf16[588,384]{1,0:T(8,128)(2,1)S(1)}, u32[]{:S(2)}, u32[]{:S(2)}) collective-permute-start(bf16[588,384]{1,0:T(8,128)(2,1)S(1)} %copy-done.6), channel_id=1, source_target_pairs={{0,16},{16,0},{1,17},{17,1},{2,18},{18,2},{3,19},{19,3},{4,20},{20... | collective-permute-start | bytes 1354760 | tf_op jit(solution)/shard_map/ppermute | solution.py:233
  43.7 10.2 %join_weights.1 = bf16[96,1152]{1,0:T(8,128)(2,1)} custom-call(s32[1]{0:T(128)} %bitcast.14.piece_ref, bf16[16,80,384]{2,1,0:T(8,128)(2,1)} %copy-done.3, bf16[128,6144]{1,0:T(8,128)(2,1)} %pos_ref.1, bf16[128,6144]{1,0:T(8,128)(2,1)} %pos_ref.1, f32[1,6144]{1,0:T(1,128)} %bitcast.179, bf16[3,6144,384]{2,1,0:T(8,128)(2,1)} %bitcast.168), custom_call_target="tpu_custom_call" | custom-call | flops 1358954496 | bytes 14155776 | tf_op jit(solution)/shard_map/join_weights/pallas_call | solution.py:86
  53.9 3.4 %collective-permute-start.1 = (bf16[96,1152]{1,0:T(8,128)(2,1)}, bf16[96,1152]{1,0:T(8,128)(2,1)S(1)}, u32[]{:S(2)}, u32[]{:S(2)}) collective-permute-start(bf16[96,1152]{1,0:T(8,128)(2,1)} %join_weights.1), channel_id=1, source_target_pairs={{0,0},{1,8},{2,32},{3,40},{4,64},{5,72},{6,96},{7,104},{16,16},{17... | collective-permute-start | bytes 663560 | tf_op jit(solution)/shard_map/ppermute | solution.py:35
  57.3 1.0 constant_dynamic-slice_fusion.1
  58.3 3.0 %collective-permute-done.1 = bf16[96,1152]{1,0:T(8,128)(2,1)S(1)} collective-permute-done((bf16[96,1152]{1,0:T(8,128)(2,1)}, bf16[96,1152]{1,0:T(8,128)(2,1)S(1)}, u32[]{:S(2)}, u32[]{:S(2)}) %collective-permute-start.1) | collective-permute-done | bytes 221216 | tf_op jit(solution)/shard_map/ppermute | solution.py:35
  61.3 1.3 broadcast_in_dim.36
  62.7 14.1 %all-to-all-start.1 = ((bf16[8,96,1152]{2,1,0:T(8,128)(2,1)}), bf16[8,96,1152]{2,1,0:T(8,128)(2,1)}, u32[]{:S(2)}, u32[]{:S(2)}) async-start(bf16[8,96,1152]{2,1,0:T(8,128)(2,1)} %broadcast_in_dim.36), calls=%async_computation.1 | async-start | bytes 3538944 | tf_op jit(solution)/shard_map/all_to_all | solution.py:231
  76.7 0.0 all-gather.4.cloned.1.call-start
  76.8 0.1 broadcast_select_fusion.1
  76.9 0.1 fusion.8
  77.0 0.1 pad_maximum_fusion.1
  77.1 1.7 copy.16
  78.8 1.5 fusion.29
  80.4 1.6 copy-done.4
  82.0 0.5 multiply_reduce_fusion
  82.5 3.4 %collective-permute-start.8 = (f32[2,8,128]{2,1,0:T(8,128)S(1)}, f32[2,8,128]{2,1,0:T(8,128)S(1)}, u32[]{:S(2)}, u32[]{:S(2)}) collective-permute-start(f32[2,8,128]{2,1,0:T(8,128)S(1)} %pad_maximum_fusion.5), channel_id=1, source_target_pairs={{0,104},{1,105},{2,106},{3,107},{4,108},{5,109},{6,110},{7,111},{1... | collective-permute-start | bytes 24584 | tf_op jit(solution)/shard_map/ppermute | solution.py:35
  85.9 3.3 %collective-permute-start.5 = (f32[2,8,128]{2,1,0:T(8,128)S(1)}, f32[2,8,128]{2,1,0:T(8,128)S(1)}, u32[]{:S(2)}, u32[]{:S(2)}) collective-permute-start(f32[2,8,128]{2,1,0:T(8,128)S(1)} %pad_maximum_fusion.5), channel_id=1, source_target_pairs={{0,64},{1,65},{2,66},{3,67},{4,68},{5,69},{6,70},{7,71},{16,80},{1... | collective-permute-start | bytes 24584 | tf_op jit(solution)/shard_map/ppermute | solution.py:35
  89.3 0.2 collective-permute-start.4
  89.5 1.5 collective-permute-start.3
  90.9 0.5 collective-permute-start.2
  91.4 8.1 %all-to-all-done.1 = bf16[8,96,1152]{2,1,0:T(8,128)(2,1)} async-done(((bf16[8,96,1152]{2,1,0:T(8,128)(2,1)}), bf16[8,96,1152]{2,1,0:T(8,128)(2,1)}, u32[]{:S(2)}, u32[]{:S(2)}) %all-to-all-start.1) | async-done | bytes 1769504 | tf_op jit(solution)/shard_map/all_to_all | solution.py:231
  99.6 0.6 fusion.15.scale_ref
  100.2 11.1 %attend.1 = bf16[8,128,384]{2,1,0:T(8,128)(2,1)} custom-call(bf16[8,128,768]{2,1,0:T(8,128)(2,1)} %bitcast.172, bf16[768,1152]{1,0:T(8,128)(2,1)} %bitcast.17.query_w_ref.key_w_ref.value_w_ref, bf16[768,1152]{1,0:T(8,128)(2,1)} %bitcast.17.query_w_ref.key_w_ref.value_w_ref, bf16[768,1152]{1,0:T(8,128)(2,1)} %bitcast.17.query_w_ref.key_w_ref.value_w_ref, ...), custom_call_target="tpu_custom_call" | custom-call | flops 3623878656 | bytes 7864320 | tf_op jit(solution)/shard_map/attend/pallas_call | solution.py:146
  111.3 58.7 %all_to_all.20 = bf16[8,2,384,384]{3,2,1,0:T(8,128)(2,1)} all-to-all(bf16[8,2,384,384]{3,2,1,0:T(8,128)(2,1)} %broadcast_in_dim.32), channel_id=1, replica_groups=mesh['x'=4,'yh'=2,'core'=2,'yl'=2,'z'=4] {'yl','z'}, dimensions={0} | all-to-all | bytes 9437184 | tf_op jit(solution)/shard_map/all_to_all | solution.py:253
  170.0 7.5 %fusion.7 = f32[8,1,128,384]{3,2,1,0:T(8,128)S(1)} fusion(f32[8,128,768]{2,1,0:T(8,128)} %copy-done.4, bf16[8,128,384,8]{2,1,0,3:T(8,128)(2,1)} %bitcast.180, bf16[8,2,384,384]{3,2,1,0:T(8,128)(2,1)} %all_to_all.20), kind=kOutput, calls=%fused_computation.14 | convolution fusion | flops 2416312320 | bytes 11796480 | tf_op jit(solution)/shard_map/gtc,gcd->td/dot_general | solution.py:260
  177.5 0.5 copy-done.8
  178.0 3.4 %fusion.6 = f32[8,1,128,384]{3,2,1,0:T(8,128)S(1)} fusion(f32[8,128,768]{2,1,0:T(8,128)S(1)} %copy-done.5, bf16[8,128,384,8]{2,1,0,3:T(8,128)(2,1)S(1)} %bitcast.181, bf16[8,2,384,384]{3,2,1,0:T(8,128)(2,1)S(1)} %copy-done.2), kind=kOutput, calls=%fused_computation.12 | convolution fusion | flops 2416312320 | bytes 11796480 | tf_op jit(solution)/shard_map/gtc,gcd->td/dot_general | solution.py:260
  181.5 1.2 copy-done.1
  182.6 1.4 fusion.1
  184.0 6.1 %all-to-all-start.3 = ((bf16[8,2,128,384]{3,2,1,0:T(8,128)(2,1)}), bf16[8,2,128,384]{3,2,1,0:T(8,128)(2,1)S(1)}, u32[]{:S(2)}, u32[]{:S(2)}) async-start(bf16[8,2,128,384]{3,2,1,0:T(8,128)(2,1)} %fusion.1), calls=%async_computation.3 | async-start | bytes 3145728 | tf_op jit(solution)/shard_map/all_to_all | solution.py:271
  190.2 1.6 fusion
  191.8 3.2 %collective-permute-start.9 = (f32[128,384]{1,0:T(8,128)S(1)}, f32[128,384]{1,0:T(8,128)S(1)}, u32[]{:S(2)}, u32[]{:S(2)}) collective-permute-start(f32[128,384]{1,0:T(8,128)S(1)} %select_bitcast_fusion), channel_id=1, source_target_pairs={{0,16},{16,0},{1,17},{17,1},{2,18},{18,2},{3,19},{19,3},{4,20},{20... | collective-permute-start | bytes 589832 | tf_op jit(solution)/shard_map/ppermute | solution.py:269
  195.1 5.2 %collective-permute-done.9 = f32[128,384]{1,0:T(8,128)S(1)} collective-permute-done((f32[128,384]{1,0:T(8,128)S(1)}, f32[128,384]{1,0:T(8,128)S(1)}, u32[]{:S(2)}, u32[]{:S(2)}) %collective-permute-start.9) | collective-permute-done | bytes 196640 | tf_op jit(solution)/shard_map/ppermute | solution.py:269
  200.2 0.8 broadcast_in_dim.39
  201.1 9.7 %all-to-all-done.3.in_ref = bf16[8,2,128,384]{3,2,1,0:T(8,128)(2,1)S(1)} async-done(((bf16[8,2,128,384]{3,2,1,0:T(8,128)(2,1)}), bf16[8,2,128,384]{3,2,1,0:T(8,128)(2,1)S(1)}, u32[]{:S(2)}, u32[]{:S(2)}) %all-to-all-start.3) | async-done | bytes 1572896 | tf_op jit(solution)/shard_map/all_to_all | solution.py:271
  210.7 1.2 copy-done
  211.9 3.6 %assemble.1 = bf16[128,6144]{1,0:T(8,128)(2,1)} custom-call(bf16[8,2,128,384]{3,2,1,0:T(8,128)(2,1)} %copy-done), custom_call_target="tpu_custom_call" | custom-call | tf_op jit(solution)/shard_map/assemble/pallas_call | solution.py:180
  (37 shorter events, 0.2 us)
Async XLA Ops:
  7.2 69.9 %all-gather.6.cloned.1.call-start = ((), (), s32[]{:S(2)}) async-start(), calls=%async_computation.5 | async-start | bytes 1769472 | tf_op jit(solution)/shard_map/all_gather | solution.py:214
  11.2 26.8 %all-to-all-start = ((bf16[16,80,384]{2,1,0:T(8,128)(2,1)}), bf16[16,80,384]{2,1,0:T(8,128)(2,1)S(1)}, u32[]{:S(2)}, u32[]{:S(2)}) async-start(bf16[16,80,384]{2,1,0:T(8,128)(2,1)} %bitcast.9), calls=%async_computation | async-start | bytes 1966080 | tf_op jit(solution)/shard_map/all_to_all | solution.py:218
  20.8 20.0 %copy-start.6 = (bf16[588,384]{1,0:T(8,128)(2,1)S(1)}, bf16[588,384]{1,0:T(8,128)(2,1)}, u32[]{:S(2)}) copy-start(bf16[588,384]{1,0:T(8,128)(2,1)} %param.11) | copy-start | bytes 1354756
  38.0 2.9 %copy-start.3 = (bf16[16,80,384]{2,1,0:T(8,128)(2,1)}, bf16[16,80,384]{2,1,0:T(8,128)(2,1)S(1)}, u32[]{:S(2)}) copy-start(bf16[16,80,384]{2,1,0:T(8,128)(2,1)S(1)} %all-to-all-done.pixel_ref) | copy-start | bytes 2949124
  40.8 35.9 %collective-permute-start = (bf16[588,384]{1,0:T(8,128)(2,1)S(1)}, bf16[588,384]{1,0:T(8,128)(2,1)S(1)}, u32[]{:S(2)}, u32[]{:S(2)}) collective-permute-start(bf16[588,384]{1,0:T(8,128)(2,1)S(1)} %copy-done.6), channel_id=1, source_target_pairs={{0,16},{16,0},{1,17},{17,1},{2,18},{18,2},{3,19},{19,3},{4,20},{20... | collective-permute-start | bytes 1354760 | tf_op jit(solution)/shard_map/ppermute | solution.py:233
  53.9 7.5 %collective-permute-start.1 = (bf16[96,1152]{1,0:T(8,128)(2,1)}, bf16[96,1152]{1,0:T(8,128)(2,1)S(1)}, u32[]{:S(2)}, u32[]{:S(2)}) collective-permute-start(bf16[96,1152]{1,0:T(8,128)(2,1)} %join_weights.1), channel_id=1, source_target_pairs={{0,0},{1,8},{2,32},{3,40},{4,64},{5,72},{6,96},{7,104},{16,16},{17... | collective-permute-start | bytes 663560 | tf_op jit(solution)/shard_map/ppermute | solution.py:35
  62.7 36.9 %all-to-all-start.1 = ((bf16[8,96,1152]{2,1,0:T(8,128)(2,1)}), bf16[8,96,1152]{2,1,0:T(8,128)(2,1)}, u32[]{:S(2)}, u32[]{:S(2)}) async-start(bf16[8,96,1152]{2,1,0:T(8,128)(2,1)} %broadcast_in_dim.36), calls=%async_computation.1 | async-start | bytes 3538944 | tf_op jit(solution)/shard_map/all_to_all | solution.py:231
  76.7 93.2 %all-gather.4.cloned.1.call-start = ((), (), s32[]{:S(2)}) async-start(), calls=%async_computation.4 | async-start | bytes 7077888 | tf_op jit(solution)/shard_map/all_gather | solution.py:257
  78.8 1.6 copy-start.7
  80.4 1.6 copy-start.4
  82.5 6.9 %collective-permute-start.8 = (f32[2,8,128]{2,1,0:T(8,128)S(1)}, f32[2,8,128]{2,1,0:T(8,128)S(1)}, u32[]{:S(2)}, u32[]{:S(2)}) collective-permute-start(f32[2,8,128]{2,1,0:T(8,128)S(1)} %pad_maximum_fusion.5), channel_id=1, source_target_pairs={{0,104},{1,105},{2,106},{3,107},{4,108},{5,109},{6,110},{7,111},{1... | collective-permute-start | bytes 24584 | tf_op jit(solution)/shard_map/ppermute | solution.py:35
  85.9 5.0 %collective-permute-start.7 = (f32[2,8,128]{2,1,0:T(8,128)S(1)}, f32[2,8,128]{2,1,0:T(8,128)S(1)}, u32[]{:S(2)}, u32[]{:S(2)}) collective-permute-start(f32[2,8,128]{2,1,0:T(8,128)S(1)} %pad_maximum_fusion.5), channel_id=1, source_target_pairs={{0,96},{1,97},{2,98},{3,99},{4,100},{5,101},{6,102},{7,103},{16,11... | collective-permute-start | bytes 24584 | tf_op jit(solution)/shard_map/ppermute | solution.py:35
  85.9 13.6 %collective-permute-start.6 = (f32[2,8,128]{2,1,0:T(8,128)S(1)}, f32[2,8,128]{2,1,0:T(8,128)S(1)}, u32[]{:S(2)}, u32[]{:S(2)}) collective-permute-start(f32[2,8,128]{2,1,0:T(8,128)S(1)} %pad_maximum_fusion.5), channel_id=1, source_target_pairs={{0,72},{1,73},{2,74},{3,75},{4,76},{5,77},{6,78},{7,79},{16,88},{1... | collective-permute-start | bytes 24584 | tf_op jit(solution)/shard_map/ppermute | solution.py:35
  85.9 13.6 %collective-permute-start.5 = (f32[2,8,128]{2,1,0:T(8,128)S(1)}, f32[2,8,128]{2,1,0:T(8,128)S(1)}, u32[]{:S(2)}, u32[]{:S(2)}) collective-permute-start(f32[2,8,128]{2,1,0:T(8,128)S(1)} %pad_maximum_fusion.5), channel_id=1, source_target_pairs={{0,64},{1,65},{2,66},{3,67},{4,68},{5,69},{6,70},{7,71},{16,80},{1... | collective-permute-start | bytes 24584 | tf_op jit(solution)/shard_map/ppermute | solution.py:35
  89.3 10.3 %collective-permute-start.4 = (f32[2,8,128]{2,1,0:T(8,128)S(1)}, f32[2,8,128]{2,1,0:T(8,128)S(1)}, u32[]{:S(2)}, u32[]{:S(2)}) collective-permute-start(f32[2,8,128]{2,1,0:T(8,128)S(1)} %pad_maximum_fusion.5), channel_id=1, source_target_pairs={{0,40},{1,41},{2,42},{3,43},{4,44},{5,45},{6,46},{7,47},{16,56},{1... | collective-permute-start | bytes 24584 | tf_op jit(solution)/shard_map/ppermute | solution.py:35
  89.5 10.1 %collective-permute-start.3 = (f32[2,8,128]{2,1,0:T(8,128)S(1)}, f32[2,8,128]{2,1,0:T(8,128)S(1)}, u32[]{:S(2)}, u32[]{:S(2)}) collective-permute-start(f32[2,8,128]{2,1,0:T(8,128)S(1)} %pad_maximum_fusion.5), channel_id=1, source_target_pairs={{0,32},{1,33},{2,34},{3,35},{4,36},{5,37},{6,38},{7,39},{16,48},{1... | collective-permute-start | bytes 24584 | tf_op jit(solution)/shard_map/ppermute | solution.py:35
  90.9 8.6 %collective-permute-start.2 = (f32[2,8,128]{2,1,0:T(8,128)S(1)}, f32[2,8,128]{2,1,0:T(8,128)S(1)}, u32[]{:S(2)}, u32[]{:S(2)}) collective-permute-start(f32[2,8,128]{2,1,0:T(8,128)S(1)} %pad_maximum_fusion.5), channel_id=1, source_target_pairs={{0,8},{1,9},{2,10},{3,11},{4,12},{5,13},{6,14},{7,15},{16,24},{17,... | collective-permute-start | bytes 24584 | tf_op jit(solution)/shard_map/ppermute | solution.py:35
  170.0 7.5 %copy-start.2 = (bf16[8,2,384,384]{3,2,1,0:T(8,128)(2,1)S(1)}, bf16[8,2,384,384]{3,2,1,0:T(8,128)(2,1)}, u32[]{:S(2)}) copy-start(bf16[8,2,384,384]{3,2,1,0:T(8,128)(2,1)} %all_to_all.20) | copy-start | bytes 14155780
  170.0 7.5 %copy-start.5 = (f32[8,128,768]{2,1,0:T(8,128)S(1)}, f32[8,128,768]{2,1,0:T(8,128)}, u32[]{:S(2)}) copy-start(f32[8,128,768]{2,1,0:T(8,128)} %copy-done.4) | copy-start | bytes 9437188
  170.0 8.0 %copy-start.8 = (bf16[8,1024,384]{2,1,0:T(8,128)(2,1)S(1)}, bf16[8,1024,384]{2,1,0:T(8,128)(2,1)}, u32[]{:S(2)}) copy-start(bf16[8,1024,384]{2,1,0:T(8,128)(2,1)} %all-gather.4.cloned.1.call-done) | copy-start | bytes 18874372
  181.5 1.2 copy-start.1
  184.0 26.7 %all-to-all-start.3 = ((bf16[8,2,128,384]{3,2,1,0:T(8,128)(2,1)}), bf16[8,2,128,384]{3,2,1,0:T(8,128)(2,1)S(1)}, u32[]{:S(2)}, u32[]{:S(2)}) async-start(bf16[8,2,128,384]{3,2,1,0:T(8,128)(2,1)} %fusion.1), calls=%async_computation.3 | async-start | bytes 3145728 | tf_op jit(solution)/shard_map/all_to_all | solution.py:271
  191.8 8.4 %collective-permute-start.9 = (f32[128,384]{1,0:T(8,128)S(1)}, f32[128,384]{1,0:T(8,128)S(1)}, u32[]{:S(2)}, u32[]{:S(2)}) collective-permute-start(f32[128,384]{1,0:T(8,128)S(1)} %select_bitcast_fusion), channel_id=1, source_target_pairs={{0,16},{16,0},{1,17},{17,1},{2,18},{18,2},{3,19},{19,3},{4,20},{20... | collective-permute-start | bytes 589832 | tf_op jit(solution)/shard_map/ppermute | solution.py:269
  210.7 1.2 copy-start
Sparse Core Ops, SparseCore 0:
  10.2 34.0 all-gather.5
  111.4 41.1 all-gather.3
where the time goes:
time: 223 us; the launch traced here: 222 us
  blocking collectives  58.7 us (26%)
  starting transfers between devices  47 us (21%)
  waiting for transfers between devices  43.2 us (19%)
  Pallas kernels  24.8 us (11%)
  local copies, waits for them, and re-layouts  15.4 us (7%)
  between operations  14.3 us (6%)
  matrix products  12.5 us (6%)
  other arithmetic  6.34 us (3%)
    all_to_all x1, blocking collectives, block(): out_all = lax.all_to_all(out_mine, MP, 0, 0, tiled=True)  58.7 us
    all_to_all x1, waiting for transfers between devices, block(): pixel_rows = lax.all_to_all(mine, DP, 0, 0, tiled=True)  17.1 us
    all_to_all x1, starting transfers between devices, block(): joined = lax.all_to_all(joined, MP, 0, 0, tiled=True).reshape(8 * ROWS, -1)  14.1 us
    ppermute x8, starting transfers between devices, send(): return lax.ppermute(array, AXES, pairs)  12.3 us
    pallas_call x1, Pallas kernels, attend(): pl.pallas_call(attention_kernel, out_shape=jax.ShapeDtypeStruct((copies,...  11.1 us
    dot_general x2, matrix products, block(): jnp.einsum('gtc,gcd->td', head_all, out_all[:, yb], preferred_element_typ...  10.9 us
    pallas_call x1, Pallas kernels, join_weights(): pl.pallas_call(join_kernel, out_shape=jax.ShapeDtypeStruct((ROWS, 3 * gro...  10.2 us
    all_to_all x1, waiting for transfers between devices, block(): moved = lax.all_to_all(output.astype(bf16), GROUP, 0, 0, tiled=True)  9.69 us
  transfers between devices with their start and end apart: 15, of which 5 were waited for; matrix products, arithmetic and copies ran while one was open for 7% of the time, Pallas kernels for 5%

commit v1 on v0

--- a/solution.py
+++ b/solution.py
@@ -76,7 +76,12 @@
 
     @pl.when(step == pl.num_programs(0) - 1)
     def _():
-        out_ref[...] = acc_ref[...].astype(bf16)
+        for j in range(acc_ref.shape[1] // HEAD_DIM):
+            lanes = slice(j * HEAD_DIM, (j + 1) * HEAD_DIM)
+            block = acc_ref[:, lanes]
+            if 3 * j < 2 * (acc_ref.shape[1] // HEAD_DIM):
+                block = block - jnp.mean(block, axis=1, keepdims=True)
+            out_ref[:, lanes] = block.astype(bf16)
 
 
 def join_weights(piece, pixel_rows, position_table, gain, qkv):
@@ -111,32 +116,37 @@
     )(piece, pixel_rows, position_table, position_table, gain, qkv)
 
 
-def head_norm(raw, scale, gain):
-    average = jnp.mean(raw, axis=-1, keepdims=True)
-    centred = raw - average
+def head_norm(centred, scale, gain):
     variance = jnp.mean(centred * centred, axis=-1, keepdims=True)
-    return (centred * (scale * lax.rsqrt(variance * scale * scale + epsilon)) * gain).astype(bf16)
+    return (centred * (scale * lax.rsqrt(variance * (scale * scale) + epsilon)) * gain).astype(bf16)
 
 
 def attention_kernel(
-    lhs_ref, query_w_ref, key_w_ref, value_w_ref, scale_ref, query_gain_ref, key_gain_ref, out_ref, proj_ref
+    lhs_ref, query_w_ref, key_w_ref, value_w_ref, scale_ref, query_gain_ref, key_gain_ref, out_ref, proj_ref, scale_all
 ):
     copies, patches, rows = lhs_ref.shape
+
+    @pl.when(pl.program_id(0) == 0)
+    def _():
+        shape = (patches, patches)
+        diagonal = lax.broadcasted_iota(jnp.int32, shape, 0) == lax.broadcasted_iota(jnp.int32, shape, 1)
+        for c in range(copies):
+            row = jnp.broadcast_to(scale_ref[c : c + 1, :], shape)
+            column = jnp.sum(jnp.where(diagonal, row, 0.0), axis=1, keepdims=True)
+            scale_all[c] = jnp.broadcast_to(column, (patches, HEAD_DIM))
+
     weights = jnp.concatenate([query_w_ref[...], key_w_ref[...], value_w_ref[...]], axis=1)
     proj_ref[...] = dot(lhs_ref[...].reshape(copies * patches, rows), weights, ((1,), (0,)))
-    diagonal = lax.broadcasted_iota(jnp.int32, (patches, patches), 0) == lax.broadcasted_iota(
-        jnp.int32, (patches, patches), 1
-    )
+    ones = jnp.ones((patches, HEAD_DIM), bf16)
     for c in range(copies):
         here = slice(c * patches, (c + 1) * patches)
-        scale_row = jnp.broadcast_to(scale_ref[c : c + 1, :], (patches, patches))
-        scale = jnp.sum(jnp.where(diagonal, scale_row, 0.0), axis=1, keepdims=True)
+        scale = scale_all[c]
         query = head_norm(proj_ref[here, :HEAD_DIM], scale, query_gain_ref[...])
         key_vec = head_norm(proj_ref[here, HEAD_DIM : 2 * HEAD_DIM], scale, key_gain_ref[...])
         value = (proj_ref[here, 2 * HEAD_DIM :] * scale).astype(bf16)
-        exp_scores = jnp.exp(dot(query, key_vec, ((1,), (1,))) * HEAD_DIM ** (-0.5))
-        probs = (exp_scores / jnp.sum(exp_scores, axis=-1, keepdims=True)).astype(bf16)
-        out_ref[c] = dot(probs, value, ((1,), (0,))).astype(bf16)
+        exp_scores = jnp.exp(dot(query, key_vec, ((1,), (1,))) * HEAD_DIM ** (-0.5)).astype(bf16)
+        mixed = dot(exp_scores, jnp.concatenate([value, ones], axis=1), ((1,), (0,)))
+        out_ref[c] = (mixed[:, :HEAD_DIM] / mixed[:, HEAD_DIM:]).astype(bf16)
 
 
 def attend(lhs, joined, scale, query_gain, key_gain):
@@ -157,7 +167,10 @@
             pl.BlockSpec((1, HEAD_DIM), lambda h: (0, 0)),
         ],
         out_specs=pl.BlockSpec((copies, patches, HEAD_DIM), lambda h: (0, 0, h)),
-        scratch_shapes=[pltpu.VMEM((copies * patches, 3 * HEAD_DIM), f32)],
+        scratch_shapes=[
+            pltpu.VMEM((copies * patches, 3 * HEAD_DIM), f32),
+            pltpu.VMEM((copies, patches, HEAD_DIM), f32),
+        ],
         cost_estimate=pl.CostEstimate(
             flops=4 * copies * rows * patches * group_cols * 3,
             transcendentals=copies * patches * group_cols,
@@ -167,22 +180,34 @@
     )(lhs, joined, joined, joined, scale, query_gain[None], key_gain[None])
 
 
-def assemble_kernel(in_ref, out_ref):
-    cores, halves, _, cols = in_ref.shape
-    for yb in range(halves):
-        for c in range(cores):
-            start = (yb * cores + c) * cols
-            out_ref[:, start : start + cols] = in_ref[c, yb]
+def assemble_kernel(in_ref, out_ref, sems):
+    shares, _, both = in_ref.shape
+    cols = both // 2
+    copies = []
+    for g in range(shares):
+        for yb in range(2):
+            start = ((g // 2 * 2 + yb) * 2 + g % 2) * cols
+            copies.append(
+                pltpu.make_async_copy(
+                    in_ref.at[g, :, yb * cols : (yb + 1) * cols],
+                    out_ref.at[:, start : start + cols],
+                    sems.at[g, yb],
+                )
+            )
+    for copy in copies:
+        copy.start()
+    for copy in copies:
+        copy.wait()
 
 
 def assemble(moved):
-    shares, halves, patches, cols = moved.shape
+    shares, patches, both = moved.shape
     return pl.pallas_call(
         assemble_kernel,
-        out_shape=jax.ShapeDtypeStruct((patches, shares * halves * cols), bf16),
-        grid=(shares // 2,),
-        in_specs=[pl.BlockSpec((2, halves, patches, cols), lambda i: (i, 0, 0, 0))],
-        out_specs=pl.BlockSpec((patches, 2 * halves * cols), lambda i: (0, i)),
+        out_shape=jax.ShapeDtypeStruct((patches, shares * both), bf16),
+        in_specs=[pl.BlockSpec(memory_space=pl.ANY)],
+        out_specs=pl.BlockSpec(memory_space=pl.ANY),
+        scratch_shapes=[pltpu.SemaphoreType.DMA((shares, 2))],
         name="assemble",
     )(moved)
 
@@ -209,16 +234,17 @@
             lax.dynamic_slice_in_dim(array, start + yb * 2 * cols, cols, axis=1) for yb in range(2)
         ]
 
-    noisy = (clean_image[0].astype(f32) + 0.5 * noise_draw[0, 0].astype(f32)).astype(bf16)
-    lhs_own = extended(noisy, jnp.eye(patches, dtype=bf16)).T
-    lhs = lax.all_gather(lhs_own, GROUP)
-
     mine = pixel_pieces(embed_weight).reshape(4, 1, 2, PIX_ROWS, cols)
     mine = jnp.broadcast_to(mine, (4, 2, 2, PIX_ROWS, cols)).reshape(shares, PIX_ROWS, cols)
     pixel_rows = lax.all_to_all(mine, DP, 0, 0, tiled=True)
-    out_mine = jnp.stack(my_columns(out_weight))
+    noisy = (clean_image[0].astype(f32) + 0.5 * noise_draw[0, 0].astype(f32)).astype(bf16)
+    lhs_own = extended(noisy, jnp.eye(patches, dtype=bf16)).T
+    out_mine = jnp.concatenate(my_columns(out_weight), axis=1)
     out_mine = jnp.broadcast_to(out_mine[None], (8, *out_mine.shape))
-    out_mine, pixel_rows, own_weight = lax.optimization_barrier((out_mine, pixel_rows, embed_weight))
+    out_mine, lhs_own, pixel_rows, own_weight = lax.optimization_barrier(
+        (out_mine, lhs_own, pixel_rows, embed_weight)
+    )
+    lhs = lax.all_gather(lhs_own, GROUP)
     piece = join_weights(
         (2 * xi + ci).astype(jnp.int32).reshape(1),
         pixel_rows,
@@ -255,17 +281,12 @@
     head_out = attend(lhs, joined, scale, query_gain, key_gain)
     head_out = head_out.reshape(8 * patches, -1)
     head_all = lax.all_gather(head_out, GROUP)
-    halves = []
-    for yb in range(2):
-        attention = jnp.einsum("gtc,gcd->td", head_all, out_all[:, yb], preferred_element_type=f32)
-        halves.append(
-            embedded[:, :, yb * cols : (yb + 1) * cols] + attention.reshape(8, patches, cols)
-        )
-    output = jnp.stack(halves, axis=1)
+    attention = jnp.einsum("gtc,gcd->td", head_all, out_all, preferred_element_type=f32)
+    output = embedded + attention.reshape(8, patches, 2 * cols)
 
     summed = jnp.sum(output, axis=0) * (1.0 / 16)
-    kept = jnp.where(yhi == 0, summed[0], summed[1])
-    sent = jnp.where(yhi == 0, summed[1], summed[0])
+    kept = jnp.where(yhi == 0, summed[:, :cols], summed[:, cols:])
+    sent = jnp.where(yhi == 0, summed[:, cols:], summed[:, :cols])
     smoothed = (kept + lax.ppermute(sent, "yh", [(0, 1), (1, 0)]))[:, None, :]
 
     moved = lax.all_to_all(output.astype(bf16), GROUP, 0, 0, tiled=True)

time: 223 us -> 259 us (1.16)
  Pallas kernels: 24.8 us -> 66.6 us
  waiting for transfers between devices: 43.2 us -> 38.6 us
  starting transfers between devices: 47 us -> 51 us
  local copies, waits for them, and re-layouts: 15.4 us -> 12.7 us
    pallas_call x1, Pallas kernels: 3.58 us -> 48.9 us  [assemble(): pl.pallas_call(assemble_kernel, out_shape=jax.ShapeDtypeStruct((patches,...]
    pallas_call x1, Pallas kernels: 11.1 us -> 7.26 us  [attend(): pl.pallas_call(attention_kernel, out_shape=jax.ShapeDtypeStruct((copies,...]
    all_to_all x1, waiting for transfers between devices: 8.14 us -> 4.59 us  [block(): joined = lax.all_to_all(joined, MP, 0, 0, tiled=True).reshape(8 * ROWS, -1)]
    unnamed x18 -> x10, local copies, waits for them, and re-layouts: 4.53 us -> 1.18 us
    all_to_all x1, waiting for transfers between devices: 17.1 us -> 14 us  [block(): pixel_rows = lax.all_to_all(mine, DP, 0, 0, tiled=True)]
    dot_general x2 -> x1, matrix products: 10.9 us -> 7.98 us  [block(): jnp.einsum('gtc,gcd->td', head_all, out_all, preferred_element_type=f32)]
  transfers between devices with their start and end apart: 15 -> 15, of which waited for: 5 -> 5; matrix products, arithmetic and copies ran while one was open for 7% -> 5% of each run, Pallas kernels for 5% -> 4%
where the time goes in v1:
time: 259 us; the launch traced here: 258 us
  Pallas kernels  66.6 us (26%)
  blocking collectives  58.7 us (23%)
  starting transfers between devices  51 us (20%)
  waiting for transfers between devices  38.6 us (15%)
  between operations  14.3 us (6%)
  local copies, waits for them, and re-layouts  12.7 us (5%)
  matrix products  11.2 us (4%)
  other arithmetic  5.08 us (2%)
    all_to_all x1, blocking collectives, block(): out_all = lax.all_to_all(out_mine, MP, 0, 0, tiled=True)  58.7 us
    pallas_call x1, Pallas kernels, assemble(): pl.pallas_call(assemble_kernel, out_shape=jax.ShapeDtypeStruct((patches,...  48.9 us
    all_to_all x1, starting transfers between devices, block(): joined = lax.all_to_all(joined, MP, 0, 0, tiled=True).reshape(8 * ROWS, -1)  16.1 us
    ppermute x8, starting transfers between devices, send(): return lax.ppermute(array, AXES, pairs)  14.3 us
    all_to_all x1, waiting for transfers between devices, block(): pixel_rows = lax.all_to_all(mine, DP, 0, 0, tiled=True)  14 us
    all_to_all x1, waiting for transfers between devices, block(): moved = lax.all_to_all(output.astype(bf16), GROUP, 0, 0, tiled=True)  11.6 us
    pallas_call x1, Pallas kernels, join_weights(): pl.pallas_call(join_kernel, out_shape=jax.ShapeDtypeStruct((ROWS, 3 * gro...  10.5 us
    all_to_all x1, starting transfers between devices, block(): pixel_rows = lax.all_to_all(mine, DP, 0, 0, tiled=True)  8.44 us
  transfers between devices with their start and end apart: 15, of which 5 were waited for; matrix products, arithmetic and copies ran while one was open for 5% of the time, Pallas kernels for 4%

profile of v1, /device:TPU:1, one launch (start us, length us, event | category | flops | bytes accessed | tf_op | source)
XLA Modules:
  0.0 258.1 jit_solution(8826161134289816265)
XLA Ops:
  7.2 1.1 pad.13
  8.2 0.0 copy-start.3
  8.2 0.0 copy-start.4
  8.3 1.0 broadcast_in_dim.34
  9.3 8.4 %all-to-all-start = ((bf16[16,80,384]{2,1,0:T(8,128)(2,1)}), bf16[16,80,384]{2,1,0:T(8,128)(2,1)S(1)}, u32[]{:S(2)}, u32[]{:S(2)}) async-start(bf16[16,80,384]{2,1,0:T(8,128)(2,1)} %bitcast.6), calls=%async_computation | async-start | bytes 1966080 | tf_op jit(solution)/shard_map/all_to_all | solution.py:239
  17.7 0.0 all-gather.6.cloned.1.call-start
  17.8 0.1 fusion.3
  17.9 0.1 fusion.4
  18.0 0.7 pad_maximum_fusion.2
  18.7 1.1 constant_dynamic-slice_fusion.3
  19.8 0.1 pad_maximum_fusion.1
  19.9 14.0 %all-to-all-done.pixel_ref = bf16[16,80,384]{2,1,0:T(8,128)(2,1)S(1)} async-done(((bf16[16,80,384]{2,1,0:T(8,128)(2,1)}), bf16[16,80,384]{2,1,0:T(8,128)(2,1)S(1)}, u32[]{:S(2)}, u32[]{:S(2)}) %all-to-all-start) | async-done | bytes 983072 | tf_op jit(solution)/shard_map/all_to_all | solution.py:239
  33.9 2.5 broadcast_in_dim.32
  36.4 0.0 all-gather.6.cloned.1.call-update
  36.5 1.2 collective-permute-start
  37.7 10.5 %join_weights.1 = bf16[96,1152]{1,0:T(8,128)(2,1)} custom-call(s32[1]{0:T(128)} %bitcast.12.piece_ref, bf16[16,80,384]{2,1,0:T(8,128)(2,1)} %copy-done.1, bf16[128,6144]{1,0:T(8,128)(2,1)} %pos_ref.1, bf16[128,6144]{1,0:T(8,128)(2,1)} %pos_ref.1, f32[1,6144]{1,0:T(1,128)} %bitcast.136, bf16[3,6144,384]{2,1,0:T(8,128)(2,1)} %bitcast.124), custom_call_target="tpu_custom_call" | custom-call | flops 1358954496 | bytes 14155776 | tf_op jit(solution)/shard_map/join_weights/pallas_call | solution.py:91
  48.1 3.8 %collective-permute-start.1 = (bf16[96,1152]{1,0:T(8,128)(2,1)}, bf16[96,1152]{1,0:T(8,128)(2,1)S(1)}, u32[]{:S(2)}, u32[]{:S(2)}) collective-permute-start(bf16[96,1152]{1,0:T(8,128)(2,1)} %join_weights.1), channel_id=1, source_target_pairs={{0,0},{1,8},{2,32},{3,40},{4,64},{5,72},{6,96},{7,104},{16,16},{17... | collective-permute-start | bytes 663560 | tf_op jit(solution)/shard_map/ppermute | solution.py:35
  51.9 1.0 constant_dynamic-slice_fusion.1
  53.0 2.8 %collective-permute-done.1 = bf16[96,1152]{1,0:T(8,128)(2,1)S(1)} collective-permute-done((bf16[96,1152]{1,0:T(8,128)(2,1)}, bf16[96,1152]{1,0:T(8,128)(2,1)S(1)}, u32[]{:S(2)}, u32[]{:S(2)}) %collective-permute-start.1) | collective-permute-done | bytes 221216 | tf_op jit(solution)/shard_map/ppermute | solution.py:35
  55.8 1.3 broadcast_in_dim.36
  57.1 16.1 %all-to-all-start.1 = ((bf16[8,96,1152]{2,1,0:T(8,128)(2,1)}), bf16[8,96,1152]{2,1,0:T(8,128)(2,1)}, u32[]{:S(2)}, u32[]{:S(2)}) async-start(bf16[8,96,1152]{2,1,0:T(8,128)(2,1)} %broadcast_in_dim.36), calls=%async_computation.1 | async-start | bytes 3538944 | tf_op jit(solution)/shard_map/all_to_all | solution.py:257
  73.2 0.0 all-gather.4.cloned.1.call-start
  73.2 0.0 collective-permute-done
  73.2 0.1 broadcast_select_fusion.1
  73.3 0.1 fusion.2
  73.4 1.1 pad_maximum_fusion
  74.6 2.6 copy.13
  77.1 3.3 %fusion.23 = (f32[8,128]{1,0:T(8,128)S(1)}, f32[8,128,768]{2,1,0:T(8,128)S(1)}) fusion(bf16[8,128,768]{2,1,0:T(8,128)(2,1)} %bitcast.128, bf16[768,768,1]{1,0,2:T(8,128)(2,1)} %bitcast.131), kind=kOutput, calls=%fused_computation.60 | convolution fusion | flops 1208744960 | bytes 5902336 | tf_op jit(solution)/shard_map/cpk,kd->cpd/dot_general | solution.py:266
  80.4 0.5 multiply_reduce_fusion
  80.9 5.0 %collective-permute-start.8 = (f32[2,8,128]{2,1,0:T(8,128)S(1)}, f32[2,8,128]{2,1,0:T(8,128)S(1)}, u32[]{:S(2)}, u32[]{:S(2)}) collective-permute-start(f32[2,8,128]{2,1,0:T(8,128)S(1)} %pad_maximum_fusion.4), channel_id=1, source_target_pairs={{0,104},{1,105},{2,106},{3,107},{4,108},{5,109},{6,110},{7,111},{1... | collective-permute-start | bytes 24584 | tf_op jit(solution)/shard_map/ppermute | solution.py:35
  85.9 3.3 %collective-permute-start.5 = (f32[2,8,128]{2,1,0:T(8,128)S(1)}, f32[2,8,128]{2,1,0:T(8,128)S(1)}, u32[]{:S(2)}, u32[]{:S(2)}) collective-permute-start(f32[2,8,128]{2,1,0:T(8,128)S(1)} %pad_maximum_fusion.4), channel_id=1, source_target_pairs={{0,64},{1,65},{2,66},{3,67},{4,68},{5,69},{6,70},{7,71},{16,80},{1... | collective-permute-start | bytes 24584 | tf_op jit(solution)/shard_map/ppermute | solution.py:35
  89.2 0.3 collective-permute-start.4
  89.5 1.4 collective-permute-start.3
  90.9 0.5 collective-permute-start.2
  91.4 4.6 %all-to-all-done.1 = bf16[8,96,1152]{2,1,0:T(8,128)(2,1)} async-done(((bf16[8,96,1152]{2,1,0:T(8,128)(2,1)}), bf16[8,96,1152]{2,1,0:T(8,128)(2,1)}, u32[]{:S(2)}, u32[]{:S(2)}) %all-to-all-start.1) | async-done | bytes 1769504 | tf_op jit(solution)/shard_map/all_to_all | solution.py:257
  96.0 0.6 fusion.9.scale_ref
  96.6 7.3 %attend.1 = bf16[8,128,384]{2,1,0:T(8,128)(2,1)} custom-call(bf16[8,128,768]{2,1,0:T(8,128)(2,1)} %bitcast.129, bf16[768,1152]{1,0:T(8,128)(2,1)} %bitcast.15.query_w_ref.key_w_ref.value_w_ref, bf16[768,1152]{1,0:T(8,128)(2,1)} %bitcast.15.query_w_ref.key_w_ref.value_w_ref, bf16[768,1152]{1,0:T(8,128)(2,1)} %bitcast.15.query_w_ref.key_w_ref.value_w_ref, ...), custom_call_target="tpu_custom_call" | custom-call | flops 3623878656 | bytes 7864320 | tf_op jit(solution)/shard_map/attend/pallas_call | solution.py:156
  103.9 0.0 all-gather.4.cloned.1.call-update
  103.9 58.7 %all_to_all.20 = bf16[8,384,768]{2,1,0:T(8,128)(2,1)} all-to-all(bf16[8,384,768]{2,1,0:T(8,128)(2,1)} %broadcast_in_dim.32), channel_id=1, replica_groups=mesh['x'=4,'yh'=2,'core'=2,'yl'=2,'z'=4] {'yl','z'}, dimensions={0} | all-to-all | bytes 9437184 | tf_op jit(solution)/shard_map/all_to_all | solution.py:279
  162.6 8.0 %fusion.24 = f32[1024,768,1]{1,0,2:T(8,128)S(1)} fusion(bf16[8,1024,384]{2,1,0:T(8,128)(2,1)} %all-gather.4.cloned.1.call-done, bf16[8,384,768]{2,1,0:T(8,128)(2,1)} %all_to_all.20), kind=kOutput, calls=%fused_computation.61 | convolution fusion | flops 4831838208 | bytes 14155776 | tf_op jit(solution)/shard_map/gtc,gcd->td/dot_general | solution.py:284
  170.6 1.7 add_reduce_fusion
  172.3 8.4 %all-to-all-start.3 = ((bf16[8,128,768]{2,1,0:T(8,128)(2,1)}), bf16[8,128,768]{2,1,0:T(8,128)(2,1)S(1)}, u32[]{:S(2)}, u32[]{:S(2)}) async-start(bf16[8,128,768]{2,1,0:T(8,128)(2,1)} %get-tuple-element.15), calls=%async_computation.3 | async-start | bytes 3145728 | tf_op jit(solution)/shard_map/all_to_all | solution.py:292
  180.7 2.5 collective-permute-start.9
  183.2 5.5 %collective-permute-done.9 = f32[128,384]{1,0:T(8,128)S(1)} collective-permute-done((f32[128,384]{1,0:T(8,128)S(1)}, f32[128,384]{1,0:T(8,128)S(1)}, u32[]{:S(2)}, u32[]{:S(2)}) %collective-permute-start.9) | collective-permute-done | bytes 196640 | tf_op jit(solution)/shard_map/ppermute | solution.py:290
  188.8 0.8 broadcast_in_dim.39
  189.6 11.6 %all-to-all-done.3.in_ref = bf16[8,128,768]{2,1,0:T(8,128)(2,1)S(1)} async-done(((bf16[8,128,768]{2,1,0:T(8,128)(2,1)}), bf16[8,128,768]{2,1,0:T(8,128)(2,1)S(1)}, u32[]{:S(2)}, u32[]{:S(2)}) %all-to-all-start.3) | async-done | bytes 1572896 | tf_op jit(solution)/shard_map/all_to_all | solution.py:292
  201.2 1.2 copy-done
  202.4 48.9 %assemble.1 = bf16[128,6144]{1,0:T(8,128)(2,1)} custom-call(bf16[8,128,768]{2,1,0:T(8,128)(2,1)} %copy-done), custom_call_target="tpu_custom_call" | custom-call | tf_op jit(solution)/shard_map/assemble/pallas_call | solution.py:205
  (27 shorter events, 0.2 us)
Async XLA Ops:
  8.2 9.5 %copy-start.3 = (bf16[1,1,588,128]{3,2,1,0:T(8,128)(2,1)S(1)}, bf16[1,1,588,128]{3,2,1,0:T(8,128)(2,1)}, u32[]{:S(2)}) copy-start(bf16[1,1,588,128]{3,2,1,0:T(8,128)(2,1)} %param.10) | copy-start | bytes 451588
  8.2 9.5 %copy-start.4 = (bf16[1,588,128]{2,1,0:T(8,128)(2,1)S(1)}, bf16[1,588,128]{2,1,0:T(8,128)(2,1)}, u32[]{:S(2)}) copy-start(bf16[1,588,128]{2,1,0:T(8,128)(2,1)} %param.9) | copy-start | bytes 451588
  9.3 24.6 %all-to-all-start = ((bf16[16,80,384]{2,1,0:T(8,128)(2,1)}), bf16[16,80,384]{2,1,0:T(8,128)(2,1)S(1)}, u32[]{:S(2)}, u32[]{:S(2)}) async-start(bf16[16,80,384]{2,1,0:T(8,128)(2,1)} %bitcast.6), calls=%async_computation | async-start | bytes 1966080 | tf_op jit(solution)/shard_map/all_to_all | solution.py:239
  17.7 56.8 %all-gather.6.cloned.1.call-start = ((), (), s32[]{:S(2)}) async-start(), calls=%async_computation.5 | async-start | bytes 1769472 | tf_op jit(solution)/shard_map/all_gather | solution.py:247
  33.9 2.6 copy-start.1
  33.9 2.6 copy-start.2
  36.5 36.8 %collective-permute-start = (bf16[588,384]{1,0:T(8,128)(2,1)S(1)}, bf16[588,384]{1,0:T(8,128)(2,1)S(1)}, u32[]{:S(2)}, u32[]{:S(2)}) collective-permute-start(bf16[588,384]{1,0:T(8,128)(2,1)S(1)} %copy-done.2), channel_id=1, source_target_pairs={{0,16},{16,0},{1,17},{17,1},{2,18},{18,2},{3,19},{19,3},{4,20},{20... | collective-permute-start | bytes 1354760 | tf_op jit(solution)/shard_map/ppermute | solution.py:259
  48.1 7.6 %collective-permute-start.1 = (bf16[96,1152]{1,0:T(8,128)(2,1)}, bf16[96,1152]{1,0:T(8,128)(2,1)S(1)}, u32[]{:S(2)}, u32[]{:S(2)}) collective-permute-start(bf16[96,1152]{1,0:T(8,128)(2,1)} %join_weights.1), channel_id=1, source_target_pairs={{0,0},{1,8},{2,32},{3,40},{4,64},{5,72},{6,96},{7,104},{16,16},{17... | collective-permute-start | bytes 663560 | tf_op jit(solution)/shard_map/ppermute | solution.py:35
  57.1 38.9 %all-to-all-start.1 = ((bf16[8,96,1152]{2,1,0:T(8,128)(2,1)}), bf16[8,96,1152]{2,1,0:T(8,128)(2,1)}, u32[]{:S(2)}, u32[]{:S(2)}) async-start(bf16[8,96,1152]{2,1,0:T(8,128)(2,1)} %broadcast_in_dim.36), calls=%async_computation.1 | async-start | bytes 3538944 | tf_op jit(solution)/shard_map/all_to_all | solution.py:257
  73.2 89.4 %all-gather.4.cloned.1.call-start = ((), (), s32[]{:S(2)}) async-start(), calls=%async_computation.4 | async-start | bytes 7077888 | tf_op jit(solution)/shard_map/all_gather | solution.py:283
  80.9 8.7 %collective-permute-start.8 = (f32[2,8,128]{2,1,0:T(8,128)S(1)}, f32[2,8,128]{2,1,0:T(8,128)S(1)}, u32[]{:S(2)}, u32[]{:S(2)}) collective-permute-start(f32[2,8,128]{2,1,0:T(8,128)S(1)} %pad_maximum_fusion.4), channel_id=1, source_target_pairs={{0,104},{1,105},{2,106},{3,107},{4,108},{5,109},{6,110},{7,111},{1... | collective-permute-start | bytes 24584 | tf_op jit(solution)/shard_map/ppermute | solution.py:35
  85.9 5.0 %collective-permute-start.7 = (f32[2,8,128]{2,1,0:T(8,128)S(1)}, f32[2,8,128]{2,1,0:T(8,128)S(1)}, u32[]{:S(2)}, u32[]{:S(2)}) collective-permute-start(f32[2,8,128]{2,1,0:T(8,128)S(1)} %pad_maximum_fusion.4), channel_id=1, source_target_pairs={{0,96},{1,97},{2,98},{3,99},{4,100},{5,101},{6,102},{7,103},{16,11... | collective-permute-start | bytes 24584 | tf_op jit(solution)/shard_map/ppermute | solution.py:35
  85.9 10.1 %collective-permute-start.6 = (f32[2,8,128]{2,1,0:T(8,128)S(1)}, f32[2,8,128]{2,1,0:T(8,128)S(1)}, u32[]{:S(2)}, u32[]{:S(2)}) collective-permute-start(f32[2,8,128]{2,1,0:T(8,128)S(1)} %pad_maximum_fusion.4), channel_id=1, source_target_pairs={{0,72},{1,73},{2,74},{3,75},{4,76},{5,77},{6,78},{7,79},{16,88},{1... | collective-permute-start | bytes 24584 | tf_op jit(solution)/shard_map/ppermute | solution.py:35
  85.9 10.1 %collective-permute-start.5 = (f32[2,8,128]{2,1,0:T(8,128)S(1)}, f32[2,8,128]{2,1,0:T(8,128)S(1)}, u32[]{:S(2)}, u32[]{:S(2)}) collective-permute-start(f32[2,8,128]{2,1,0:T(8,128)S(1)} %pad_maximum_fusion.4), channel_id=1, source_target_pairs={{0,64},{1,65},{2,66},{3,67},{4,68},{5,69},{6,70},{7,71},{16,80},{1... | collective-permute-start | bytes 24584 | tf_op jit(solution)/shard_map/ppermute | solution.py:35
  89.2 6.7 %collective-permute-start.4 = (f32[2,8,128]{2,1,0:T(8,128)S(1)}, f32[2,8,128]{2,1,0:T(8,128)S(1)}, u32[]{:S(2)}, u32[]{:S(2)}) collective-permute-start(f32[2,8,128]{2,1,0:T(8,128)S(1)} %pad_maximum_fusion.4), channel_id=1, source_target_pairs={{0,40},{1,41},{2,42},{3,43},{4,44},{5,45},{6,46},{7,47},{16,56},{1... | collective-permute-start | bytes 24584 | tf_op jit(solution)/shard_map/ppermute | solution.py:35
  89.5 6.5 %collective-permute-start.3 = (f32[2,8,128]{2,1,0:T(8,128)S(1)}, f32[2,8,128]{2,1,0:T(8,128)S(1)}, u32[]{:S(2)}, u32[]{:S(2)}) collective-permute-start(f32[2,8,128]{2,1,0:T(8,128)S(1)} %pad_maximum_fusion.4), channel_id=1, source_target_pairs={{0,32},{1,33},{2,34},{3,35},{4,36},{5,37},{6,38},{7,39},{16,48},{1... | collective-permute-start | bytes 24584 | tf_op jit(solution)/shard_map/ppermute | solution.py:35
  90.9 5.1 %collective-permute-start.2 = (f32[2,8,128]{2,1,0:T(8,128)S(1)}, f32[2,8,128]{2,1,0:T(8,128)S(1)}, u32[]{:S(2)}, u32[]{:S(2)}) collective-permute-start(f32[2,8,128]{2,1,0:T(8,128)S(1)} %pad_maximum_fusion.4), channel_id=1, source_target_pairs={{0,8},{1,9},{2,10},{3,11},{4,12},{5,13},{6,14},{7,15},{16,24},{17,... | collective-permute-start | bytes 24584 | tf_op jit(solution)/shard_map/ppermute | solution.py:35
  172.3 28.9 %all-to-all-start.3 = ((bf16[8,128,768]{2,1,0:T(8,128)(2,1)}), bf16[8,128,768]{2,1,0:T(8,128)(2,1)S(1)}, u32[]{:S(2)}, u32[]{:S(2)}) async-start(bf16[8,128,768]{2,1,0:T(8,128)(2,1)} %get-tuple-element.15), calls=%async_computation.3 | async-start | bytes 3145728 | tf_op jit(solution)/shard_map/all_to_all | solution.py:292
  180.7 8.0 %collective-permute-start.9 = (f32[128,384]{1,0:T(8,128)S(1)}, f32[128,384]{1,0:T(8,128)S(1)}, u32[]{:S(2)}, u32[]{:S(2)}) collective-permute-start(f32[128,384]{1,0:T(8,128)S(1)} %slice_select_fusion), channel_id=1, source_target_pairs={{0,16},{16,0},{1,17},{17,1},{2,18},{18,2},{3,19},{19,3},{4,20},{20... | collective-permute-start | bytes 589832 | tf_op jit(solution)/shard_map/ppermute | solution.py:290
  201.2 1.2 copy-start
Sparse Core Ops, SparseCore 0:
  36.6 29.5 all-gather.5
  104.0 42.6 all-gather.3

commit v2 on v1

--- a/solution.py
+++ b/solution.py
@@ -30,6 +30,13 @@
     return [(xc, yh, m) for xc in range(8) for yh in range(2) for m in range(8)]
 
 
+NEAR = [
+    [device_id(2 * x + c, yh, ((yh ^ s) * 4 + z)) for x in range(4) for yh in range(2) for c in range(2)]
+    for s in range(2)
+    for z in range(4)
+]
+
+
 def send(array, target):
     pairs = [(device_id(*s), device_id(*target(*s))) for s in everyone()]
     return lax.ppermute(array, AXES, pairs)
@@ -38,12 +45,6 @@
 def pixel_pieces(rows):
     k, n = rows.shape
     return jnp.pad(rows, ((0, PIECES * PIX_ROWS - k), (0, 0))).reshape(PIECES, PIX_ROWS, n)
-
-
-def extended(pixel_rows, pos_rows):
-    n = pixel_rows.shape[1]
-    both = [pixel_pieces(pixel_rows), pos_rows.reshape(PIECES, POS_ROWS, n)]
-    return jnp.concatenate(both, axis=1).reshape(PIECES * ROWS, n)
 
 
 def dot(left, right, dims):
@@ -122,7 +123,8 @@
 
 
 def attention_kernel(
-    lhs_ref, query_w_ref, key_w_ref, value_w_ref, scale_ref, query_gain_ref, key_gain_ref, out_ref, proj_ref, scale_all
+    lhs_ref, query_w_ref, key_w_ref, value_w_ref, query_p_ref, key_p_ref, value_p_ref,
+    scale_ref, query_gain_ref, key_gain_ref, out_ref, proj_ref, scale_all,
 ):
     copies, patches, rows = lhs_ref.shape
 
@@ -135,15 +137,19 @@
             column = jnp.sum(jnp.where(diagonal, row, 0.0), axis=1, keepdims=True)
             scale_all[c] = jnp.broadcast_to(column, (patches, HEAD_DIM))
 
-    weights = jnp.concatenate([query_w_ref[...], key_w_ref[...], value_w_ref[...]], axis=1)
+    weights = jnp.concatenate([query_w_ref[...], key_w_ref[...], value_w_ref[...]], axis=2)
+    weights = weights.reshape(rows, 3 * HEAD_DIM)
     proj_ref[...] = dot(lhs_ref[...].reshape(copies * patches, rows), weights, ((1,), (0,)))
+    query_p, key_p, value_p = (
+        ref[...].astype(f32).reshape(patches, HEAD_DIM) for ref in (query_p_ref, key_p_ref, value_p_ref)
+    )
     ones = jnp.ones((patches, HEAD_DIM), bf16)
     for c in range(copies):
         here = slice(c * patches, (c + 1) * patches)
         scale = scale_all[c]
-        query = head_norm(proj_ref[here, :HEAD_DIM], scale, query_gain_ref[...])
-        key_vec = head_norm(proj_ref[here, HEAD_DIM : 2 * HEAD_DIM], scale, key_gain_ref[...])
-        value = (proj_ref[here, 2 * HEAD_DIM :] * scale).astype(bf16)
+        query = head_norm(proj_ref[here, :HEAD_DIM] + query_p, scale, query_gain_ref[...])
+        key_vec = head_norm(proj_ref[here, HEAD_DIM : 2 * HEAD_DIM] + key_p, scale, key_gain_ref[...])
+        value = ((proj_ref[here, 2 * HEAD_DIM :] + value_p) * scale).astype(bf16)
         exp_scores = jnp.exp(dot(query, key_vec, ((1,), (1,))) * HEAD_DIM ** (-0.5)).astype(bf16)
         mixed = dot(exp_scores, jnp.concatenate([value, ones], axis=1), ((1,), (0,)))
         out_ref[c] = (mixed[:, :HEAD_DIM] / mixed[:, HEAD_DIM:]).astype(bf16)
@@ -151,17 +157,20 @@
 
 def attend(lhs, joined, scale, query_gain, key_gain):
     copies, patches, rows = lhs.shape
-    group_cols = joined.shape[1] // 3
+    group_cols = joined.shape[2] // 3
     heads = group_cols // HEAD_DIM
+
+    def columns(t, count, first):
+        return pl.BlockSpec((PIECES, count, HEAD_DIM), lambda h: (0, first // count, t * heads + h))
+
     return pl.pallas_call(
         attention_kernel,
         out_shape=jax.ShapeDtypeStruct((copies, patches, group_cols), bf16),
         grid=(heads,),
         in_specs=[
             pl.BlockSpec((copies, patches, rows), lambda h: (0, 0, 0)),
-            pl.BlockSpec((rows, HEAD_DIM), lambda h: (0, h)),
-            pl.BlockSpec((rows, HEAD_DIM), lambda h: (0, heads + h)),
-            pl.BlockSpec((rows, HEAD_DIM), lambda h: (0, 2 * heads + h)),
+            *[columns(t, PIX_ROWS, 0) for t in range(3)],
+            *[columns(t, POS_ROWS, PIX_ROWS) for t in range(3)],
             pl.BlockSpec((copies, patches), lambda h: (0, 0)),
             pl.BlockSpec((1, HEAD_DIM), lambda h: (0, 0)),
             pl.BlockSpec((1, HEAD_DIM), lambda h: (0, 0)),
@@ -177,27 +186,16 @@
             bytes_accessed=20 * copies * patches * group_cols,
         ),
         name="attend",
-    )(lhs, joined, joined, joined, scale, query_gain[None], key_gain[None])
-
-
-def assemble_kernel(in_ref, out_ref, sems):
-    shares, _, both = in_ref.shape
+    )(lhs, *[joined] * 6, scale, query_gain[None], key_gain[None])
+
+
+def assemble_kernel(in_ref, out_ref):
+    cores, _, both = in_ref.shape
     cols = both // 2
-    copies = []
-    for g in range(shares):
-        for yb in range(2):
-            start = ((g // 2 * 2 + yb) * 2 + g % 2) * cols
-            copies.append(
-                pltpu.make_async_copy(
-                    in_ref.at[g, :, yb * cols : (yb + 1) * cols],
-                    out_ref.at[:, start : start + cols],
-                    sems.at[g, yb],
-                )
-            )
-    for copy in copies:
-        copy.start()
-    for copy in copies:
-        copy.wait()
+    for yb in range(2):
+        for c in range(cores):
+            start = (yb * cores + c) * cols
+            out_ref[:, start : start + cols] = in_ref[c, :, yb * cols : (yb + 1) * cols]
 
 
 def assemble(moved):
@@ -205,9 +203,9 @@
     return pl.pallas_call(
         assemble_kernel,
         out_shape=jax.ShapeDtypeStruct((patches, shares * both), bf16),
-        in_specs=[pl.BlockSpec(memory_space=pl.ANY)],
-        out_specs=pl.BlockSpec(memory_space=pl.ANY),
-        scratch_shapes=[pltpu.SemaphoreType.DMA((shares, 2))],
+        grid=(shares // 2,),
+        in_specs=[pl.BlockSpec((2, patches, both), lambda i: (i, 0, 0))],
+        out_specs=pl.BlockSpec((patches, 2 * both), lambda i: (0, i)),
         name="assemble",
     )(moved)
 
@@ -236,9 +234,9 @@
 
     mine = pixel_pieces(embed_weight).reshape(4, 1, 2, PIX_ROWS, cols)
     mine = jnp.broadcast_to(mine, (4, 2, 2, PIX_ROWS, cols)).reshape(shares, PIX_ROWS, cols)
-    pixel_rows = lax.all_to_all(mine, DP, 0, 0, tiled=True)
+    pixel_rows = lax.all_to_all(mine, AXES, 0, 0, axis_index_groups=NEAR, tiled=True)
     noisy = (clean_image[0].astype(f32) + 0.5 * noise_draw[0, 0].astype(f32)).astype(bf16)
-    lhs_own = extended(noisy, jnp.eye(patches, dtype=bf16)).T
+    lhs_own = jnp.pad(noisy, ((0, PIECES * PIX_ROWS - noisy.shape[0]), (0, 0))).T
     out_mine = jnp.concatenate(my_columns(out_weight), axis=1)
     out_mine = jnp.broadcast_to(out_mine[None], (8, *out_mine.shape))
     out_mine, lhs_own, pixel_rows, own_weight = lax.optimization_barrier(
@@ -254,16 +252,15 @@
     )
     piece = send(piece, lambda xc, yh, m: (m, yh, xc))
     joined = jnp.broadcast_to(piece[None], (8, *piece.shape))
-    joined = lax.all_to_all(joined, MP, 0, 0, tiled=True).reshape(8 * ROWS, -1)
-
-    other_weight = lax.ppermute(own_weight, "yh", [(0, 1), (1, 0)])
+    joined = lax.all_to_all(joined, MP, 0, 0, tiled=True)
+
+    other_weight = send(own_weight, lambda xc, yh, m: (xc, 1 - yh, m ^ 4))
     first = jnp.where(yhi == 0, embed_weight, other_weight)
     second = jnp.where(yhi == 0, other_weight, embed_weight)
-    weight_two = extended(
-        jnp.concatenate([first, second], axis=1),
-        jnp.concatenate(my_columns(position_table), axis=1),
-    )
-    embedded = jnp.einsum("cpk,kd->cpd", lhs, weight_two, preferred_element_type=f32)
+    weight_two = jnp.concatenate([first, second], axis=1)
+    weight_two = jnp.pad(weight_two, ((0, PIECES * PIX_ROWS - weight_two.shape[0]), (0, 0)))
+    position_two = jnp.concatenate(my_columns(position_table), axis=1).astype(f32)
+    embedded = jnp.einsum("cpk,kd->cpd", lhs, weight_two, preferred_element_type=f32) + position_two
 
     average = jnp.mean(embedded, axis=-1)
     spread = jnp.mean(jnp.square(embedded - average[..., None]), axis=-1)

time: 259 us -> 214 us (0.83)
  Pallas kernels: 66.6 us -> 22.7 us
  starting transfers between devices: 51 us -> 48 us
    pallas_call x1, Pallas kernels: 48.9 us -> 3.58 us  [assemble(): pl.pallas_call(assemble_kernel, out_shape=jax.ShapeDtypeStruct((patches,...]
    ppermute x8 -> x9, starting transfers between devices: 14.3 us -> 14.8 us  [send(): return lax.ppermute(array, AXES, pairs)]
  transfers between devices with their start and end apart: 15 -> 15, of which waited for: 5 -> 5; matrix products, arithmetic and copies ran while one was open for 5% -> 5% of each run, Pallas kernels for 4% -> 5%
where the time goes in v2:
time: 214 us; the launch traced here: 213 us
  blocking collectives  58.7 us (27%)
  starting transfers between devices  48 us (22%)
  waiting for transfers between devices  39.9 us (19%)
  Pallas kernels  22.7 us (11%)
  between operations  14.3 us (7%)
  local copies, waits for them, and re-layouts  13.1 us (6%)
  matrix products  11.2 us (5%)
  other arithmetic  5.02 us (2%)
    all_to_all x1, blocking collectives, block(): out_all = lax.all_to_all(out_mine, MP, 0, 0, tiled=True)  58.7 us
    all_to_all x1, starting transfers between devices, block(): joined = lax.all_to_all(joined, MP, 0, 0, tiled=True)  15 us
    ppermute x9, starting transfers between devices, send(): return lax.ppermute(array, AXES, pairs)  14.8 us
    all_to_all x1, waiting for transfers between devices, block(): lax.all_to_all(mine, AXES, 0, 0, axis_index_groups=NEAR, tiled=True)  13.9 us
    all_to_all x1, waiting for transfers between devices, block(): moved = lax.all_to_all(output.astype(bf16), GROUP, 0, 0, tiled=True)  11.6 us
    pallas_call x1, Pallas kernels, join_weights(): pl.pallas_call(join_kernel, out_shape=jax.ShapeDtypeStruct((ROWS, 3 * gro...  10.4 us
    pallas_call x1, Pallas kernels, attend(): pl.pallas_call(attention_kernel, out_shape=jax.ShapeDtypeStruct((copies,...  8.7 us
    all_to_all x1, starting transfers between devices, block(): lax.all_to_all(mine, AXES, 0, 0, axis_index_groups=NEAR, tiled=True)  8.26 us
  transfers between devices with their start and end apart: 15, of which 5 were waited for; matrix products, arithmetic and copies ran while one was open for 5% of the time, Pallas kernels for 5%

profile of v2, /device:TPU:1, one launch (start us, length us, event | category | flops | bytes accessed | tf_op | source)
XLA Modules:
  0.0 212.9 jit_solution(14749875101779173894)
XLA Ops:
  7.2 1.1 pad.13
  8.3 1.0 broadcast_in_dim.35
  9.3 8.3 %all-to-all-start = ((bf16[16,80,384]{2,1,0:T(8,128)(2,1)}), bf16[16,80,384]{2,1,0:T(8,128)(2,1)S(1)}, u32[]{:S(2)}, u32[]{:S(2)}) async-start(bf16[16,80,384]{2,1,0:T(8,128)(2,1)} %bitcast.4), calls=%async_computation | async-start | bytes 1966080 | tf_op jit(solution)/shard_map/all_to_all | solution.py:237
  17.6 0.0 all-gather.6.cloned.1.call-start
  17.7 0.1 fusion.13
  17.7 0.7 pad_bitcast_fusion
  18.4 1.1 constant_dynamic-slice_fusion.3
  19.5 0.0 copy-start.6
  19.5 0.1 pad_maximum_fusion
  19.6 13.9 %all-to-all-done.pixel_ref = bf16[16,80,384]{2,1,0:T(8,128)(2,1)S(1)} async-done(((bf16[16,80,384]{2,1,0:T(8,128)(2,1)}), bf16[16,80,384]{2,1,0:T(8,128)(2,1)S(1)}, u32[]{:S(2)}, u32[]{:S(2)}) %all-to-all-start) | async-done | bytes 983072 | tf_op jit(solution)/shard_map/all_to_all | solution.py:237
  33.5 2.6 %broadcast_in_dim.16 = bf16[8,384,768]{2,1,0:T(8,128)(2,1)} broadcast(bf16[384,768]{1,0:T(8,128)(2,1)S(1)} %pad_maximum_fusion), dimensions={1,2} | broadcast | bytes 5308416 | tf_op jit(solution)/shard_map/broadcast_in_dim | solution.py:241
  36.0 0.0 all-gather.6.cloned.1.call-update
  36.0 1.2 collective-permute-start
  37.3 10.4 %join_weights.1 = bf16[96,1152]{1,0:T(8,128)(2,1)} custom-call(s32[1]{0:T(128)} %bitcast.7.piece_ref, bf16[16,80,384]{2,1,0:T(8,128)(2,1)} %copy-done.5, bf16[128,6144]{1,0:T(8,128)(2,1)} %pos_ref.1, bf16[128,6144]{1,0:T(8,128)(2,1)} %pos_ref.1, f32[1,6144]{1,0:T(1,128)} %bitcast.127, bf16[3,6144,384]{2,1,0:T(8,128)(2,1)} %bitcast.120), custom_call_target="tpu_custom_call" | custom-call | flops 1358954496 | bytes 14155776 | tf_op jit(solution)/shard_map/join_weights/pallas_call | solution.py:92
  47.7 3.8 %collective-permute-start.1 = (bf16[96,1152]{1,0:T(8,128)(2,1)}, bf16[96,1152]{1,0:T(8,128)(2,1)S(1)}, u32[]{:S(2)}, u32[]{:S(2)}) collective-permute-start(bf16[96,1152]{1,0:T(8,128)(2,1)} %join_weights.1), channel_id=1, source_target_pairs={{0,0},{1,8},{2,32},{3,40},{4,64},{5,72},{6,96},{7,104},{16,16},{17... | collective-permute-start | bytes 663560 | tf_op jit(solution)/shard_map/ppermute | solution.py:42
  51.5 1.0 constant_dynamic-slice_fusion.1
  52.4 2.8 %collective-permute-done.1 = bf16[96,1152]{1,0:T(8,128)(2,1)S(1)} collective-permute-done((bf16[96,1152]{1,0:T(8,128)(2,1)}, bf16[96,1152]{1,0:T(8,128)(2,1)S(1)}, u32[]{:S(2)}, u32[]{:S(2)}) %collective-permute-start.1) | collective-permute-done | bytes 221216 | tf_op jit(solution)/shard_map/ppermute | solution.py:42
  55.3 1.4 broadcast_in_dim.37
  56.7 15.0 %all-to-all-start.1 = ((bf16[8,96,1152]{2,1,0:T(8,128)(2,1)}), bf16[8,96,1152]{2,1,0:T(8,128)(2,1)S(1)}, u32[]{:S(2)}, u32[]{:S(2)}) async-start(bf16[8,96,1152]{2,1,0:T(8,128)(2,1)} %broadcast_in_dim.37), calls=%async_computation.1 | async-start | bytes 3538944 | tf_op jit(solution)/shard_map/all_to_all | solution.py:255
  71.7 0.0 all-gather.4.cloned.1.call-start
  71.8 0.0 collective-permute-done
  71.8 1.0 broadcast_select_fusion.1
  72.8 1.7 copy.12
  74.5 0.0 copy-start.4
  74.5 3.1 %add_reduce_fusion = (f32[8,128]{1,0:T(8,128)S(1)}, f32[8,128,768]{2,1,0:T(8,128)S(1)}) fusion(f32[128,768]{1,0:T(8,128)S(1)} %maximum_convert_fusion, bf16[8,128,640]{2,1,0:T(8,128)(2,1)S(1)} %bitcast.121, bf16[588,384]{1,0:T(8,128)(2,1)} %get-tuple-element.21, bf16[588,384]{1,0:T(8,128)(2,1)} %get-tuple-element.20), kind=kOutput, calls=%fused_computation.2 | convolution fusion | flops 1011645440 | bytes 5756928 | tf_op jit(solution)/shard_map/cpk,kd->cpd/dot_general | solution.py:263
  77.7 0.6 multiply_reduce_fusion
  78.3 4.3 %collective-permute-start.8 = (f32[2,8,128]{2,1,0:T(8,128)S(1)}, f32[2,8,128]{2,1,0:T(8,128)S(1)}, u32[]{:S(2)}, u32[]{:S(2)}) collective-permute-start(f32[2,8,128]{2,1,0:T(8,128)S(1)} %pad_maximum_fusion.1), channel_id=1, source_target_pairs={{0,104},{1,105},{2,106},{3,107},{4,108},{5,109},{6,110},{7,111},{1... | collective-permute-start | bytes 24584 | tf_op jit(solution)/shard_map/ppermute | solution.py:42
  82.7 3.3 %collective-permute-start.5 = (f32[2,8,128]{2,1,0:T(8,128)S(1)}, f32[2,8,128]{2,1,0:T(8,128)S(1)}, u32[]{:S(2)}, u32[]{:S(2)}) collective-permute-start(f32[2,8,128]{2,1,0:T(8,128)S(1)} %pad_maximum_fusion.1), channel_id=1, source_target_pairs={{0,64},{1,65},{2,66},{3,67},{4,68},{5,69},{6,70},{7,71},{16,80},{1... | collective-permute-start | bytes 24584 | tf_op jit(solution)/shard_map/ppermute | solution.py:42
  86.0 0.2 collective-permute-start.4
  86.2 1.5 collective-permute-start.3
  87.7 0.5 collective-permute-start.2
  88.2 6.2 %all-to-all-done.1.query_w_ref.key_w_ref.value_w_ref.query_p_ref.key_p_ref.value_p_ref = bf16[8,96,1152]{2,1,0:T(8,128)(2,1)S(1)} async-done(((bf16[8,96,1152]{2,1,0:T(8,128)(2,1)}), bf16[8,96,1152]{2,1,0:T(8,128)(2,1)S(1)}, u32[]{:S(2)}, u32[]{:S(2)}) %all-to-all-start.1) | async-done | bytes 1769504 | tf_op jit(solution)/shard_map/all_to_all | solution.py:255
  94.4 0.0 collective-permute-done.4
  94.4 0.0 collective-permute-done.3
  94.4 0.7 fusion.18.scale_ref
  95.2 0.5 copy-done
  95.7 8.7 %attend.1 = bf16[8,128,384]{2,1,0:T(8,128)(2,1)} custom-call(bf16[8,128,640]{2,1,0:T(8,128)(2,1)} %bitcast.122, bf16[8,96,1152]{2,1,0:T(8,128)(2,1)} %copy-done, bf16[8,96,1152]{2,1,0:T(8,128)(2,1)} %copy-done, bf16[8,96,1152]{2,1,0:T(8,128)(2,1)} %copy-done, bf16[8,96,1152]{2,1,0:T(8,128)(2,1)} %copy-done, bf16[8,96,1152]{2,1,0:T(8,128)(2,1)} %copy-done, ...), custom_call_target="tpu_custom_call" | custom-call | flops 3019898880 | bytes 7864320 | tf_op jit(solution)/shard_map/attend/pallas_call | solution.py:166
  104.4 0.0 all-gather.4.cloned.1.call-update
  104.4 58.7 %all_to_all.20 = bf16[8,384,768]{2,1,0:T(8,128)(2,1)} all-to-all(bf16[8,384,768]{2,1,0:T(8,128)(2,1)} %broadcast_in_dim.16), channel_id=1, replica_groups=mesh['x'=4,'yh'=2,'core'=2,'yl'=2,'z'=4] {'yl','z'}, dimensions={0} | all-to-all | bytes 9437184 | tf_op jit(solution)/shard_map/all_to_all | solution.py:276
  163.1 8.1 %fusion.35 = f32[1024,768,1]{1,0,2:T(8,128)S(1)} fusion(bf16[8,1024,384]{2,1,0:T(8,128)(2,1)} %all-gather.4.cloned.1.call-done, bf16[8,384,768]{2,1,0:T(8,128)(2,1)} %all_to_all.20), kind=kOutput, calls=%fused_computation.67 | convolution fusion | flops 4831838208 | bytes 14155776 | tf_op jit(solution)/shard_map/gtc,gcd->td/dot_general | solution.py:281
  171.2 2.4 %fusion.2 = (f32[128,768]{1,0:T(8,128)}, bf16[8,128,768]{2,1,0:T(8,128)(2,1)}) fusion(f32[8,128,768]{2,1,0:T(8,128)S(1)} %bitcast.124, f32[8,128,768]{2,1,0:T(8,128)S(1)} %copy-done.2, f32[128,768]{1,0:T(8,128)S(1)} %maximum_convert_fusion), kind=kLoop, calls=%fused_computation.6 | loop fusion | flops 3047424 | bytes 8650752 | tf_op jit(solution)/shard_map/reduce_sum | solution.py:284
  173.6 7.0 %all-to-all-start.3 = ((bf16[8,128,768]{2,1,0:T(8,128)(2,1)}), bf16[8,128,768]{2,1,0:T(8,128)(2,1)S(1)}, u32[]{:S(2)}, u32[]{:S(2)}) async-start(bf16[8,128,768]{2,1,0:T(8,128)(2,1)} %get-tuple-element.15), calls=%async_computation.3 | async-start | bytes 3145728 | tf_op jit(solution)/shard_map/all_to_all | solution.py:289
  180.7 2.8 %collective-permute-start.9 = (f32[128,384]{1,0:T(8,128)S(1)}, f32[128,384]{1,0:T(8,128)S(1)}, u32[]{:S(2)}, u32[]{:S(2)}) collective-permute-start(f32[128,384]{1,0:T(8,128)S(1)} %slice_select_fusion), channel_id=1, source_target_pairs={{0,16},{16,0},{1,17},{17,1},{2,18},{18,2},{3,19},{19,3},{4,20},{20... | collective-permute-start | bytes 589832 | tf_op jit(solution)/shard_map/ppermute | solution.py:287
  183.5 5.2 %collective-permute-done.9 = f32[128,384]{1,0:T(8,128)S(1)} collective-permute-done((f32[128,384]{1,0:T(8,128)S(1)}, f32[128,384]{1,0:T(8,128)S(1)}, u32[]{:S(2)}, u32[]{:S(2)}) %collective-permute-start.9) | collective-permute-done | bytes 196640 | tf_op jit(solution)/shard_map/ppermute | solution.py:287
  188.8 0.8 broadcast_in_dim.40
  189.6 11.6 %all-to-all-done.3.in_ref = bf16[8,128,768]{2,1,0:T(8,128)(2,1)S(1)} async-done(((bf16[8,128,768]{2,1,0:T(8,128)(2,1)}), bf16[8,128,768]{2,1,0:T(8,128)(2,1)S(1)}, u32[]{:S(2)}, u32[]{:S(2)}) %all-to-all-start.3) | async-done | bytes 1572896 | tf_op jit(solution)/shard_map/all_to_all | solution.py:289
  201.2 1.2 copy-done.3
  202.4 3.6 %assemble.1 = bf16[128,6144]{1,0:T(8,128)(2,1)} custom-call(bf16[8,128,768]{2,1,0:T(8,128)(2,1)} %copy-done.3), custom_call_target="tpu_custom_call" | custom-call | tf_op jit(solution)/shard_map/assemble/pallas_call | solution.py:203
  (32 shorter events, 0.2 us)
Async XLA Ops:
  7.2 10.5 %copy-start.8 = (bf16[1,1,588,128]{3,2,1,0:T(8,128)(2,1)S(1)}, bf16[1,1,588,128]{3,2,1,0:T(8,128)(2,1)}, u32[]{:S(2)}) copy-start(bf16[1,1,588,128]{3,2,1,0:T(8,128)(2,1)} %param.10) | copy-start | bytes 451588
  7.2 10.5 %copy-start.9 = (bf16[1,588,128]{2,1,0:T(8,128)(2,1)S(1)}, bf16[1,588,128]{2,1,0:T(8,128)(2,1)}, u32[]{:S(2)}) copy-start(bf16[1,588,128]{2,1,0:T(8,128)(2,1)} %param.9) | copy-start | bytes 451588
  9.3 24.1 %all-to-all-start = ((bf16[16,80,384]{2,1,0:T(8,128)(2,1)}), bf16[16,80,384]{2,1,0:T(8,128)(2,1)S(1)}, u32[]{:S(2)}, u32[]{:S(2)}) async-start(bf16[16,80,384]{2,1,0:T(8,128)(2,1)} %bitcast.4), calls=%async_computation | async-start | bytes 1966080 | tf_op jit(solution)/shard_map/all_to_all | solution.py:237
  17.6 55.2 %all-gather.6.cloned.1.call-start = ((), (), s32[]{:S(2)}) async-start(), calls=%async_computation.5 | async-start | bytes 1474560 | tf_op jit(solution)/shard_map/all_gather | solution.py:245
  19.5 16.5 %copy-start.6 = (bf16[588,384]{1,0:T(8,128)(2,1)S(1)}, bf16[588,384]{1,0:T(8,128)(2,1)}, u32[]{:S(2)}) copy-start(bf16[588,384]{1,0:T(8,128)(2,1)} %param.11) | copy-start | bytes 1354756
  33.4 3.8 %copy-start.5 = (bf16[16,80,384]{2,1,0:T(8,128)(2,1)}, bf16[16,80,384]{2,1,0:T(8,128)(2,1)S(1)}, u32[]{:S(2)}) copy-start(bf16[16,80,384]{2,1,0:T(8,128)(2,1)S(1)} %all-to-all-done.pixel_ref) | copy-start | bytes 2949124
  36.0 35.8 %collective-permute-start = (bf16[588,384]{1,0:T(8,128)(2,1)S(1)}, bf16[588,384]{1,0:T(8,128)(2,1)S(1)}, u32[]{:S(2)}, u32[]{:S(2)}) collective-permute-start(bf16[588,384]{1,0:T(8,128)(2,1)S(1)} %copy-done.6), channel_id=1, source_target_pairs={{0,20},{1,21},{2,22},{3,23},{4,16},{5,17},{6,18},{7,19},{16,4},{17... | collective-permute-start | bytes 1354760 | tf_op jit(solution)/shard_map/ppermute | solution.py:42
  47.7 7.6 %collective-permute-start.1 = (bf16[96,1152]{1,0:T(8,128)(2,1)}, bf16[96,1152]{1,0:T(8,128)(2,1)S(1)}, u32[]{:S(2)}, u32[]{:S(2)}) collective-permute-start(bf16[96,1152]{1,0:T(8,128)(2,1)} %join_weights.1), channel_id=1, source_target_pairs={{0,0},{1,8},{2,32},{3,40},{4,64},{5,72},{6,96},{7,104},{16,16},{17... | collective-permute-start | bytes 663560 | tf_op jit(solution)/shard_map/ppermute | solution.py:42
  56.7 37.7 %all-to-all-start.1 = ((bf16[8,96,1152]{2,1,0:T(8,128)(2,1)}), bf16[8,96,1152]{2,1,0:T(8,128)(2,1)S(1)}, u32[]{:S(2)}, u32[]{:S(2)}) async-start(bf16[8,96,1152]{2,1,0:T(8,128)(2,1)} %broadcast_in_dim.37), calls=%async_computation.1 | async-start | bytes 3538944 | tf_op jit(solution)/shard_map/all_to_all | solution.py:255
  71.7 91.4 %all-gather.4.cloned.1.call-start = ((), (), s32[]{:S(2)}) async-start(), calls=%async_computation.4 | async-start | bytes 7077888 | tf_op jit(solution)/shard_map/all_gather | solution.py:280
  74.5 3.1 %copy-start.4 = (bf16[1024,640]{1,0:T(8,128)(2,1)}, bf16[1024,640]{1,0:T(8,128)(2,1)S(1)}, u32[]{:S(2)}) copy-start(bf16[1024,640]{1,0:T(8,128)(2,1)S(1)} %copy.12) | copy-start | bytes 3932164
  77.7 10.0 %copy-start.1 = (f32[8,128,768]{2,1,0:T(8,128)}, f32[8,128,768]{2,1,0:T(8,128)S(1)}, u32[]{:S(2)}) copy-start(f32[8,128,768]{2,1,0:T(8,128)S(1)} %get-tuple-element.25) | copy-start | bytes 9437188
  78.3 7.9 %collective-permute-start.8 = (f32[2,8,128]{2,1,0:T(8,128)S(1)}, f32[2,8,128]{2,1,0:T(8,128)S(1)}, u32[]{:S(2)}, u32[]{:S(2)}) collective-permute-start(f32[2,8,128]{2,1,0:T(8,128)S(1)} %pad_maximum_fusion.1), channel_id=1, source_target_pairs={{0,104},{1,105},{2,106},{3,107},{4,108},{5,109},{6,110},{7,111},{1... | collective-permute-start | bytes 24584 | tf_op jit(solution)/shard_map/ppermute | solution.py:42
  82.7 5.0 %collective-permute-start.7 = (f32[2,8,128]{2,1,0:T(8,128)S(1)}, f32[2,8,128]{2,1,0:T(8,128)S(1)}, u32[]{:S(2)}, u32[]{:S(2)}) collective-permute-start(f32[2,8,128]{2,1,0:T(8,128)S(1)} %pad_maximum_fusion.1), channel_id=1, source_target_pairs={{0,96},{1,97},{2,98},{3,99},{4,100},{5,101},{6,102},{7,103},{16,11... | collective-permute-start | bytes 24584 | tf_op jit(solution)/shard_map/ppermute | solution.py:42
  82.7 11.7 %collective-permute-start.6 = (f32[2,8,128]{2,1,0:T(8,128)S(1)}, f32[2,8,128]{2,1,0:T(8,128)S(1)}, u32[]{:S(2)}, u32[]{:S(2)}) collective-permute-start(f32[2,8,128]{2,1,0:T(8,128)S(1)} %pad_maximum_fusion.1), channel_id=1, source_target_pairs={{0,72},{1,73},{2,74},{3,75},{4,76},{5,77},{6,78},{7,79},{16,88},{1... | collective-permute-start | bytes 24584 | tf_op jit(solution)/shard_map/ppermute | solution.py:42
  82.7 11.7 %collective-permute-start.5 = (f32[2,8,128]{2,1,0:T(8,128)S(1)}, f32[2,8,128]{2,1,0:T(8,128)S(1)}, u32[]{:S(2)}, u32[]{:S(2)}) collective-permute-start(f32[2,8,128]{2,1,0:T(8,128)S(1)} %pad_maximum_fusion.1), channel_id=1, source_target_pairs={{0,64},{1,65},{2,66},{3,67},{4,68},{5,69},{6,70},{7,71},{16,80},{1... | collective-permute-start | bytes 24584 | tf_op jit(solution)/shard_map/ppermute | solution.py:42
  86.0 8.4 %collective-permute-start.4 = (f32[2,8,128]{2,1,0:T(8,128)S(1)}, f32[2,8,128]{2,1,0:T(8,128)S(1)}, u32[]{:S(2)}, u32[]{:S(2)}) collective-permute-start(f32[2,8,128]{2,1,0:T(8,128)S(1)} %pad_maximum_fusion.1), channel_id=1, source_target_pairs={{0,40},{1,41},{2,42},{3,43},{4,44},{5,45},{6,46},{7,47},{16,56},{1... | collective-permute-start | bytes 24584 | tf_op jit(solution)/shard_map/ppermute | solution.py:42
  86.2 8.2 %collective-permute-start.3 = (f32[2,8,128]{2,1,0:T(8,128)S(1)}, f32[2,8,128]{2,1,0:T(8,128)S(1)}, u32[]{:S(2)}, u32[]{:S(2)}) collective-permute-start(f32[2,8,128]{2,1,0:T(8,128)S(1)} %pad_maximum_fusion.1), channel_id=1, source_target_pairs={{0,32},{1,33},{2,34},{3,35},{4,36},{5,37},{6,38},{7,39},{16,48},{1... | collective-permute-start | bytes 24584 | tf_op jit(solution)/shard_map/ppermute | solution.py:42
  87.7 6.8 %collective-permute-start.2 = (f32[2,8,128]{2,1,0:T(8,128)S(1)}, f32[2,8,128]{2,1,0:T(8,128)S(1)}, u32[]{:S(2)}, u32[]{:S(2)}) collective-permute-start(f32[2,8,128]{2,1,0:T(8,128)S(1)} %pad_maximum_fusion.1), channel_id=1, source_target_pairs={{0,8},{1,9},{2,10},{3,11},{4,12},{5,13},{6,14},{7,15},{16,24},{17,... | collective-permute-start | bytes 24584 | tf_op jit(solution)/shard_map/ppermute | solution.py:42
  94.4 1.3 copy-start
  163.1 8.1 %copy-start.2 = (f32[8,128,768]{2,1,0:T(8,128)S(1)}, f32[8,128,768]{2,1,0:T(8,128)}, u32[]{:S(2)}) copy-start(f32[8,128,768]{2,1,0:T(8,128)} %copy-done.1) | copy-start | bytes 9437188
  173.6 7.0 %copy-start.7 = (f32[128,768]{1,0:T(8,128)S(1)}, f32[128,768]{1,0:T(8,128)}, u32[]{:S(2)}) copy-start(f32[128,768]{1,0:T(8,128)} %get-tuple-element.14) | copy-start | bytes 1179652
  173.6 27.6 %all-to-all-start.3 = ((bf16[8,128,768]{2,1,0:T(8,128)(2,1)}), bf16[8,128,768]{2,1,0:T(8,128)(2,1)S(1)}, u32[]{:S(2)}, u32[]{:S(2)}) async-start(bf16[8,128,768]{2,1,0:T(8,128)(2,1)} %get-tuple-element.15), calls=%async_computation.3 | async-start | bytes 3145728 | tf_op jit(solution)/shard_map/all_to_all | solution.py:289
  180.7 8.0 %collective-permute-start.9 = (f32[128,384]{1,0:T(8,128)S(1)}, f32[128,384]{1,0:T(8,128)S(1)}, u32[]{:S(2)}, u32[]{:S(2)}) collective-permute-start(f32[128,384]{1,0:T(8,128)S(1)} %slice_select_fusion), channel_id=1, source_target_pairs={{0,16},{16,0},{1,17},{17,1},{2,18},{18,2},{3,19},{19,3},{4,20},{20... | collective-permute-start | bytes 589832 | tf_op jit(solution)/shard_map/ppermute | solution.py:287
  201.2 1.2 copy-start.3
Sparse Core Ops, SparseCore 0:
  36.2 28.2 all-gather.5
  104.5 41.4 all-gather.3

commit v3 on v1

v3 whole, which is shorter than its diff:
```python
import jax
import jax.numpy as jnp
from jax import lax
from jax.experimental import pallas as pl
from jax.experimental.pallas import tpu as pltpu
from jax.sharding import Mesh
from jax.sharding import PartitionSpec as P


HEAD_DIM = 128
epsilon = 1e-06
bf16 = jnp.bfloat16
f32 = jnp.float32

AXES = ("x", "yh", "core", "yl", "z")
GROUP = ("x", "core")
DP = ("x", "yh", "core")
MP = ("yl", "z")
PIECES = 16
ROWS = 48
PIX_ROWS = 13 * ROWS
LHS_ROWS = 640


def device_id(xc, yh, m):
    return (((xc // 2) * 2 + yh) * 2 + xc % 2) * 8 + m


def everyone():
    return [(xc, yh, m) for xc in range(8) for yh in range(2) for m in range(8)]


NEAR = [
    [device_id(2 * x + c, yh, ((yh ^ s) * 4 + z)) for x in range(4) for yh in range(2) for c in range(2)]
    for s in range(2)
    for z in range(4)
]
HOLDERS = [
    [device_id(xc, yh, 2 * x + c) for x in range(4) for yh in range(2) for c in range(2)] for xc in range(8)
]


def send(array, target):
    pairs = [(device_id(*s), device_id(*target(*s))) for s in everyone()]
    return lax.ppermute(array, AXES, pairs)


def padded(rows, count):
    return jnp.pad(rows, ((0, count - rows.shape[0]), (0, 0)))


def dot(left, right, dims):
    return lax.dot_general(left, right, (dims, ((), ())), preferred_element_type=f32)


def join_kernel(rows_ref, gain_ref, qkv_ref, out_ref, mean_ref, acc_ref):
    step = pl.program_id(0)
    shares, _, cols = rows_ref.shape

    @pl.when(step == 0)
    def _():
        total = jnp.zeros((ROWS, HEAD_DIM), f32)
        for k in range(shares):
            for j in range(cols // HEAD_DIM):
                total += rows_ref[k, :, j * HEAD_DIM : (j + 1) * HEAD_DIM].astype(f32)
        mean = jnp.sum(total, axis=1, keepdims=True) * (1.0 / (shares * cols))
        mean_ref[...] = jnp.broadcast_to(mean, (ROWS, HEAD_DIM))
        acc_ref[...] = jnp.zeros_like(acc_ref)

    per_step = qkv_ref.shape[1] // cols
    rows = jnp.concatenate([rows_ref[per_step * step + k] for k in range(per_step)], axis=1)
    centred = ((rows.astype(f32) - mean_ref[:, :1]) * gain_ref[...]).astype(bf16)
    qkv = jnp.concatenate([qkv_ref[t] for t in range(3)], axis=1)
    acc_ref[...] += dot(centred, qkv, ((1,), (0,)))

    @pl.when(step == pl.num_programs(0) - 1)
    def _():
        for j in range(acc_ref.shape[1] // HEAD_DIM):
            lanes = slice(j * HEAD_DIM, (j + 1) * HEAD_DIM)
            block = acc_ref[:, lanes]
            if 3 * j < 2 * (acc_ref.shape[1] // HEAD_DIM):
                block = block - jnp.mean(block, axis=1, keepdims=True)
            out_ref[:, lanes] = block.astype(bf16)


def join_weights(rows, gain, qkv):
    shares, _, cols = rows.shape
    width, group_cols = qkv.shape[1:]
    per_step = 2
    return pl.pallas_call(
        join_kernel,
        out_shape=jax.ShapeDtypeStruct((ROWS, 3 * group_cols), bf16),
        grid=(shares // per_step,),
        in_specs=[
            pl.BlockSpec((shares, ROWS, cols), lambda i: (0, 0, 0)),
            pl.BlockSpec((1, per_step * cols), lambda i: (0, i)),
            pl.BlockSpec((3, per_step * cols, group_cols), lambda i: (0, i, 0)),
        ],
        out_specs=pl.BlockSpec((ROWS, 3 * group_cols), lambda i: (0, 0)),
        scratch_shapes=[
            pltpu.VMEM((ROWS, HEAD_DIM), f32),
            pltpu.VMEM((ROWS, 3 * group_cols), f32),
        ],
        cost_estimate=pl.CostEstimate(
            flops=6 * width * ROWS * group_cols,
            transcendentals=0,
            bytes_accessed=6 * width * group_cols,
        ),
        name="join_weights",
    )(rows, gain, qkv)


def head_norm(centred, scale, gain):
    variance = jnp.mean(centred * centred, axis=-1, keepdims=True)
    return (centred * (scale * lax.rsqrt(variance * (scale * scale) + epsilon)) * gain).astype(bf16)


def attention_kernel(
    lhs_ref, query_w_ref, key_w_ref, value_w_ref, query_p_ref, key_p_ref, value_p_ref,
    scale_ref, query_gain_ref, key_gain_ref, out_ref, proj_ref, scale_all,
):
    copies, patches, rows = lhs_ref.shape

    @pl.when(pl.program_id(0) == 0)
    def _():
        shape = (patches, patches)
        diagonal = lax.broadcasted_iota(jnp.int32, shape, 0) == lax.broadcasted_iota(jnp.int32, shape, 1)
        for c in range(copies):
            row = jnp.broadcast_to(scale_ref[c : c + 1, :], shape)
            column = jnp.sum(jnp.where(diagonal, row, 0.0), axis=1, keepdims=True)
            scale_all[c] = jnp.broadcast_to(column, (patches, HEAD_DIM))

    weights = jnp.concatenate([query_w_ref[...], key_w_ref[...], value_w_ref[...]], axis=1)
    proj_ref[...] = dot(lhs_ref[...].reshape(copies * patches, rows), weights, ((1,), (0,)))
    first = PIX_ROWS % query_p_ref.shape[0]
    query_p, key_p, value_p = (
        ref[first : first + patches].astype(f32) for ref in (query_p_ref, key_p_ref, value_p_ref)
    )
    ones = jnp.ones((patches, HEAD_DIM), bf16)
    for c in range(copies):
        here = slice(c * patches, (c + 1) * patches)
        scale = scale_all[c]
        query = head_norm(proj_ref[here, :HEAD_DIM] + query_p, scale, query_gain_ref[...])
        key_vec = head_norm(proj_ref[here, HEAD_DIM : 2 * HEAD_DIM] + key_p, scale, key_gain_ref[...])
        value = ((proj_ref[here, 2 * HEAD_DIM :] + value_p) * scale).astype(bf16)
        exp_scores = jnp.exp(dot(query, key_vec, ((1,), (1,))) * HEAD_DIM ** (-0.5)).astype(bf16)
        mixed = dot(exp_scores, jnp.concatenate([value, ones], axis=1), ((1,), (0,)))
        out_ref[c] = (mixed[:, :HEAD_DIM] / mixed[:, HEAD_DIM:]).astype(bf16)


def attend(lhs, joined, scale, query_gain, key_gain):
    copies, patches, rows = lhs.shape
    group_cols = joined.shape[1] // 3
    heads = group_cols // HEAD_DIM
    tail = 256

    def columns(t, count, block):
        return pl.BlockSpec((count, HEAD_DIM), lambda h: (block, t * heads + h))

    return pl.pallas_call(
        attention_kernel,
        out_shape=jax.ShapeDtypeStruct((copies, patches, group_cols), bf16),
        grid=(heads,),
        in_specs=[
            pl.BlockSpec((copies, patches, rows), lambda h: (0, 0, 0)),
            *[columns(t, rows, 0) for t in range(3)],
            *[columns(t, tail, PIX_ROWS // tail) for t in range(3)],
            pl.BlockSpec((copies, patches), lambda h: (0, 0)),
            pl.BlockSpec((1, HEAD_DIM), lambda h: (0, 0)),
            pl.BlockSpec((1, HEAD_DIM), lambda h: (0, 0)),
        ],
        out_specs=pl.BlockSpec((copies, patches, HEAD_DIM), lambda h: (0, 0, h)),
        scratch_shapes=[
            pltpu.VMEM((copies * patches, 3 * HEAD_DIM), f32),
            pltpu.VMEM((copies, patches, HEAD_DIM), f32),
        ],
        cost_estimate=pl.CostEstimate(
            flops=4 * copies * rows * patches * group_cols * 3,
            transcendentals=copies * patches * group_cols,
            bytes_accessed=20 * copies * patches * group_cols,
        ),
        name="attend",
    )(lhs, *[joined] * 6, scale, query_gain[None], key_gain[None])


def assemble_kernel(in_ref, out_ref, sems):
    shares, _, both = in_ref.shape
    cols = both // 2
    copies = []
    for g in range(shares):
        for yb in range(2):
            start = ((g // 2 * 2 + yb) * 2 + g % 2) * cols
            copies.append(
                pltpu.make_async_copy(
                    in_ref.at[g, :, yb * cols : (yb + 1) * cols],
                    out_ref.at[:, start : start + cols],
                    sems.at[g, yb],
                )
            )
    for copy in copies:
        copy.start()
    for copy in copies:
        copy.wait()


def assemble(moved):
    shares, patches, both = moved.shape
    return pl.pallas_call(
        assemble_kernel,
        out_shape=jax.ShapeDtypeStruct((patches, shares * both), bf16),
        in_specs=[pl.BlockSpec(memory_space=pltpu.VMEM)],
        out_specs=pl.BlockSpec(memory_space=pl.ANY),
        scratch_shapes=[pltpu.SemaphoreType.DMA((shares, 2))],
        name="assemble",
    )(moved)


def block(
    clean_image,
    noise_draw,
    embed_weight,
    position_table,
    norm_gain,
    qkv_weight,
    query_gain,
    key_gain,
    out_weight,
):
    xi, yhi, ci = (lax.axis_index(a) for a in ("x", "yh", "core"))
    patches, width = position_table.shape
    cols = embed_weight.shape[1]

    def my_columns(array):
        start = (xi * 4 + ci) * cols
        return [
            lax.dynamic_slice_in_dim(array, start + yb * 2 * cols, cols, axis=1) for yb in range(2)
        ]

    position_here = lax.dynamic_slice_in_dim(position_table, lax.axis_index(DP) * cols, cols, axis=1)
    rows = [padded(embed_weight, PIX_ROWS), padded(position_here, PIECES * ROWS - PIX_ROWS)]
    rows = jnp.concatenate(rows, axis=0).reshape(PIECES, ROWS, cols)
    rows = lax.all_to_all(rows, AXES, 0, 0, axis_index_groups=NEAR, tiled=True)
    noisy = (clean_image[0].astype(f32) + 0.5 * noise_draw[0, 0].astype(f32)).astype(bf16)
    lhs_own = padded(noisy, LHS_ROWS).T
    out_mine = jnp.concatenate(my_columns(out_weight), axis=1)
    out_mine = jnp.broadcast_to(out_mine[None], (8, *out_mine.shape))
    out_mine, lhs_own, rows, own_weight = lax.optimization_barrier(
        (out_mine, lhs_own, rows, embed_weight)
    )
    lhs = lax.all_gather(lhs_own, GROUP)
    piece = join_weights(rows, norm_gain[None], jnp.transpose(qkv_weight, (1, 0, 2)))
    piece = send(piece, lambda xc, yh, m: (m, yh, xc))
    joined = jnp.broadcast_to(piece[None], (PIECES, *piece.shape))
    joined = lax.all_to_all(joined, AXES, 0, 0, axis_index_groups=HOLDERS, tiled=True)
    joined = joined.reshape(PIECES * ROWS, -1)

    other_weight = send(own_weight, lambda xc, yh, m: (xc, 1 - yh, m ^ 4))
    first = jnp.where(yhi == 0, embed_weight, other_weight)
    second = jnp.where(yhi == 0, other_weight, embed_weight)
    weight_two = jnp.concatenate([first, second], axis=1)
    weight_two = padded(weight_two, LHS_ROWS)
    position_two = jnp.concatenate(my_columns(position_table), axis=1).astype(f32)
    embedded = jnp.einsum("cpk,kd->cpd", lhs, weight_two, preferred_element_type=f32) + position_two

    average = jnp.mean(embedded, axis=-1)
    spread = jnp.mean(jnp.square(embedded - average[..., None]), axis=-1)
    stat = jnp.stack([average, spread])
    stats = [stat]
    for k in range(1, 8):
        stats.append(send(stat, lambda xc, yh, m, k=k: (xc ^ k, yh, m)))
    average = sum(each[0] for each in stats) * 0.125
    spread = sum(each[1] + jnp.square(each[0] - average) for each in stats) * 0.125
    scale = lax.rsqrt(spread + epsilon)

    out_mine, joined = lax.optimization_barrier((out_mine, joined))
    out_all = lax.all_to_all(out_mine, MP, 0, 0, tiled=True)

    head_out = attend(lhs, joined, scale, query_gain, key_gain)
    head_out = head_out.reshape(8 * patches, -1)
    head_all = lax.all_gather(head_out, GROUP)
    attention = jnp.einsum("gtc,gcd->td", head_all, out_all, preferred_element_type=f32)
    output = embedded + attention.reshape(8, patches, 2 * cols)

    summed = jnp.sum(output, axis=0) * (1.0 / 16)
    kept = jnp.where(yhi == 0, summed[:, :cols], summed[:, cols:])
    sent = jnp.where(yhi == 0, summed[:, cols:], summed[:, :cols])
    smoothed = (kept + lax.ppermute(sent, "yh", [(0, 1), (1, 0)]))[:, None, :]

    moved = lax.all_to_all(output.astype(bf16), GROUP, 0, 0, tiled=True)
    features = assemble(moved).reshape(patches, 1, 1, width)
    return features, smoothed


def solution(mesh):
    fine = Mesh(mesh.devices.reshape(4, 2, 2, 2, 4), AXES)
    placed = (
        P(MP, None, None),
        P(MP, DP, None, None),
        P(None, DP),
        P(),
        P(),
        P(None, None, MP),
        P(),
        P(),
        P(MP, None),
    )
    return jax.shard_map(
        block,
        mesh=fine,
        in_specs=placed,
        out_specs=(P(None, DP, MP, None), P(None, MP, DP)),
        check_vma=False,
    )
```

time: 259 us -> 205 us (0.79)
  Pallas kernels: 66.6 us -> 21.4 us
  starting transfers between devices: 51 us -> 45.4 us
  waiting for transfers between devices: 38.6 us -> 34.8 us
  other arithmetic: 5.08 us -> 7.88 us
    pallas_call x1, Pallas kernels: 48.9 us -> 2.67 us  [assemble(): pl.pallas_call(assemble_kernel, out_shape=jax.ShapeDtypeStruct((patches,...]
    all_to_all x2, waiting for transfers between devices: 18.6 us -> 14.9 us  [the longest x1 8.48 us: block(): rows = lax.all_to_all(rows, AXES, 0, 0, axis_index_groups=NEAR, tiled=True)]
    all_to_all x2, starting transfers between devices: 24.5 us -> 21.1 us  [the longest x1 12.8 us: block(): lax.all_to_all(joined, AXES, 0, 0, axis_index_groups=HOLDERS, tiled=True)]
    ppermute x8 -> x9, starting transfers between devices: 14.3 us -> 13.9 us  [send(): return lax.ppermute(array, AXES, pairs)]
  transfers between devices with their start and end apart: 15 -> 15, of which waited for: 5 -> 5; matrix products, arithmetic and copies ran while one was open for 5% -> 6% of each run, Pallas kernels for 4% -> 5%
where the time goes in v3:
time: 205 us; the launch traced here: 204 us
  blocking collectives  58 us (28%)
  starting transfers between devices  45.4 us (22%)
  waiting for transfers between devices  34.8 us (17%)
  Pallas kernels  21.4 us (10%)
  between operations  14.3 us (7%)
  matrix products  11.2 us (5%)
  local copies, waits for them, and re-layouts  11 us (5%)
  other arithmetic  7.88 us (4%)
    all_to_all x1, blocking collectives, block(): out_all = lax.all_to_all(out_mine, MP, 0, 0, tiled=True)  58 us
    ppermute x9, starting transfers between devices, send(): return lax.ppermute(array, AXES, pairs)  13.9 us
    all_to_all x1, starting transfers between devices, block(): lax.all_to_all(joined, AXES, 0, 0, axis_index_groups=HOLDERS, tiled=True)  12.8 us
    all_to_all x1, waiting for transfers between devices, block(): moved = lax.all_to_all(output.astype(bf16), GROUP, 0, 0, tiled=True)  11.8 us
    pallas_call x1, Pallas kernels, join_weights(): pl.pallas_call(join_kernel, out_shape=jax.ShapeDtypeStruct((ROWS, 3 * gro...  10 us
    pallas_call x1, Pallas kernels, attend(): pl.pallas_call(attention_kernel, out_shape=jax.ShapeDtypeStruct((copies,...  8.76 us
    all_to_all x1, waiting for transfers between devices, block(): rows = lax.all_to_all(rows, AXES, 0, 0, axis_index_groups=NEAR, tiled=True)  8.48 us
    all_to_all x1, starting transfers between devices, block(): rows = lax.all_to_all(rows, AXES, 0, 0, axis_index_groups=NEAR, tiled=True)  8.26 us
  transfers between devices with their start and end apart: 15, of which 5 were waited for; matrix products, arithmetic and copies ran while one was open for 6% of the time, Pallas kernels for 5%

profile of v3, /device:TPU:1, one launch (start us, length us, event | category | flops | bytes accessed | tf_op | source)
XLA Modules:
  0.0 204.0 jit_solution(2624070991593690102)
XLA Ops:
  7.2 1.0 constant_dynamic-slice_fusion.1
  8.2 1.9 fusion.14
  10.1 8.3 %all-to-all-start = ((bf16[16,48,384]{2,1,0:T(8,128)(2,1)}), bf16[16,48,384]{2,1,0:T(8,128)(2,1)S(1)}, u32[]{:S(2)}, u32[]{:S(2)}) async-start(bf16[16,48,384]{2,1,0:T(8,128)(2,1)} %bitcast.3), calls=%async_computation | async-start | bytes 1179648 | tf_op jit(solution)/shard_map/all_to_all | solution.py:242
  18.4 0.0 all-gather.6.cloned.1.call-start
  18.4 1.0 fusion.16
  19.4 0.7 pad_bitcast_fusion
  20.1 1.1 constant_dynamic-slice_fusion.4
  21.2 0.0 copy-start.6
  21.3 0.1 pad_maximum_fusion
  21.3 8.5 %all-to-all-done.rows_ref = bf16[16,48,384]{2,1,0:T(8,128)(2,1)S(1)} async-done(((bf16[16,48,384]{2,1,0:T(8,128)(2,1)}), bf16[16,48,384]{2,1,0:T(8,128)(2,1)S(1)}, u32[]{:S(2)}, u32[]{:S(2)}) %all-to-all-start) | async-done | bytes 589856 | tf_op jit(solution)/shard_map/all_to_all | solution.py:242
  29.8 2.6 %broadcast_in_dim.12 = bf16[8,384,768]{2,1,0:T(8,128)(2,1)} broadcast(bf16[384,768]{1,0:T(8,128)(2,1)S(1)} %pad_maximum_fusion), dimensions={1,2} | broadcast | bytes 5308416 | tf_op jit(solution)/shard_map/broadcast_in_dim | solution.py:246
  32.3 0.0 all-gather.6.cloned.1.call-update
  32.4 1.4 collective-permute-start
  33.8 10.0 %join_weights.1 = bf16[48,1152]{1,0:T(8,128)(2,1)} custom-call(bf16[16,48,384]{2,1,0:T(8,128)(2,1)} %copy-done.5, f32[1,6144]{1,0:T(1,128)} %bitcast.131, bf16[3,6144,384]{2,1,0:T(8,128)(2,1)} %bitcast.125), custom_call_target="tpu_custom_call" | custom-call | flops 679477248 | bytes 14155776 | tf_op jit(solution)/shard_map/join_weights/pallas_call | solution.py:90
  43.8 3.8 %collective-permute-start.1 = (bf16[48,1152]{1,0:T(8,128)(2,1)}, bf16[48,1152]{1,0:T(8,128)(2,1)S(1)}, u32[]{:S(2)}, u32[]{:S(2)}) collective-permute-start(bf16[48,1152]{1,0:T(8,128)(2,1)} %join_weights.1), channel_id=1, source_target_pairs={{0,0},{1,8},{2,32},{3,40},{4,64},{5,72},{6,96},{7,104},{16,16},{17... | collective-permute-start | bytes 331784 | tf_op jit(solution)/shard_map/ppermute | solution.py:45
  47.5 3.0 %collective-permute-done.1 = bf16[48,1152]{1,0:T(8,128)(2,1)S(1)} collective-permute-done((bf16[48,1152]{1,0:T(8,128)(2,1)}, bf16[48,1152]{1,0:T(8,128)(2,1)S(1)}, u32[]{:S(2)}, u32[]{:S(2)}) %collective-permute-start.1) | collective-permute-done | bytes 110624 | tf_op jit(solution)/shard_map/ppermute | solution.py:45
  50.6 1.4 broadcast_in_dim.28
  52.0 12.8 %all-to-all-start.1 = ((bf16[16,48,1152]{2,1,0:T(8,128)(2,1)}), bf16[16,48,1152]{2,1,0:T(8,128)(2,1)S(1)}, u32[]{:S(2)}, u32[]{:S(2)}) async-start(bf16[16,48,1152]{2,1,0:T(8,128)(2,1)} %broadcast_in_dim.28), calls=%async_computation.1 | async-start | bytes 3538944 | tf_op jit(solution)/shard_map/all_to_all | solution.py:254
  64.8 0.0 all-gather.4.cloned.1.call-start
  64.9 1.0 broadcast_select_fusion.1
  65.9 1.7 copy.12
  67.6 0.0 copy-start.4
  67.6 3.1 %add_reduce_fusion = (f32[8,128]{1,0:T(8,128)S(1)}, f32[8,128,768]{2,1,0:T(8,128)S(1)}) fusion(f32[128,768]{1,0:T(8,128)S(1)} %maximum_convert_fusion, bf16[8,128,640]{2,1,0:T(8,128)(2,1)S(1)} %bitcast.126, bf16[588,384]{1,0:T(8,128)(2,1)} %get-tuple-element.22, bf16[588,384]{1,0:T(8,128)(2,1)} %get-tuple-element.21), kind=kOutput, calls=%fused_computation.2 | convolution fusion | flops 1011645440 | bytes 5756928 | tf_op jit(solution)/shard_map/cpk,kd->cpd/dot_general | solution.py:263
  70.8 0.6 multiply_reduce_fusion
  71.4 1.9 collective-permute-start.8
  73.3 1.9 collective-permute-start.7
  75.2 2.5 %collective-permute-start.5 = (f32[2,8,128]{2,1,0:T(8,128)S(1)}, f32[2,8,128]{2,1,0:T(8,128)S(1)}, u32[]{:S(2)}, u32[]{:S(2)}) collective-permute-start(f32[2,8,128]{2,1,0:T(8,128)S(1)} %pad_maximum_fusion.1), channel_id=1, source_target_pairs={{0,64},{1,65},{2,66},{3,67},{4,68},{5,69},{6,70},{7,71},{16,80},{1... | collective-permute-start | bytes 24584 | tf_op jit(solution)/shard_map/ppermute | solution.py:45
  77.7 0.0 collective-permute-start.4
  77.7 0.0 collective-permute-done.8
  77.7 2.5 %collective-permute-start.3 = (f32[2,8,128]{2,1,0:T(8,128)S(1)}, f32[2,8,128]{2,1,0:T(8,128)S(1)}, u32[]{:S(2)}, u32[]{:S(2)}) collective-permute-start(f32[2,8,128]{2,1,0:T(8,128)S(1)} %pad_maximum_fusion.1), channel_id=1, source_target_pairs={{0,32},{1,33},{2,34},{3,35},{4,36},{5,37},{6,38},{7,39},{16,48},{1... | collective-permute-start | bytes 24584 | tf_op jit(solution)/shard_map/ppermute | solution.py:45
  80.2 0.0 collective-permute-start.2
  80.2 6.4 %all-to-all-done.1 = bf16[16,48,1152]{2,1,0:T(8,128)(2,1)S(1)} async-done(((bf16[16,48,1152]{2,1,0:T(8,128)(2,1)}), bf16[16,48,1152]{2,1,0:T(8,128)(2,1)S(1)}, u32[]{:S(2)}, u32[]{:S(2)}) %all-to-all-start.1) | async-done | bytes 1769504 | tf_op jit(solution)/shard_map/all_to_all | solution.py:254
  86.6 0.0 collective-permute-done.6
  86.6 0.0 collective-permute-done.5
  86.7 0.7 fusion.21.scale_ref
  87.4 0.5 copy-done
  87.9 8.8 %attend.1 = bf16[8,128,384]{2,1,0:T(8,128)(2,1)} custom-call(bf16[8,128,640]{2,1,0:T(8,128)(2,1)} %bitcast.127, bf16[768,1152]{1,0:T(8,128)(2,1)} %bitcast.119, bf16[768,1152]{1,0:T(8,128)(2,1)} %bitcast.120, bf16[768,1152]{1,0:T(8,128)(2,1)} %bitcast.121, bf16[768,1152]{1,0:T(8,128)(2,1)} %bitcast.122, bf16[768,1152]{1,0:T(8,128)(2,1)} %bitcast.123, ...), custom_call_target="tpu_custom_call" | custom-call | flops 3019898880 | bytes 7864320 | tf_op jit(solution)/shard_map/attend/pallas_call | solution.py:160
  96.6 0.0 all-gather.4.cloned.1.call-update
  96.7 58.0 %all_to_all.20 = bf16[8,384,768]{2,1,0:T(8,128)(2,1)} all-to-all(bf16[8,384,768]{2,1,0:T(8,128)(2,1)} %broadcast_in_dim.12), channel_id=1, replica_groups=mesh['x'=4,'yh'=2,'core'=2,'yl'=2,'z'=4] {'yl','z'}, dimensions={0} | all-to-all | bytes 9437184 | tf_op jit(solution)/shard_map/all_to_all | solution.py:276
  154.7 8.1 %fusion.38 = f32[1024,768,1]{1,0,2:T(8,128)S(1)} fusion(bf16[8,1024,384]{2,1,0:T(8,128)(2,1)} %all-gather.4.cloned.1.call-done, bf16[8,384,768]{2,1,0:T(8,128)(2,1)} %all_to_all.20), kind=kOutput, calls=%fused_computation.73 | convolution fusion | flops 4831838208 | bytes 14155776 | tf_op jit(solution)/shard_map/gtc,gcd->td/dot_general | solution.py:281
  162.8 2.4 %fusion.4 = (f32[128,768]{1,0:T(8,128)}, bf16[8,128,768]{2,1,0:T(8,128)(2,1)}) fusion(f32[8,128,768]{2,1,0:T(8,128)S(1)} %bitcast.129, f32[8,128,768]{2,1,0:T(8,128)S(1)} %copy-done.2, f32[128,768]{1,0:T(8,128)S(1)} %maximum_convert_fusion), kind=kLoop, calls=%fused_computation.10 | loop fusion | flops 3047424 | bytes 8650752 | tf_op jit(solution)/shard_map/reduce_sum | solution.py:284
  165.3 7.4 %all-to-all-start.3 = ((bf16[8,128,768]{2,1,0:T(8,128)(2,1)}), bf16[8,128,768]{2,1,0:T(8,128)(2,1)S(1)}, u32[]{:S(2)}, u32[]{:S(2)}) async-start(bf16[8,128,768]{2,1,0:T(8,128)(2,1)} %get-tuple-element.15), calls=%async_computation.3 | async-start | bytes 3145728 | tf_op jit(solution)/shard_map/all_to_all | solution.py:289
  172.7 2.9 %collective-permute-start.9 = (f32[128,384]{1,0:T(8,128)S(1)}, f32[128,384]{1,0:T(8,128)S(1)}, u32[]{:S(2)}, u32[]{:S(2)}) collective-permute-start(f32[128,384]{1,0:T(8,128)S(1)} %slice_select_fusion), channel_id=1, source_target_pairs={{0,16},{16,0},{1,17},{17,1},{2,18},{18,2},{3,19},{19,3},{4,20},{20... | collective-permute-start | bytes 589832 | tf_op jit(solution)/shard_map/ppermute | solution.py:287
  175.6 5.0 %collective-permute-done.9 = f32[128,384]{1,0:T(8,128)S(1)} collective-permute-done((f32[128,384]{1,0:T(8,128)S(1)}, f32[128,384]{1,0:T(8,128)S(1)}, u32[]{:S(2)}, u32[]{:S(2)}) %collective-permute-start.9) | collective-permute-done | bytes 196640 | tf_op jit(solution)/shard_map/ppermute | solution.py:287
  180.7 0.8 broadcast_in_dim.31
  181.5 11.8 %all-to-all-done.3.in_ref = bf16[8,128,768]{2,1,0:T(8,128)(2,1)S(1)} async-done(((bf16[8,128,768]{2,1,0:T(8,128)(2,1)}), bf16[8,128,768]{2,1,0:T(8,128)(2,1)S(1)}, u32[]{:S(2)}, u32[]{:S(2)}) %all-to-all-start.3) | async-done | bytes 1572896 | tf_op jit(solution)/shard_map/all_to_all | solution.py:289
  193.3 1.2 copy-done.3
  194.5 2.7 %assemble.1 = bf16[128,6144]{1,0:T(8,128)(2,1)} custom-call(bf16[8,128,768]{2,1,0:T(8,128)(2,1)} %copy-done.3), custom_call_target="tpu_custom_call" | custom-call | tf_op jit(solution)/shard_map/assemble/pallas_call | solution.py:208
  (27 shorter events, 0.2 us)
Async XLA Ops:
  10.1 19.7 %all-to-all-start = ((bf16[16,48,384]{2,1,0:T(8,128)(2,1)}), bf16[16,48,384]{2,1,0:T(8,128)(2,1)S(1)}, u32[]{:S(2)}, u32[]{:S(2)}) async-start(bf16[16,48,384]{2,1,0:T(8,128)(2,1)} %bitcast.3), calls=%async_computation | async-start | bytes 1179648 | tf_op jit(solution)/shard_map/all_to_all | solution.py:242
  18.4 47.6 %all-gather.6.cloned.1.call-start = ((), (), s32[]{:S(2)}) async-start(), calls=%async_computation.5 | async-start | bytes 1474560 | tf_op jit(solution)/shard_map/all_gather | solution.py:250
  21.2 11.1 %copy-start.6 = (bf16[588,384]{1,0:T(8,128)(2,1)S(1)}, bf16[588,384]{1,0:T(8,128)(2,1)}, u32[]{:S(2)}) copy-start(bf16[588,384]{1,0:T(8,128)(2,1)} %param.11) | copy-start | bytes 1354756
  29.8 4.0 %copy-start.5 = (bf16[16,48,384]{2,1,0:T(8,128)(2,1)}, bf16[16,48,384]{2,1,0:T(8,128)(2,1)S(1)}, u32[]{:S(2)}) copy-start(bf16[16,48,384]{2,1,0:T(8,128)(2,1)S(1)} %all-to-all-done.rows_ref) | copy-start | bytes 1769476
  32.4 32.5 %collective-permute-start = (bf16[588,384]{1,0:T(8,128)(2,1)S(1)}, bf16[588,384]{1,0:T(8,128)(2,1)S(1)}, u32[]{:S(2)}, u32[]{:S(2)}) collective-permute-start(bf16[588,384]{1,0:T(8,128)(2,1)S(1)} %copy-done.6), channel_id=1, source_target_pairs={{0,20},{1,21},{2,22},{3,23},{4,16},{5,17},{6,18},{7,19},{16,4},{17... | collective-permute-start | bytes 1354760 | tf_op jit(solution)/shard_map/ppermute | solution.py:45
  43.8 6.8 %collective-permute-start.1 = (bf16[48,1152]{1,0:T(8,128)(2,1)}, bf16[48,1152]{1,0:T(8,128)(2,1)S(1)}, u32[]{:S(2)}, u32[]{:S(2)}) collective-permute-start(bf16[48,1152]{1,0:T(8,128)(2,1)} %join_weights.1), channel_id=1, source_target_pairs={{0,0},{1,8},{2,32},{3,40},{4,64},{5,72},{6,96},{7,104},{16,16},{17... | collective-permute-start | bytes 331784 | tf_op jit(solution)/shard_map/ppermute | solution.py:45
  52.0 34.7 %all-to-all-start.1 = ((bf16[16,48,1152]{2,1,0:T(8,128)(2,1)}), bf16[16,48,1152]{2,1,0:T(8,128)(2,1)S(1)}, u32[]{:S(2)}, u32[]{:S(2)}) async-start(bf16[16,48,1152]{2,1,0:T(8,128)(2,1)} %broadcast_in_dim.28), calls=%async_computation.1 | async-start | bytes 3538944 | tf_op jit(solution)/shard_map/all_to_all | solution.py:254
  64.8 89.9 %all-gather.4.cloned.1.call-start = ((), (), s32[]{:S(2)}) async-start(), calls=%async_computation.4 | async-start | bytes 7077888 | tf_op jit(solution)/shard_map/all_gather | solution.py:280
  67.6 3.1 %copy-start.4 = (bf16[1024,640]{1,0:T(8,128)(2,1)}, bf16[1024,640]{1,0:T(8,128)(2,1)S(1)}, u32[]{:S(2)}) copy-start(bf16[1024,640]{1,0:T(8,128)(2,1)S(1)} %copy.12) | copy-start | bytes 3932164
  70.8 9.5 %copy-start.1 = (f32[8,128,768]{2,1,0:T(8,128)}, f32[8,128,768]{2,1,0:T(8,128)S(1)}, u32[]{:S(2)}) copy-start(f32[8,128,768]{2,1,0:T(8,128)S(1)} %get-tuple-element.26) | copy-start | bytes 9437188
  71.4 6.3 %collective-permute-start.8 = (f32[2,8,128]{2,1,0:T(8,128)S(1)}, f32[2,8,128]{2,1,0:T(8,128)S(1)}, u32[]{:S(2)}, u32[]{:S(2)}) collective-permute-start(f32[2,8,128]{2,1,0:T(8,128)S(1)} %pad_maximum_fusion.1), channel_id=1, source_target_pairs={{0,104},{1,105},{2,106},{3,107},{4,108},{5,109},{6,110},{7,111},{1... | collective-permute-start | bytes 24584 | tf_op jit(solution)/shard_map/ppermute | solution.py:45
  73.3 6.9 %collective-permute-start.7 = (f32[2,8,128]{2,1,0:T(8,128)S(1)}, f32[2,8,128]{2,1,0:T(8,128)S(1)}, u32[]{:S(2)}, u32[]{:S(2)}) collective-permute-start(f32[2,8,128]{2,1,0:T(8,128)S(1)} %pad_maximum_fusion.1), channel_id=1, source_target_pairs={{0,96},{1,97},{2,98},{3,99},{4,100},{5,101},{6,102},{7,103},{16,11... | collective-permute-start | bytes 24584 | tf_op jit(solution)/shard_map/ppermute | solution.py:45
  75.2 11.4 %collective-permute-start.6 = (f32[2,8,128]{2,1,0:T(8,128)S(1)}, f32[2,8,128]{2,1,0:T(8,128)S(1)}, u32[]{:S(2)}, u32[]{:S(2)}) collective-permute-start(f32[2,8,128]{2,1,0:T(8,128)S(1)} %pad_maximum_fusion.1), channel_id=1, source_target_pairs={{0,72},{1,73},{2,74},{3,75},{4,76},{5,77},{6,78},{7,79},{16,88},{1... | collective-permute-start | bytes 24584 | tf_op jit(solution)/shard_map/ppermute | solution.py:45
  75.2 11.4 %collective-permute-start.5 = (f32[2,8,128]{2,1,0:T(8,128)S(1)}, f32[2,8,128]{2,1,0:T(8,128)S(1)}, u32[]{:S(2)}, u32[]{:S(2)}) collective-permute-start(f32[2,8,128]{2,1,0:T(8,128)S(1)} %pad_maximum_fusion.1), channel_id=1, source_target_pairs={{0,64},{1,65},{2,66},{3,67},{4,68},{5,69},{6,70},{7,71},{16,80},{1... | collective-permute-start | bytes 24584 | tf_op jit(solution)/shard_map/ppermute | solution.py:45
  77.7 8.9 %collective-permute-start.4 = (f32[2,8,128]{2,1,0:T(8,128)S(1)}, f32[2,8,128]{2,1,0:T(8,128)S(1)}, u32[]{:S(2)}, u32[]{:S(2)}) collective-permute-start(f32[2,8,128]{2,1,0:T(8,128)S(1)} %pad_maximum_fusion.1), channel_id=1, source_target_pairs={{0,40},{1,41},{2,42},{3,43},{4,44},{5,45},{6,46},{7,47},{16,56},{1... | collective-permute-start | bytes 24584 | tf_op jit(solution)/shard_map/ppermute | solution.py:45
  77.7 8.9 %collective-permute-start.3 = (f32[2,8,128]{2,1,0:T(8,128)S(1)}, f32[2,8,128]{2,1,0:T(8,128)S(1)}, u32[]{:S(2)}, u32[]{:S(2)}) collective-permute-start(f32[2,8,128]{2,1,0:T(8,128)S(1)} %pad_maximum_fusion.1), channel_id=1, source_target_pairs={{0,32},{1,33},{2,34},{3,35},{4,36},{5,37},{6,38},{7,39},{16,48},{1... | collective-permute-start | bytes 24584 | tf_op jit(solution)/shard_map/ppermute | solution.py:45
  80.2 6.4 %collective-permute-start.2 = (f32[2,8,128]{2,1,0:T(8,128)S(1)}, f32[2,8,128]{2,1,0:T(8,128)S(1)}, u32[]{:S(2)}, u32[]{:S(2)}) collective-permute-start(f32[2,8,128]{2,1,0:T(8,128)S(1)} %pad_maximum_fusion.1), channel_id=1, source_target_pairs={{0,8},{1,9},{2,10},{3,11},{4,12},{5,13},{6,14},{7,15},{16,24},{17,... | collective-permute-start | bytes 24584 | tf_op jit(solution)/shard_map/ppermute | solution.py:45
  86.6 1.3 copy-start
  154.7 8.1 %copy-start.2 = (f32[8,128,768]{2,1,0:T(8,128)S(1)}, f32[8,128,768]{2,1,0:T(8,128)}, u32[]{:S(2)}) copy-start(f32[8,128,768]{2,1,0:T(8,128)} %copy-done.1) | copy-start | bytes 9437188
  165.3 7.4 %copy-start.7 = (f32[128,768]{1,0:T(8,128)S(1)}, f32[128,768]{1,0:T(8,128)}, u32[]{:S(2)}) copy-start(f32[128,768]{1,0:T(8,128)} %get-tuple-element.14) | copy-start | bytes 1179652
  165.3 28.0 %all-to-all-start.3 = ((bf16[8,128,768]{2,1,0:T(8,128)(2,1)}), bf16[8,128,768]{2,1,0:T(8,128)(2,1)S(1)}, u32[]{:S(2)}, u32[]{:S(2)}) async-start(bf16[8,128,768]{2,1,0:T(8,128)(2,1)} %get-tuple-element.15), calls=%async_computation.3 | async-start | bytes 3145728 | tf_op jit(solution)/shard_map/all_to_all | solution.py:289
  172.7 7.9 %collective-permute-start.9 = (f32[128,384]{1,0:T(8,128)S(1)}, f32[128,384]{1,0:T(8,128)S(1)}, u32[]{:S(2)}, u32[]{:S(2)}) collective-permute-start(f32[128,384]{1,0:T(8,128)S(1)} %slice_select_fusion), channel_id=1, source_target_pairs={{0,16},{16,0},{1,17},{17,1},{2,18},{18,2},{3,19},{19,3},{4,20},{20... | collective-permute-start | bytes 589832 | tf_op jit(solution)/shard_map/ppermute | solution.py:287
  193.3 1.2 copy-start.3
Sparse Core Ops, SparseCore 0:
  32.5 25.7 all-gather.5
  96.8 40.0 all-gather.3

commit v4 on v3

--- a/solution.py
+++ b/solution.py
@@ -2,6 +2,7 @@
 import jax.numpy as jnp
 from jax import lax
 from jax.experimental import pallas as pl
+from jax.experimental.layout import Layout, with_layout_constraint
 from jax.experimental.pallas import tpu as pltpu
 from jax.sharding import Mesh
 from jax.sharding import PartitionSpec as P
@@ -236,17 +237,15 @@
             lax.dynamic_slice_in_dim(array, start + yb * 2 * cols, cols, axis=1) for yb in range(2)
         ]
 
+    out_near = lax.all_gather(jnp.concatenate(my_columns(out_weight), axis=1), "z")
+
     position_here = lax.dynamic_slice_in_dim(position_table, lax.axis_index(DP) * cols, cols, axis=1)
     rows = [padded(embed_weight, PIX_ROWS), padded(position_here, PIECES * ROWS - PIX_ROWS)]
     rows = jnp.concatenate(rows, axis=0).reshape(PIECES, ROWS, cols)
     rows = lax.all_to_all(rows, AXES, 0, 0, axis_index_groups=NEAR, tiled=True)
     noisy = (clean_image[0].astype(f32) + 0.5 * noise_draw[0, 0].astype(f32)).astype(bf16)
-    lhs_own = padded(noisy, LHS_ROWS).T
-    out_mine = jnp.concatenate(my_columns(out_weight), axis=1)
-    out_mine = jnp.broadcast_to(out_mine[None], (8, *out_mine.shape))
-    out_mine, lhs_own, rows, own_weight = lax.optimization_barrier(
-        (out_mine, lhs_own, rows, embed_weight)
-    )
+    lhs_own = with_layout_constraint(padded(noisy, LHS_ROWS).T, Layout((0, 1)))
+    lhs_own, rows, own_weight = lax.optimization_barrier((lhs_own, rows, embed_weight))
     lhs = lax.all_gather(lhs_own, GROUP)
     piece = join_weights(rows, norm_gain[None], jnp.transpose(qkv_weight, (1, 0, 2)))
     piece = send(piece, lambda xc, yh, m: (m, yh, xc))
@@ -265,19 +264,28 @@
     average = jnp.mean(embedded, axis=-1)
     spread = jnp.mean(jnp.square(embedded - average[..., None]), axis=-1)
     stat = jnp.stack([average, spread])
-    stats = [stat]
-    for k in range(1, 8):
-        stats.append(send(stat, lambda xc, yh, m, k=k: (xc ^ k, yh, m)))
-    average = sum(each[0] for each in stats) * 0.125
-    spread = sum(each[1] + jnp.square(each[0] - average) for each in stats) * 0.125
+    for partners in ((1,), (2, 4, 6)):
+        stats = [stat]
+        for k in partners:
+            stats.append(send(stat, lambda xc, yh, m, k=k: (xc ^ k, yh, m)))
+        share = 1.0 / len(stats)
+        average = sum(each[0] for each in stats) * share
+        spread = sum(each[1] + jnp.square(each[0] - average) for each in stats) * share
+        stat = jnp.stack([average, spread])
     scale = lax.rsqrt(spread + epsilon)
-
-    out_mine, joined = lax.optimization_barrier((out_mine, joined))
-    out_all = lax.all_to_all(out_mine, MP, 0, 0, tiled=True)
 
     head_out = attend(lhs, joined, scale, query_gain, key_gain)
     head_out = head_out.reshape(8 * patches, -1)
     head_all = lax.all_gather(head_out, GROUP)
+
+    out_near, _ = lax.optimization_barrier((out_near, head_out))
+    out_far = send(out_near, lambda xc, yh, m: (xc, yh ^ (xc & 1), m ^ 4))
+
+    low = lax.axis_index("yl") == 0
+    out_all = jnp.concatenate(
+        [jnp.where(low, out_near, out_far), jnp.where(low, out_far, out_near)], axis=0
+    )
+    out_all = lax.optimization_barrier(out_all)
     attention = jnp.einsum("gtc,gcd->td", head_all, out_all, preferred_element_type=f32)
     output = embedded + attention.reshape(8, patches, 2 * cols)
 

time: 205 us -> 193 us (0.941)
  blocking collectives: 58 us -> 0 us
  waiting for transfers between devices: 34.8 us -> 85.8 us
  starting transfers between devices: 45.4 us -> 40.2 us
  other arithmetic: 7.88 us -> 12.1 us
  local copies, waits for them, and re-layouts: 11 us -> 7.98 us
    all_to_all x1 -> x0, blocking collectives: 58 us -> none  [block(): out_all = lax.all_to_all(out_mine, MP, 0, 0, tiled=True)]
    ppermute x9 -> x7, waiting for transfers between devices: 3.05 us -> 32.2 us  [send(): return lax.ppermute(array, AXES, pairs)]
    all_gather x0 -> x1, waiting for transfers between devices: none -> 8.68 us  [block(): lax.all_gather(jnp.concatenate(my_columns(out_weight), axis=1), 'z')]
    all_gather x1, waiting for transfers between devices: 0.01 us -> 7.18 us  [block(): head_all = lax.all_gather(head_out, GROUP)]
    all_to_all x1, waiting for transfers between devices: 6.38 us -> 10.5 us  [block(): lax.all_to_all(joined, AXES, 0, 0, axis_index_groups=HOLDERS, tiled=True)]
    all_to_all x1, starting transfers between devices: 7.43 us -> 3.88 us  [block(): moved = lax.all_to_all(output.astype(bf16), GROUP, 0, 0, tiled=True)]
    concatenate x1 -> x2, other arithmetic: 0.05 us -> 3.53 us  [the longest x1 2.65 us: block(): jnp.concatenate([jnp.where(low, out_near, out_far), jnp.where(low, out_fa...]
    broadcast_in_dim x1 -> x0, local copies, waits for them, and re-layouts: 2.55 us -> none  [block(): out_mine = jnp.broadcast_to(out_mine[None], (8, *out_mine.shape))]
  transfers between devices with their start and end apart: 15 -> 14, of which waited for: 5 -> 11; matrix products, arithmetic and copies ran while one was open for 6% -> 8% of each run, Pallas kernels for 5% -> 10%
where the time goes in v4:
time: 193 us; the launch traced here: 192 us
  waiting for transfers between devices  85.8 us (44%)
  starting transfers between devices  40.2 us (21%)
  Pallas kernels  21.5 us (11%)
  between operations  14 us (7%)
  other arithmetic  12.1 us (6%)
  matrix products  11 us (6%)
  local copies, waits for them, and re-layouts  7.98 us (4%)
    ppermute x7, waiting for transfers between devices, send(): return lax.ppermute(array, AXES, pairs)  32.2 us
    ppermute x7, starting transfers between devices, send(): return lax.ppermute(array, AXES, pairs)  13 us
    all_to_all x1, starting transfers between devices, block(): lax.all_to_all(joined, AXES, 0, 0, axis_index_groups=HOLDERS, tiled=True)  12.1 us
    all_to_all x1, waiting for transfers between devices, block(): moved = lax.all_to_all(output.astype(bf16), GROUP, 0, 0, tiled=True)  11.8 us
    all_to_all x1, waiting for transfers between devices, block(): lax.all_to_all(joined, AXES, 0, 0, axis_index_groups=HOLDERS, tiled=True)  10.5 us
    all_to_all x1, waiting for transfers between devices, block(): rows = lax.all_to_all(rows, AXES, 0, 0, axis_index_groups=NEAR, tiled=True)  10.3 us
    pallas_call x1, Pallas kernels, join_weights(): pl.pallas_call(join_kernel, out_shape=jax.ShapeDtypeStruct((ROWS, 3 * gro...  10 us
    pallas_call x1, Pallas kernels, attend(): pl.pallas_call(attention_kernel, out_shape=jax.ShapeDtypeStruct((copies,...  8.74 us
  transfers between devices with their start and end apart: 14, of which 11 were waited for; matrix products, arithmetic and copies ran while one was open for 8% of the time, Pallas kernels for 10%

profile of v4, /device:TPU:1, one launch (start us, length us, event | category | flops | bytes accessed | tf_op | source)
XLA Modules:
  0.0 192.5 jit_solution(17760739683561029530)
XLA Ops:
  7.2 1.1 constant_dynamic-slice_fusion.3
  8.3 1.9 fusion.14
  10.2 8.3 %all-to-all-start = ((bf16[16,48,384]{2,1,0:T(8,128)(2,1)}), bf16[16,48,384]{2,1,0:T(8,128)(2,1)S(1)}, u32[]{:S(2)}, u32[]{:S(2)}) async-start(bf16[16,48,384]{2,1,0:T(8,128)(2,1)} %bitcast.3), calls=%async_computation | async-start | bytes 1179648 | tf_op jit(solution)/shard_map/all_to_all | solution.py:245
  18.4 0.0 all-gather.8.cloned.1.call-start
  18.5 0.2 copy.13
  18.7 0.2 copy.14
  18.8 0.1 fusion.16
  18.9 0.7 pad_bitcast_fusion
  19.6 10.3 %all-to-all-done.rows_ref = bf16[16,48,384]{2,1,0:T(8,128)(2,1)S(1)} async-done(((bf16[16,48,384]{2,1,0:T(8,128)(2,1)}), bf16[16,48,384]{2,1,0:T(8,128)(2,1)S(1)}, u32[]{:S(2)}, u32[]{:S(2)}) %all-to-all-start) | async-done | bytes 589856 | tf_op jit(solution)/shard_map/all_to_all | solution.py:245
  29.9 0.0 all-gather.10.cloned.1.call-start
  29.9 1.3 constant_dynamic-slice_fusion.1
  31.2 0.9 pad_maximum_fusion.1
  32.1 1.4 collective-permute-start
  33.5 10.0 %join_weights.1 = bf16[48,1152]{1,0:T(8,128)(2,1)} custom-call(bf16[16,48,384]{2,1,0:T(8,128)(2,1)} %copy-done.4, f32[1,6144]{1,0:T(1,128)} %bitcast.121, bf16[3,6144,384]{2,1,0:T(8,128)(2,1)} %bitcast.113), custom_call_target="tpu_custom_call" | custom-call | flops 679477248 | bytes 14155776 | tf_op jit(solution)/shard_map/join_weights/pallas_call | solution.py:91
  43.5 3.7 %collective-permute-start.1 = (bf16[48,1152]{1,0:T(8,128)(2,1)}, bf16[48,1152]{1,0:T(8,128)(2,1)S(1)}, u32[]{:S(2)}, u32[]{:S(2)}) collective-permute-start(bf16[48,1152]{1,0:T(8,128)(2,1)} %join_weights.1), channel_id=1, source_target_pairs={{0,0},{1,8},{2,32},{3,40},{4,64},{5,72},{6,96},{7,104},{16,16},{17... | collective-permute-start | bytes 331784 | tf_op jit(solution)/shard_map/ppermute | solution.py:46
  47.3 2.8 %collective-permute-done.1 = bf16[48,1152]{1,0:T(8,128)(2,1)S(1)} collective-permute-done((bf16[48,1152]{1,0:T(8,128)(2,1)}, bf16[48,1152]{1,0:T(8,128)(2,1)S(1)}, u32[]{:S(2)}, u32[]{:S(2)}) %collective-permute-start.1) | collective-permute-done | bytes 110624 | tf_op jit(solution)/shard_map/ppermute | solution.py:46
  50.1 1.4 broadcast_in_dim.21
  51.5 12.1 %all-to-all-start.1 = ((bf16[16,48,1152]{2,1,0:T(8,128)(2,1)}), bf16[16,48,1152]{2,1,0:T(8,128)(2,1)S(1)}, u32[]{:S(2)}, u32[]{:S(2)}) async-start(bf16[16,48,1152]{2,1,0:T(8,128)(2,1)} %broadcast_in_dim.21), calls=%async_computation.1 | async-start | bytes 3538944 | tf_op jit(solution)/shard_map/all_to_all | solution.py:253
  63.6 0.0 all-gather.6.cloned.1.call-start
  63.7 0.9 broadcast_select_fusion.3
  64.5 3.0 %add_reduce_fusion = (f32[8,128]{1,0:T(8,128)S(1)}, f32[8,128,768]{2,1,0:T(8,128)S(1)}) fusion(f32[128,768]{1,0:T(8,128)S(1)} %maximum_convert_fusion, bf16[8,128,640]{2,1,0:T(8,128)(2,1)} %bitcast.119, bf16[588,384]{1,0:T(8,128)(2,1)} %get-tuple-element.18, bf16[588,384]{1,0:T(8,128)(2,1)S(1)} %get-tuple-element.17), kind=kOutput, calls=%fused_computation.3 | convolution fusion | flops 1011645440 | bytes 5756928 | tf_op jit(solution)/shard_map/cpk,kd->cpd/dot_general | solution.py:262
  67.5 0.6 multiply_reduce_fusion
  68.2 1.5 collective-permute-start.2
  69.7 0.8 collective-permute-done.2
  70.6 0.1 collective-permute-start.3
  70.7 1.2 collective-permute-start.4
  71.8 2.7 %collective-permute-start.5 = (f32[2,8,128]{2,1,0:T(8,128)S(1)}, f32[2,8,128]{2,1,0:T(8,128)S(1)}, u32[]{:S(2)}, u32[]{:S(2)}) collective-permute-start(f32[2,8,128]{2,1,0:T(8,128)S(1)} %pad_maximum_fusion.3), channel_id=1, source_target_pairs={{0,96},{1,97},{2,98},{3,99},{4,100},{5,101},{6,102},{7,103},{16,11... | collective-permute-start | bytes 24584 | tf_op jit(solution)/shard_map/ppermute | solution.py:46
  74.5 0.5 collective-permute-done.4
  75.0 0.9 collective-permute-done.5
  76.0 0.6 fusion.21.scale_ref
  76.6 10.5 %all-to-all-done.1 = bf16[16,48,1152]{2,1,0:T(8,128)(2,1)S(1)} async-done(((bf16[16,48,1152]{2,1,0:T(8,128)(2,1)}), bf16[16,48,1152]{2,1,0:T(8,128)(2,1)S(1)}, u32[]{:S(2)}, u32[]{:S(2)}) %all-to-all-start.1) | async-done | bytes 1769504 | tf_op jit(solution)/shard_map/all_to_all | solution.py:253
  87.1 1.2 copy-done
  88.3 8.7 %attend.1 = bf16[8,128,384]{2,1,0:T(8,128)(2,1)} custom-call(bf16[8,128,640]{2,1,0:T(8,128)(2,1)} %bitcast.120, bf16[768,1152]{1,0:T(8,128)(2,1)} %bitcast.107, bf16[768,1152]{1,0:T(8,128)(2,1)} %bitcast.108, bf16[768,1152]{1,0:T(8,128)(2,1)} %bitcast.109, bf16[768,1152]{1,0:T(8,128)(2,1)} %bitcast.110, bf16[768,1152]{1,0:T(8,128)(2,1)} %bitcast.111, ...), custom_call_target="tpu_custom_call" | custom-call | flops 3019898880 | bytes 7864320 | tf_op jit(solution)/shard_map/attend/pallas_call | solution.py:161
  97.1 8.7 %all-gather.10.cloned.1.call-done = bf16[1536,768]{1,0:T(8,128)(2,1)} async-done(((bf16[384,768]{1,0:T(8,128)(2,1)}), bf16[1536,768]{1,0:T(8,128)(2,1)}) %all-gather.10.cloned.1.call-update) | async-done | bytes 2359312 | tf_op jit(solution)/shard_map/all_gather | solution.py:240
  105.8 2.4 %collective-permute-start.6 = (bf16[4,384,768]{2,1,0:T(8,128)(2,1)}, bf16[4,384,768]{2,1,0:T(8,128)(2,1)S(1)}, u32[]{:S(2)}, u32[]{:S(2)}) collective-permute-start(bf16[4,384,768]{2,1,0:T(8,128)(2,1)} %bitcast.116), channel_id=1, source_target_pairs={{0,4},{1,5},{2,6},{3,7},{4,0},{5,1},{6,2},{7,3},{16,20},{17,21},{1... | collective-permute-start | bytes 7077896 | tf_op jit(solution)/shard_map/ppermute | solution.py:46
  108.2 27.1 %collective-permute-done.6 = bf16[4,384,768]{2,1,0:T(8,128)(2,1)S(1)} collective-permute-done((bf16[4,384,768]{2,1,0:T(8,128)(2,1)}, bf16[4,384,768]{2,1,0:T(8,128)(2,1)S(1)}, u32[]{:S(2)}, u32[]{:S(2)}) %collective-permute-start.6) | collective-permute-done | bytes 2359328 | tf_op jit(solution)/shard_map/ppermute | solution.py:46
  135.3 2.0 %broadcast_select_fusion.1 = (bf16[4,384,768]{2,1,0:T(8,128)(2,1)S(1)}, bf16[4,384,768]{2,1,0:T(8,128)(2,1)S(1)}) fusion(bf16[4,384,768]{2,1,0:T(8,128)(2,1)} %bitcast.117, bf16[4,384,768]{2,1,0:T(8,128)(2,1)S(1)} %collective-permute-done.6, pred[]{:T(512)S(6)} %eq.10), kind=kLoop, calls=%fused_computation.5 | loop fusion | flops 2359296 | bytes 9437185 | tf_op jit(solution)/shard_map/jit(_where)/select_n | solution.py:286
  137.3 2.6 %pad_maximum_fusion = bf16[8,384,768]{2,1,0:T(8,128)(2,1)} fusion(bf16[4,384,768]{2,1,0:T(8,128)(2,1)S(1)} %get-tuple-element.11, bf16[4,384,768]{2,1,0:T(8,128)(2,1)S(1)} %get-tuple-element.10), kind=kLoop, calls=%fused_computation | loop fusion | flops 2359296 | bytes 9437184 | tf_op jit(solution)/shard_map/concatenate | solution.py:285
  140.0 7.2 %all-gather.6.cloned.1.call-done = bf16[8,1024,384]{2,1,0:T(8,128)(2,1)} async-done(((bf16[1,1024,384]{2,1,0:T(8,128)(2,1)}), bf16[8,1024,384]{2,1,0:T(8,128)(2,1)}) %all-gather.6.cloned.1.call-update) | async-done | bytes 6291472 | tf_op jit(solution)/shard_map/all_gather | solution.py:279
  147.2 8.0 %fusion.38 = f32[1024,768,1]{1,0,2:T(8,128)S(1)} fusion(bf16[8,1024,384]{2,1,0:T(8,128)(2,1)} %all-gather.6.cloned.1.call-done, bf16[8,384,768]{2,1,0:T(8,128)(2,1)} %pad_maximum_fusion), kind=kOutput, calls=%fused_computation.74 | convolution fusion | flops 4831838208 | bytes 14155776 | tf_op jit(solution)/shard_map/gtc,gcd->td/dot_general | solution.py:289
  155.2 2.4 %fusion.4 = (f32[128,768]{1,0:T(8,128)}, bf16[8,128,768]{2,1,0:T(8,128)(2,1)}) fusion(f32[8,128,768]{2,1,0:T(8,128)S(1)} %bitcast.115, f32[8,128,768]{2,1,0:T(8,128)S(1)} %copy-done.2, f32[128,768]{1,0:T(8,128)S(1)} %maximum_convert_fusion), kind=kLoop, calls=%fused_computation.13 | loop fusion | flops 3047424 | bytes 8650752 | tf_op jit(solution)/shard_map/reduce_sum | solution.py:292
  157.6 3.9 %all-to-all-start.2 = ((bf16[8,128,768]{2,1,0:T(8,128)(2,1)}), bf16[8,128,768]{2,1,0:T(8,128)(2,1)S(1)}, u32[]{:S(2)}, u32[]{:S(2)}) async-start(bf16[8,128,768]{2,1,0:T(8,128)(2,1)} %get-tuple-element.9), calls=%async_computation.2 | async-start | bytes 3145728 | tf_op jit(solution)/shard_map/all_to_all | solution.py:297
  161.5 2.8 %collective-permute-start.7 = (f32[128,384]{1,0:T(8,128)S(1)}, f32[128,384]{1,0:T(8,128)S(1)}, u32[]{:S(2)}, u32[]{:S(2)}) collective-permute-start(f32[128,384]{1,0:T(8,128)S(1)} %slice_select_fusion), channel_id=1, source_target_pairs={{0,16},{16,0},{1,17},{17,1},{2,18},{18,2},{3,19},{19,3},{4,20},{20... | collective-permute-start | bytes 589832 | tf_op jit(solution)/shard_map/ppermute | solution.py:295
  164.3 5.1 %collective-permute-done.7 = f32[128,384]{1,0:T(8,128)S(1)} collective-permute-done((f32[128,384]{1,0:T(8,128)S(1)}, f32[128,384]{1,0:T(8,128)S(1)}, u32[]{:S(2)}, u32[]{:S(2)}) %collective-permute-start.7) | collective-permute-done | bytes 196640 | tf_op jit(solution)/shard_map/ppermute | solution.py:295
  169.5 0.8 broadcast_in_dim.24
  170.3 11.8 %all-to-all-done.2.in_ref = bf16[8,128,768]{2,1,0:T(8,128)(2,1)S(1)} async-done(((bf16[8,128,768]{2,1,0:T(8,128)(2,1)}), bf16[8,128,768]{2,1,0:T(8,128)(2,1)S(1)}, u32[]{:S(2)}, u32[]{:S(2)}) %all-to-all-start.2) | async-done | bytes 1572896 | tf_op jit(solution)/shard_map/all_to_all | solution.py:297
  182.1 1.2 copy-done.3
  183.3 2.7 %assemble.1 = bf16[128,6144]{1,0:T(8,128)(2,1)} custom-call(bf16[8,128,768]{2,1,0:T(8,128)(2,1)} %copy-done.3), custom_call_target="tpu_custom_call" | custom-call | tf_op jit(solution)/shard_map/assemble/pallas_call | solution.py:209
  (31 shorter events, 0.2 us)
Async XLA Ops:
  7.2 11.3 %copy-start.7 = (bf16[1,588,128]{2,1,0:T(8,128)(2,1)S(1)}, bf16[1,588,128]{2,1,0:T(8,128)(2,1)}, u32[]{:S(2)}) copy-start(bf16[1,588,128]{2,1,0:T(8,128)(2,1)} %param.9) | copy-start | bytes 451588
  7.2 11.5 %copy-start.8 = (bf16[1,1,588,128]{3,2,1,0:T(8,128)(2,1)S(1)}, bf16[1,1,588,128]{3,2,1,0:T(8,128)(2,1)}, u32[]{:S(2)}) copy-start(bf16[1,1,588,128]{3,2,1,0:T(8,128)(2,1)} %param.10) | copy-start | bytes 451588
  10.2 19.7 %all-to-all-start = ((bf16[16,48,384]{2,1,0:T(8,128)(2,1)}), bf16[16,48,384]{2,1,0:T(8,128)(2,1)S(1)}, u32[]{:S(2)}, u32[]{:S(2)}) async-start(bf16[16,48,384]{2,1,0:T(8,128)(2,1)} %bitcast.3), calls=%async_computation | async-start | bytes 1179648 | tf_op jit(solution)/shard_map/all_to_all | solution.py:245
  18.4 13.7 %copy-start.5 = (bf16[588,384]{1,0:T(8,128)(2,1)S(1)}, bf16[588,384]{1,0:T(8,128)(2,1)}, u32[]{:S(2)}) copy-start(bf16[588,384]{1,0:T(8,128)(2,1)} %param.11) | copy-start | bytes 1354756
  18.4 46.1 %all-gather.8.cloned.1.call-start = ((), (), s32[]{:S(2)}) async-start(), calls=%async_computation.4 | async-start | bytes 1474560 | tf_op jit(solution)/shard_map/all_gather | solution.py:249
  29.9 3.6 %copy-start.4 = (bf16[16,48,384]{2,1,0:T(8,128)(2,1)}, bf16[16,48,384]{2,1,0:T(8,128)(2,1)S(1)}, u32[]{:S(2)}) copy-start(bf16[16,48,384]{2,1,0:T(8,128)(2,1)S(1)} %all-to-all-done.rows_ref) | copy-start | bytes 1769476
  29.9 75.9 %all-gather.10.cloned.1.call-start = ((), (), s32[]{:S(2)}) async-start(), calls=%async_computation.5 | async-start | bytes 2949120 | tf_op jit(solution)/shard_map/all_gather | solution.py:240
  32.1 31.5 %collective-permute-start = (bf16[588,384]{1,0:T(8,128)(2,1)S(1)}, bf16[588,384]{1,0:T(8,128)(2,1)S(1)}, u32[]{:S(2)}, u32[]{:S(2)}) collective-permute-start(bf16[588,384]{1,0:T(8,128)(2,1)S(1)} %copy-done.5), channel_id=1, source_target_pairs={{0,20},{1,21},{2,22},{3,23},{4,16},{5,17},{6,18},{7,19},{16,4},{17... | collective-permute-start | bytes 1354760 | tf_op jit(solution)/shard_map/ppermute | solution.py:46
  43.5 6.6 %collective-permute-start.1 = (bf16[48,1152]{1,0:T(8,128)(2,1)}, bf16[48,1152]{1,0:T(8,128)(2,1)S(1)}, u32[]{:S(2)}, u32[]{:S(2)}) collective-permute-start(bf16[48,1152]{1,0:T(8,128)(2,1)} %join_weights.1), channel_id=1, source_target_pairs={{0,0},{1,8},{2,32},{3,40},{4,64},{5,72},{6,96},{7,104},{16,16},{17... | collective-permute-start | bytes 331784 | tf_op jit(solution)/shard_map/ppermute | solution.py:46
  51.5 35.6 %all-to-all-start.1 = ((bf16[16,48,1152]{2,1,0:T(8,128)(2,1)}), bf16[16,48,1152]{2,1,0:T(8,128)(2,1)S(1)}, u32[]{:S(2)}, u32[]{:S(2)}) async-start(bf16[16,48,1152]{2,1,0:T(8,128)(2,1)} %broadcast_in_dim.21), calls=%async_computation.1 | async-start | bytes 3538944 | tf_op jit(solution)/shard_map/all_to_all | solution.py:253
  63.6 83.6 %all-gather.6.cloned.1.call-start = ((), (), s32[]{:S(2)}) async-start(), calls=%async_computation.3 | async-start | bytes 7077888 | tf_op jit(solution)/shard_map/all_gather | solution.py:279
  67.5 8.4 %copy-start.1 = (f32[8,128,768]{2,1,0:T(8,128)}, f32[8,128,768]{2,1,0:T(8,128)S(1)}, u32[]{:S(2)}) copy-start(f32[8,128,768]{2,1,0:T(8,128)S(1)} %get-tuple-element.24) | copy-start | bytes 9437188
  68.2 2.4 %collective-permute-start.2 = (f32[2,8,128]{2,1,0:T(8,128)S(1)}, f32[2,8,128]{2,1,0:T(8,128)S(1)}, u32[]{:S(2)}, u32[]{:S(2)}) collective-permute-start(f32[2,8,128]{2,1,0:T(8,128)S(1)} %pad_maximum_fusion.2), channel_id=1, source_target_pairs={{0,8},{1,9},{2,10},{3,11},{4,12},{5,13},{6,14},{7,15},{16,24},{17,... | collective-permute-start | bytes 24584 | tf_op jit(solution)/shard_map/ppermute | solution.py:46
  70.6 3.9 %collective-permute-start.3 = (f32[2,8,128]{2,1,0:T(8,128)S(1)}, f32[2,8,128]{2,1,0:T(8,128)S(1)}, u32[]{:S(2)}, u32[]{:S(2)}) collective-permute-start(f32[2,8,128]{2,1,0:T(8,128)S(1)} %pad_maximum_fusion.3), channel_id=1, source_target_pairs={{0,32},{1,33},{2,34},{3,35},{4,36},{5,37},{6,38},{7,39},{16,48},{1... | collective-permute-start | bytes 24584 | tf_op jit(solution)/shard_map/ppermute | solution.py:46
  70.7 4.4 %collective-permute-start.4 = (f32[2,8,128]{2,1,0:T(8,128)S(1)}, f32[2,8,128]{2,1,0:T(8,128)S(1)}, u32[]{:S(2)}, u32[]{:S(2)}) collective-permute-start(f32[2,8,128]{2,1,0:T(8,128)S(1)} %pad_maximum_fusion.3), channel_id=1, source_target_pairs={{0,64},{1,65},{2,66},{3,67},{4,68},{5,69},{6,70},{7,71},{16,80},{1... | collective-permute-start | bytes 24584 | tf_op jit(solution)/shard_map/ppermute | solution.py:46
  71.8 4.1 %collective-permute-start.5 = (f32[2,8,128]{2,1,0:T(8,128)S(1)}, f32[2,8,128]{2,1,0:T(8,128)S(1)}, u32[]{:S(2)}, u32[]{:S(2)}) collective-permute-start(f32[2,8,128]{2,1,0:T(8,128)S(1)} %pad_maximum_fusion.3), channel_id=1, source_target_pairs={{0,96},{1,97},{2,98},{3,99},{4,100},{5,101},{6,102},{7,103},{16,11... | collective-permute-start | bytes 24584 | tf_op jit(solution)/shard_map/ppermute | solution.py:46
  87.1 1.2 copy-start
  105.8 29.5 %collective-permute-start.6 = (bf16[4,384,768]{2,1,0:T(8,128)(2,1)}, bf16[4,384,768]{2,1,0:T(8,128)(2,1)S(1)}, u32[]{:S(2)}, u32[]{:S(2)}) collective-permute-start(bf16[4,384,768]{2,1,0:T(8,128)(2,1)} %bitcast.116), channel_id=1, source_target_pairs={{0,4},{1,5},{2,6},{3,7},{4,0},{5,1},{6,2},{7,3},{16,20},{17,21},{1... | collective-permute-start | bytes 7077896 | tf_op jit(solution)/shard_map/ppermute | solution.py:46
  140.0 15.2 %copy-start.2 = (f32[8,128,768]{2,1,0:T(8,128)S(1)}, f32[8,128,768]{2,1,0:T(8,128)}, u32[]{:S(2)}) copy-start(f32[8,128,768]{2,1,0:T(8,128)} %copy-done.1) | copy-start | bytes 9437188
  157.6 3.9 %copy-start.6 = (f32[128,768]{1,0:T(8,128)S(1)}, f32[128,768]{1,0:T(8,128)}, u32[]{:S(2)}) copy-start(f32[128,768]{1,0:T(8,128)} %get-tuple-element.8) | copy-start | bytes 1179652
  157.6 24.5 %all-to-all-start.2 = ((bf16[8,128,768]{2,1,0:T(8,128)(2,1)}), bf16[8,128,768]{2,1,0:T(8,128)(2,1)S(1)}, u32[]{:S(2)}, u32[]{:S(2)}) async-start(bf16[8,128,768]{2,1,0:T(8,128)(2,1)} %get-tuple-element.9), calls=%async_computation.2 | async-start | bytes 3145728 | tf_op jit(solution)/shard_map/all_to_all | solution.py:297
  161.5 7.9 %collective-permute-start.7 = (f32[128,384]{1,0:T(8,128)S(1)}, f32[128,384]{1,0:T(8,128)S(1)}, u32[]{:S(2)}, u32[]{:S(2)}) collective-permute-start(f32[128,384]{1,0:T(8,128)S(1)} %slice_select_fusion), channel_id=1, source_target_pairs={{0,16},{16,0},{1,17},{17,1},{2,18},{18,2},{3,19},{19,3},{4,20},{20... | collective-permute-start | bytes 589832 | tf_op jit(solution)/shard_map/ppermute | solution.py:295
  182.1 1.2 copy-start.3
Sparse Core Ops, SparseCore 0:
  30.0 24.5 all-gather.7
  56.2 49.5 all-gather.9
  108.1 39.0 all-gather.5

commit v5 on v4

--- a/solution.py
+++ b/solution.py
@@ -44,6 +44,14 @@
 def send(array, target):
     pairs = [(device_id(*s), device_id(*target(*s))) for s in everyone()]
     return lax.ppermute(array, AXES, pairs)
+
+
+def x_partner(k):
+    return lambda xc, yh, m: (xc ^ (2 * k), yh, m)
+
+
+def core_partner(xc, yh, m):
+    return xc ^ 1, yh, m
 
 
 def padded(rows, count):
@@ -237,25 +245,36 @@
             lax.dynamic_slice_in_dim(array, start + yb * 2 * cols, cols, axis=1) for yb in range(2)
         ]
 
-    out_near = lax.all_gather(jnp.concatenate(my_columns(out_weight), axis=1), "z")
-
     position_here = lax.dynamic_slice_in_dim(position_table, lax.axis_index(DP) * cols, cols, axis=1)
     rows = [padded(embed_weight, PIX_ROWS), padded(position_here, PIECES * ROWS - PIX_ROWS)]
     rows = jnp.concatenate(rows, axis=0).reshape(PIECES, ROWS, cols)
     rows = lax.all_to_all(rows, AXES, 0, 0, axis_index_groups=NEAR, tiled=True)
     noisy = (clean_image[0].astype(f32) + 0.5 * noise_draw[0, 0].astype(f32)).astype(bf16)
     lhs_own = with_layout_constraint(padded(noisy, LHS_ROWS).T, Layout((0, 1)))
-    lhs_own, rows, own_weight = lax.optimization_barrier((lhs_own, rows, embed_weight))
-    lhs = lax.all_gather(lhs_own, GROUP)
+    lhs_own = [lhs_own] + [send(lhs_own, x_partner(k)) for k in (1, 2, 3)]
+
+    out_near = jnp.concatenate(my_columns(out_weight), axis=1)
+    out_near = [out_near] + [
+        send(out_near, lambda xc, yh, m, k=k: (xc, yh, m ^ k)) for k in (1, 2, 3)
+    ]
+
     piece = join_weights(rows, norm_gain[None], jnp.transpose(qkv_weight, (1, 0, 2)))
+    lhs_own, own_weight, piece = lax.optimization_barrier((lhs_own, embed_weight, piece))
     piece = send(piece, lambda xc, yh, m: (m, yh, xc))
+    other_weight = send(own_weight, lambda xc, yh, m: (xc, 1 - yh, m ^ 4))
+    lhs_own = jnp.stack(lhs_own)
     joined = jnp.broadcast_to(piece[None], (PIECES, *piece.shape))
     joined = lax.all_to_all(joined, AXES, 0, 0, axis_index_groups=HOLDERS, tiled=True)
     joined = joined.reshape(PIECES * ROWS, -1)
 
-    other_weight = send(own_weight, lambda xc, yh, m: (xc, 1 - yh, m ^ 4))
-    first = jnp.where(yhi == 0, embed_weight, other_weight)
-    second = jnp.where(yhi == 0, other_weight, embed_weight)
+    lhs_mate = send(lhs_own, core_partner)
+    lhs = jnp.zeros((8, patches, LHS_ROWS), bf16)
+    for k in range(4):
+        lhs = lax.dynamic_update_slice(lhs, lhs_own[k : k + 1], (2 * (xi ^ k) + ci, 0, 0))
+        lhs = lax.dynamic_update_slice(lhs, lhs_mate[k : k + 1], (2 * (xi ^ k) + 1 - ci, 0, 0))
+
+    first = jnp.where(yhi == 0, own_weight, other_weight)
+    second = jnp.where(yhi == 0, other_weight, own_weight)
     weight_two = jnp.concatenate([first, second], axis=1)
     weight_two = padded(weight_two, LHS_ROWS)
     position_two = jnp.concatenate(my_columns(position_table), axis=1).astype(f32)
@@ -272,22 +291,41 @@
         average = sum(each[0] for each in stats) * share
         spread = sum(each[1] + jnp.square(each[0] - average) for each in stats) * share
         stat = jnp.stack([average, spread])
-    scale = lax.rsqrt(spread + epsilon)
+    scale = lax.rsqrt(stat[1] + epsilon)
+
+    out_near, joined = lax.optimization_barrier((jnp.stack(out_near), joined))
+    out_far = send(out_near, lambda xc, yh, m: (xc, yh ^ (xc & 1), m ^ 4))
 
     head_out = attend(lhs, joined, scale, query_gain, key_gain)
     head_out = head_out.reshape(8 * patches, -1)
-    head_all = lax.all_gather(head_out, GROUP)
-
-    out_near, _ = lax.optimization_barrier((out_near, head_out))
-    out_far = send(out_near, lambda xc, yh, m: (xc, yh ^ (xc & 1), m ^ 4))
-
-    low = lax.axis_index("yl") == 0
-    out_all = jnp.concatenate(
-        [jnp.where(low, out_near, out_far), jnp.where(low, out_far, out_near)], axis=0
-    )
-    out_all = lax.optimization_barrier(out_all)
-    attention = jnp.einsum("gtc,gcd->td", head_all, out_all, preferred_element_type=f32)
-    output = embedded + attention.reshape(8, patches, 2 * cols)
+
+    tokens = head_out.shape[0]
+    heads = [None] * 8
+    heads[0] = head_out
+    heads[1] = send(head_out, core_partner)
+    heads[2] = send(head_out, x_partner(1))
+    heads[6] = send(head_out, x_partner(3))
+    relayed = [
+        send(heads[6][: tokens // 2], x_partner(1)),
+        send(heads[2][tokens // 2 :], x_partner(3)),
+    ]
+    heads[3] = send(heads[2], core_partner)
+    heads[7] = send(heads[6], core_partner)
+    mates = [send(half, core_partner) for half in relayed]
+    heads[4] = lax.optimization_barrier(jnp.concatenate(relayed, axis=0))
+    heads[5] = lax.optimization_barrier(jnp.concatenate(mates, axis=0))
+
+    order = lax.axis_index(MP) ^ (2 * xi + ci)
+    out_all = jnp.zeros((8, *out_near.shape[1:]), bf16)
+    for k in range(4):
+        out_all = lax.dynamic_update_slice(out_all, out_near[k : k + 1], (order ^ k, 0, 0))
+        out_all = lax.dynamic_update_slice(out_all, out_far[k : k + 1], (order ^ (4 + k), 0, 0))
+    output = embedded.reshape(tokens, 2 * cols)
+    for k in (0, 1, 2, 6, 3, 7):
+        output = lax.optimization_barrier(output + dot(heads[k], out_all[k], ((1,), (0,))))
+    for k in (4, 5):
+        output = lax.optimization_barrier(output + dot(heads[k], out_all[k], ((1,), (0,))))
+    output = output.reshape(8, patches, 2 * cols)
 
     summed = jnp.sum(output, axis=0) * (1.0 / 16)
     kept = jnp.where(yhi == 0, summed[:, :cols], summed[:, cols:])

time: 193 us -> 192 us (level)
  between operations: 14 us -> 1.35 us
  local copies, waits for them, and re-layouts: 7.98 us -> 19.8 us
  waiting for transfers between devices: 85.8 us -> 81.1 us
  other arithmetic: 12.1 us -> 15.7 us
    ppermute x7 -> x23, waiting for transfers between devices: 32.2 us -> 55.4 us  [send(): return lax.ppermute(array, AXES, pairs)]
    all_gather x3 -> x0, waiting for transfers between devices: 15.9 us -> none  [the longest x1 8.68 us: block(): lax.all_gather(jnp.concatenate(my_columns(out_weight), axis=1), 'z')]
    ppermute x7 -> x23, starting transfers between devices: 13 us -> 25.4 us  [send(): return lax.ppermute(array, AXES, pairs)]
    dynamic_update_slice x0 -> x16, local copies, waits for them, and re-layouts: none -> 10.5 us  [the longest x4 4.61 us: block(): lax.dynamic_update_slice(out_all, out_far[k:k + 1], (order ^ 4 + k, 0, 0))]
    all_to_all x1, waiting for transfers between devices: 10.5 us -> 1.52 us  [block(): lax.all_to_all(joined, AXES, 0, 0, axis_index_groups=HOLDERS, tiled=True)]
    all_to_all x1, starting transfers between devices: 12.1 us -> 3.71 us  [block(): lax.all_to_all(joined, AXES, 0, 0, axis_index_groups=HOLDERS, tiled=True)]
    all_to_all x1, waiting for transfers between devices: 10.3 us -> 5.06 us  [block(): rows = lax.all_to_all(rows, AXES, 0, 0, axis_index_groups=NEAR, tiled=True)]
    another operation x0 -> x3, other arithmetic: none -> 5.19 us  [the longest x2 4.22 us: block(): out_near, joined = lax.optimization_barrier((jnp.stack(out_near), joined))]
  transfers between devices with their start and end apart: 14 -> 27, of which waited for: 11 -> 11; matrix products, arithmetic and copies ran while one was open for 8% -> 17% of each run, Pallas kernels for 10% -> 10%
where the time goes in v5:
time: 192 us; the launch traced here: 191 us
  waiting for transfers between devices  81.1 us (42%)
  starting transfers between devices  42 us (22%)
  Pallas kernels  21.4 us (11%)
  local copies, waits for them, and re-layouts  19.8 us (10%)
  other arithmetic  15.7 us (8%)
  matrix products  9.35 us (5%)
    ppermute x23, waiting for transfers between devices, send(): return lax.ppermute(array, AXES, pairs)  55.4 us
    ppermute x23, starting transfers between devices, send(): return lax.ppermute(array, AXES, pairs)  25.4 us
    all_to_all x1, waiting for transfers between devices, block(): moved = lax.all_to_all(output.astype(bf16), GROUP, 0, 0, tiled=True)  11.6 us
    pallas_call x1, Pallas kernels, join_weights(): pl.pallas_call(join_kernel, out_shape=jax.ShapeDtypeStruct((ROWS, 3 * gro...  9.94 us
    pallas_call x1, Pallas kernels, attend(): pl.pallas_call(attention_kernel, out_shape=jax.ShapeDtypeStruct((copies,...  8.8 us
    all_to_all x1, starting transfers between devices, block(): rows = lax.all_to_all(rows, AXES, 0, 0, axis_index_groups=NEAR, tiled=True)  8.26 us
    dot_general x8, matrix products, dot(): lax.dot_general(left, right, (dims, ((), ())), preferred_element_type=f32)  7.8 us
    ppermute x1, waiting for transfers between devices, block(): smoothed = (kept + lax.ppermute(sent, 'yh', [(0, 1), (1, 0)]))[:, None, :]  7.58 us
  transfers between devices with their start and end apart: 27, of which 11 were waited for; matrix products, arithmetic and copies ran while one was open for 17% of the time, Pallas kernels for 10%

profile of v5, /device:TPU:1, one launch (start us, length us, event | category | flops | bytes accessed | tf_op | source)
XLA Modules:
  0.0 190.7 jit_solution(8637574795542675884)
XLA Ops:
  0.7 1.1 constant_dynamic-slice_fusion.3
  1.7 1.9 fusion.11
  3.6 8.3 %all-to-all-start = ((bf16[16,48,384]{2,1,0:T(8,128)(2,1)}), bf16[16,48,384]{2,1,0:T(8,128)(2,1)S(1)}, u32[]{:S(2)}, u32[]{:S(2)}) async-start(bf16[16,48,384]{2,1,0:T(8,128)(2,1)} %bitcast.3), calls=%async_computation | async-start | bytes 1179648 | tf_op jit(solution)/shard_map/all_to_all | solution.py:251
  11.9 1.1 copy.12
  13.2 1.4 collective-permute-start
  14.6 2.4 %collective-permute-start.1 = (bf16[128,640]{1,0:T(8,128)(2,1)S(1)}, bf16[128,640]{1,0:T(8,128)(2,1)S(1)}, u32[]{:S(2)}, u32[]{:S(2)}) collective-permute-start(bf16[128,640]{1,0:T(8,128)(2,1)S(1)} %pad_bitcast_fusion), channel_id=1, source_target_pairs={{0,64},{1,65},{2,66},{3,67},{4,68},{5,69},{6,70},{7,71},{16,80},{1... | collective-permute-start | bytes 491528 | tf_op jit(solution)/shard_map/ppermute | solution.py:46
  17.1 1.1 constant_dynamic-slice_fusion.1
  18.2 5.1 %all-to-all-done.rows_ref = bf16[16,48,384]{2,1,0:T(8,128)(2,1)S(1)} async-done(((bf16[16,48,384]{2,1,0:T(8,128)(2,1)}), bf16[16,48,384]{2,1,0:T(8,128)(2,1)S(1)}, u32[]{:S(2)}, u32[]{:S(2)}) %all-to-all-start) | async-done | bytes 589856 | tf_op jit(solution)/shard_map/all_to_all | solution.py:251
  24.1 9.9 %join_weights.1 = bf16[48,1152]{1,0:T(8,128)(2,1)} custom-call(bf16[16,48,384]{2,1,0:T(8,128)(2,1)} %copy-done.7, f32[1,6144]{1,0:T(1,128)} %bitcast.168, bf16[3,6144,384]{2,1,0:T(8,128)(2,1)} %bitcast.158), custom_call_target="tpu_custom_call" | custom-call | flops 679477248 | bytes 14155776 | tf_op jit(solution)/shard_map/join_weights/pallas_call | solution.py:99
  35.1 1.9 collective-permute-start.3
  37.0 1.1 fusion.40
  38.1 3.8 %collective-permute-start.7 = (bf16[384,768]{1,0:T(8,128)(2,1)}, bf16[384,768]{1,0:T(8,128)(2,1)}, u32[]{:S(2)}, u32[]{:S(2)}) collective-permute-start(bf16[384,768]{1,0:T(8,128)(2,1)} %get-tuple-element.26), channel_id=1, source_target_pairs={{0,3},{1,2},{2,1},{3,0},{4,7},{5,6},{6,5},{7,4},{16,19},{17,18},{1... | collective-permute-start | bytes 1769480 | tf_op jit(solution)/shard_map/ppermute | solution.py:46
  42.7 3.4 %collective-permute-start.8 = (bf16[48,1152]{1,0:T(8,128)(2,1)S(1)}, bf16[48,1152]{1,0:T(8,128)(2,1)S(1)}, u32[]{:S(2)}, u32[]{:S(2)}) collective-permute-start(bf16[48,1152]{1,0:T(8,128)(2,1)S(1)} %copy-done.17), channel_id=1, source_target_pairs={{0,0},{1,8},{2,32},{3,40},{4,64},{5,72},{6,96},{7,104},{16,16},{17... | collective-permute-start | bytes 331784 | tf_op jit(solution)/shard_map/ppermute | solution.py:46
  46.2 14.0 %collective-permute-done.8 = bf16[48,1152]{1,0:T(8,128)(2,1)S(1)} collective-permute-done((bf16[48,1152]{1,0:T(8,128)(2,1)S(1)}, bf16[48,1152]{1,0:T(8,128)(2,1)S(1)}, u32[]{:S(2)}, u32[]{:S(2)}) %collective-permute-start.8) | collective-permute-done | bytes 110624 | tf_op jit(solution)/shard_map/ppermute | solution.py:46
  60.2 1.3 broadcast_in_dim.28
  61.6 3.7 %all-to-all-start.1 = ((bf16[16,48,1152]{2,1,0:T(8,128)(2,1)}), bf16[16,48,1152]{2,1,0:T(8,128)(2,1)S(1)}, u32[]{:S(2)}, u32[]{:S(2)}) async-start(bf16[16,48,1152]{2,1,0:T(8,128)(2,1)} %broadcast_in_dim.28), calls=%async_computation.1 | async-start | bytes 3538944 | tf_op jit(solution)/shard_map/all_to_all | solution.py:267
  65.4 1.2 broadcast_select_fusion.1
  72.3 1.6 fusion.41
  73.9 1.6 copy-done.1
  76.0 1.6 collective-permute-start.9
  77.6 12.4 %collective-permute-done.5 = bf16[384,768]{1,0:T(8,128)(2,1)} collective-permute-done((bf16[384,768]{1,0:T(8,128)(2,1)}, bf16[384,768]{1,0:T(8,128)(2,1)}, u32[]{:S(2)}, u32[]{:S(2)}) %collective-permute-start.5) | collective-permute-done | bytes 589856 | tf_op jit(solution)/shard_map/ppermute | solution.py:46
  90.0 3.1 %pad_maximum_fusion = bf16[4,384,768]{2,1,0:T(8,128)(2,1)} fusion(bf16[1,384,768]{2,1,0:T(8,128)(2,1)} %bitcast.15, bf16[1,384,768]{2,1,0:T(8,128)(2,1)} %bitcast.14, bf16[1,384,768]{2,1,0:T(8,128)(2,1)} %bitcast.13, bf16[1,384,768]{2,1,0:T(8,128)(2,1)S(1)} %copy-done.6), kind=kLoop, calls=%fused_computation.2 | loop fusion | flops 3538944 | bytes 4718592 | tf_op jit(solution)/shard_map/stack | solution.py:296
  93.1 1.5 all-to-all-done.1
  94.7 3.3 %collective-permute-start.11 = (f32[2,8,128]{2,1,0:T(8,128)S(1)}, f32[2,8,128]{2,1,0:T(8,128)S(1)}, u32[]{:S(2)}, u32[]{:S(2)}) collective-permute-start(f32[2,8,128]{2,1,0:T(8,128)S(1)} %pad_maximum_fusion.6), channel_id=1, source_target_pairs={{0,64},{1,65},{2,66},{3,67},{4,68},{5,69},{6,70},{7,71},{16,80},{1... | collective-permute-start | bytes 24584 | tf_op jit(solution)/shard_map/ppermute | solution.py:46
  99.1 1.9 collective-permute-done.10
  101.6 8.8 %attend.1 = bf16[8,128,384]{2,1,0:T(8,128)(2,1)} custom-call(bf16[8,128,640]{2,1,0:T(8,128)(2,1)} %copy-done.4, bf16[768,1152]{1,0:T(8,128)(2,1)} %bitcast.151, bf16[768,1152]{1,0:T(8,128)(2,1)} %bitcast.152, bf16[768,1152]{1,0:T(8,128)(2,1)} %bitcast.153, bf16[768,1152]{1,0:T(8,128)(2,1)} %bitcast.154, bf16[768,1152]{1,0:T(8,128)(2,1)} %bitcast.155, ...), custom_call_target="tpu_custom_call" | custom-call | flops 3019898880 | bytes 7864320 | tf_op jit(solution)/shard_map/attend/pallas_call | solution.py:169
  111.1 1.4 collective-permute-start.16
  112.5 17.1 %collective-permute-done.15 = bf16[1024,384]{1,0:T(8,128)(2,1)S(1)} collective-permute-done((bf16[1024,384]{1,0:T(8,128)(2,1)}, bf16[1024,384]{1,0:T(8,128)(2,1)S(1)}, u32[]{:S(2)}, u32[]{:S(2)}) %collective-permute-start.15) | collective-permute-done | bytes 786464 | tf_op jit(solution)/shard_map/ppermute | solution.py:46
  129.7 1.9 %collective-permute-start.20 = (bf16[512,384]{1,0:T(8,128)(2,1)S(1)}, bf16[512,384]{1,0:T(8,128)(2,1)S(1)}, u32[]{:S(2)}, u32[]{:S(2)}) collective-permute-start(bf16[512,384]{1,0:T(8,128)(2,1)S(1)} %slice.157), channel_id=1, source_target_pairs={{0,96},{1,97},{2,98},{3,99},{4,100},{5,101},{6,102},{7,103},{16,11... | collective-permute-start | bytes 1179656 | tf_op jit(solution)/shard_map/ppermute | solution.py:46
  131.7 8.9 %collective-permute-done.20 = bf16[512,384]{1,0:T(8,128)(2,1)S(1)} collective-permute-done((bf16[512,384]{1,0:T(8,128)(2,1)S(1)}, bf16[512,384]{1,0:T(8,128)(2,1)S(1)}, u32[]{:S(2)}, u32[]{:S(2)}) %collective-permute-start.20) | collective-permute-done | bytes 393248 | tf_op jit(solution)/shard_map/ppermute | solution.py:46
  140.7 1.8 collective-permute-start.22
  144.5 1.1 pad_maximum_fusion.1
  146.2 1.2 pad_maximum_fusion.2
  147.4 1.1 slice_dynamic-update-slice_fusion.3
  148.6 1.3 slice_dynamic-update-slice_fusion.2
  149.9 1.1 slice_dynamic-update-slice_fusion.1
  151.1 1.1 slice_dynamic-update-slice_fusion
  152.2 1.0 bitcast_add_fusion
  153.2 1.0 convolution_add_fusion.2
  154.2 1.0 fusion.15
  155.6 1.0 fusion.14
  157.0 1.0 convolution_add_fusion.1
  160.7 1.0 convolution_add_fusion
  161.7 1.3 bitcast_convert_fusion
  163.0 4.2 %all-to-all-start.2 = ((bf16[8,128,768]{2,1,0:T(8,128)(2,1)}), bf16[8,128,768]{2,1,0:T(8,128)(2,1)}, u32[]{:S(2)}, u32[]{:S(2)}) async-start(bf16[8,128,768]{2,1,0:T(8,128)(2,1)} %bitcast_convert_fusion), calls=%async_computation.2 | async-start | bytes 3145728 | tf_op jit(solution)/shard_map/all_to_all | solution.py:335
  167.9 7.6 %collective-permute-done.23 = f32[128,384]{1,0:T(8,128)S(1)} collective-permute-done((f32[128,384]{1,0:T(8,128)S(1)}, f32[128,384]{1,0:T(8,128)S(1)}, u32[]{:S(2)}, u32[]{:S(2)}) %collective-permute-start.23) | collective-permute-done | bytes 196640 | tf_op jit(solution)/shard_map/ppermute | solution.py:333
  176.3 11.6 %all-to-all-done.2.in_ref = bf16[8,128,768]{2,1,0:T(8,128)(2,1)} async-done(((bf16[8,128,768]{2,1,0:T(8,128)(2,1)}), bf16[8,128,768]{2,1,0:T(8,128)(2,1)}, u32[]{:S(2)}, u32[]{:S(2)}) %all-to-all-start.2) | async-done | bytes 1572896 | tf_op jit(solution)/shard_map/all_to_all | solution.py:335
  187.9 2.7 %assemble.1 = bf16[128,6144]{1,0:T(8,128)(2,1)} custom-call(bf16[8,128,768]{2,1,0:T(8,128)(2,1)} %all-to-all-done.2.in_ref), custom_call_target="tpu_custom_call" | custom-call | tf_op jit(solution)/shard_map/assemble/pallas_call | solution.py:217
  (106 shorter events, 19.8 us)
Async XLA Ops:
  0.6 12.3 %copy-start.16 = (bf16[1,588,128]{2,1,0:T(8,128)(2,1)S(1)}, bf16[1,588,128]{2,1,0:T(8,128)(2,1)}, u32[]{:S(2)}) copy-start(bf16[1,588,128]{2,1,0:T(8,128)(2,1)} %param.9) | copy-start | bytes 451588
  3.6 19.7 %all-to-all-start = ((bf16[16,48,384]{2,1,0:T(8,128)(2,1)}), bf16[16,48,384]{2,1,0:T(8,128)(2,1)S(1)}, u32[]{:S(2)}, u32[]{:S(2)}) async-start(bf16[16,48,384]{2,1,0:T(8,128)(2,1)} %bitcast.3), calls=%async_computation | async-start | bytes 1179648 | tf_op jit(solution)/shard_map/all_to_all | solution.py:251
  13.2 20.9 %collective-permute-start = (bf16[128,640]{1,0:T(8,128)(2,1)S(1)}, bf16[128,640]{1,0:T(8,128)(2,1)S(1)}, u32[]{:S(2)}, u32[]{:S(2)}) collective-permute-start(bf16[128,640]{1,0:T(8,128)(2,1)S(1)} %pad_bitcast_fusion), channel_id=1, source_target_pairs={{0,32},{1,33},{2,34},{3,35},{4,36},{5,37},{6,38},{7,39},{16,48},{1... | collective-permute-start | bytes 491528 | tf_op jit(solution)/shard_map/ppermute | solution.py:46
  14.6 19.5 %collective-permute-start.1 = (bf16[128,640]{1,0:T(8,128)(2,1)S(1)}, bf16[128,640]{1,0:T(8,128)(2,1)S(1)}, u32[]{:S(2)}, u32[]{:S(2)}) collective-permute-start(bf16[128,640]{1,0:T(8,128)(2,1)S(1)} %pad_bitcast_fusion), channel_id=1, source_target_pairs={{0,64},{1,65},{2,66},{3,67},{4,68},{5,69},{6,70},{7,71},{16,80},{1... | collective-permute-start | bytes 491528 | tf_op jit(solution)/shard_map/ppermute | solution.py:46
  17.0 17.1 %collective-permute-start.2 = (bf16[128,640]{1,0:T(8,128)(2,1)S(1)}, bf16[128,640]{1,0:T(8,128)(2,1)S(1)}, u32[]{:S(2)}, u32[]{:S(2)}) collective-permute-start(bf16[128,640]{1,0:T(8,128)(2,1)S(1)} %pad_bitcast_fusion), channel_id=1, source_target_pairs={{0,96},{1,97},{2,98},{3,99},{4,100},{5,101},{6,102},{7,103},{16,11... | collective-permute-start | bytes 491528 | tf_op jit(solution)/shard_map/ppermute | solution.py:46
  23.3 0.8 copy-start.7
  24.1 12.9 %copy-start.8 = (bf16[588,384]{1,0:T(8,128)(2,1)S(1)}, bf16[588,384]{1,0:T(8,128)(2,1)}, u32[]{:S(2)}) copy-start(bf16[588,384]{1,0:T(8,128)(2,1)} %param.11) | copy-start | bytes 1354756
  34.1 8.6 %copy-start.17 = (bf16[48,1152]{1,0:T(8,128)(2,1)S(1)}, bf16[48,1152]{1,0:T(8,128)(2,1)}, u32[]{:S(2)}) copy-start(bf16[48,1152]{1,0:T(8,128)(2,1)} %join_weights.1) | copy-start | bytes 331780
  34.1 8.6 %copy-start.14 = (bf16[128,640]{1,0:T(8,128)(2,1)}, bf16[128,640]{1,0:T(8,128)(2,1)S(1)}, u32[]{:S(2)}) copy-start(bf16[128,640]{1,0:T(8,128)(2,1)S(1)} %collective-permute-done) | copy-start | bytes 491524
  34.1 27.5 %copy-start.13 = (bf16[128,640]{1,0:T(8,128)(2,1)}, bf16[128,640]{1,0:T(8,128)(2,1)S(1)}, u32[]{:S(2)}) copy-start(bf16[128,640]{1,0:T(8,128)(2,1)S(1)} %collective-permute-done.1) | copy-start | bytes 491524
  34.1 27.5 %copy-start.11 = (bf16[128,640]{1,0:T(8,128)(2,1)}, bf16[128,640]{1,0:T(8,128)(2,1)S(1)}, u32[]{:S(2)}) copy-start(bf16[128,640]{1,0:T(8,128)(2,1)S(1)} %collective-permute-done.2) | copy-start | bytes 491524
  35.1 31.4 %collective-permute-start.3 = (bf16[4,128,640]{2,1,0:T(8,128)(2,1)}, bf16[4,128,640]{2,1,0:T(8,128)(2,1)}, u32[]{:S(2)}, u32[]{:S(2)}) collective-permute-start(bf16[4,128,640]{2,1,0:T(8,128)(2,1)} %pad_maximum_fusion.3), channel_id=1, source_target_pairs={{0,8},{1,9},{2,10},{3,11},{4,12},{5,13},{6,14},{7,15},{16,24},{17,... | collective-permute-start | bytes 1966088 | tf_op jit(solution)/shard_map/ppermute | solution.py:46
  37.0 28.4 %collective-permute-start.4 = (bf16[588,384]{1,0:T(8,128)(2,1)S(1)}, bf16[588,384]{1,0:T(8,128)(2,1)}, u32[]{:S(2)}, u32[]{:S(2)}) collective-permute-start(bf16[588,384]{1,0:T(8,128)(2,1)S(1)} %copy-done.8), channel_id=1, source_target_pairs={{0,20},{1,21},{2,22},{3,23},{4,16},{5,17},{6,18},{7,19},{16,4},{17... | collective-permute-start | bytes 1354760 | tf_op jit(solution)/shard_map/ppermute | solution.py:46
  38.1 39.5 %collective-permute-start.7 = (bf16[384,768]{1,0:T(8,128)(2,1)}, bf16[384,768]{1,0:T(8,128)(2,1)}, u32[]{:S(2)}, u32[]{:S(2)}) collective-permute-start(bf16[384,768]{1,0:T(8,128)(2,1)} %get-tuple-element.26), channel_id=1, source_target_pairs={{0,3},{1,2},{2,1},{3,0},{4,7},{5,6},{6,5},{7,4},{16,19},{17,18},{1... | collective-permute-start | bytes 1769480 | tf_op jit(solution)/shard_map/ppermute | solution.py:46
  41.9 35.7 %collective-permute-start.6 = (bf16[384,768]{1,0:T(8,128)(2,1)}, bf16[384,768]{1,0:T(8,128)(2,1)}, u32[]{:S(2)}, u32[]{:S(2)}) collective-permute-start(bf16[384,768]{1,0:T(8,128)(2,1)} %get-tuple-element.26), channel_id=1, source_target_pairs={{0,2},{1,3},{2,0},{3,1},{4,6},{5,7},{6,4},{7,5},{16,18},{17,19},{1... | collective-permute-start | bytes 1769480 | tf_op jit(solution)/shard_map/ppermute | solution.py:46
  42.7 17.5 %collective-permute-start.8 = (bf16[48,1152]{1,0:T(8,128)(2,1)S(1)}, bf16[48,1152]{1,0:T(8,128)(2,1)S(1)}, u32[]{:S(2)}, u32[]{:S(2)}) collective-permute-start(bf16[48,1152]{1,0:T(8,128)(2,1)S(1)} %copy-done.17), channel_id=1, source_target_pairs={{0,0},{1,8},{2,32},{3,40},{4,64},{5,72},{6,96},{7,104},{16,16},{17... | collective-permute-start | bytes 331784 | tf_op jit(solution)/shard_map/ppermute | solution.py:46
  60.2 29.7 %collective-permute-start.5 = (bf16[384,768]{1,0:T(8,128)(2,1)}, bf16[384,768]{1,0:T(8,128)(2,1)}, u32[]{:S(2)}, u32[]{:S(2)}) collective-permute-start(bf16[384,768]{1,0:T(8,128)(2,1)} %get-tuple-element.26), channel_id=1, source_target_pairs={{0,1},{1,0},{2,3},{3,2},{4,5},{5,4},{6,7},{7,6},{16,17},{17,16},{1... | collective-permute-start | bytes 1769480 | tf_op jit(solution)/shard_map/ppermute | solution.py:46
  61.6 33.0 %all-to-all-start.1 = ((bf16[16,48,1152]{2,1,0:T(8,128)(2,1)}), bf16[16,48,1152]{2,1,0:T(8,128)(2,1)S(1)}, u32[]{:S(2)}, u32[]{:S(2)}) async-start(bf16[16,48,1152]{2,1,0:T(8,128)(2,1)} %broadcast_in_dim.28), calls=%async_computation.1 | async-start | bytes 3538944 | tf_op jit(solution)/shard_map/all_to_all | solution.py:267
  65.3 5.9 %copy-start.12 = (bf16[128,640]{1,0:T(8,128)(2,1)S(1)}, bf16[128,640]{1,0:T(8,128)(2,1)}, u32[]{:S(2)}) copy-start(bf16[128,640]{1,0:T(8,128)(2,1)} %copy-done.11) | copy-start | bytes 491524
  65.3 6.9 %copy-start.15 = (f32[128,768]{1,0:T(8,128)S(1)}, f32[128,768]{1,0:T(8,128)}, u32[]{:S(2)}) copy-start(f32[128,768]{1,0:T(8,128)} %maximum_convert_fusion) | copy-start | bytes 1179652
  72.2 1.6 copy-start.4
  73.8 1.6 copy-start.1
  73.8 16.1 %copy-start.6 = (bf16[1,384,768]{2,1,0:T(8,128)(2,1)S(1)}, bf16[1,384,768]{2,1,0:T(8,128)(2,1)}, u32[]{:S(2)}) copy-start(bf16[1,384,768]{2,1,0:T(8,128)(2,1)} %get-tuple-element.25) | copy-start | bytes 1769476
  76.0 18.6 %collective-permute-start.9 = (f32[2,8,128]{2,1,0:T(8,128)S(1)}, f32[2,8,128]{2,1,0:T(8,128)S(1)}, u32[]{:S(2)}, u32[]{:S(2)}) collective-permute-start(f32[2,8,128]{2,1,0:T(8,128)S(1)} %pad_maximum_fusion.5), channel_id=1, source_target_pairs={{0,8},{1,9},{2,10},{3,11},{4,12},{5,13},{6,14},{7,15},{16,24},{17,... | collective-permute-start | bytes 24584 | tf_op jit(solution)/shard_map/ppermute | solution.py:46
  94.6 7.0 %copy-start = (bf16[16,48,1152]{2,1,0:T(8,128)(2,1)}, bf16[16,48,1152]{2,1,0:T(8,128)(2,1)S(1)}, u32[]{:S(2)}) copy-start(bf16[16,48,1152]{2,1,0:T(8,128)(2,1)S(1)} %all-to-all-done.1) | copy-start | bytes 5308420
  94.6 52.8 %collective-permute-start.13 = (bf16[4,384,768]{2,1,0:T(8,128)(2,1)}, bf16[4,384,768]{2,1,0:T(8,128)(2,1)}, u32[]{:S(2)}, u32[]{:S(2)}) collective-permute-start(bf16[4,384,768]{2,1,0:T(8,128)(2,1)} %pad_maximum_fusion), channel_id=1, source_target_pairs={{0,4},{1,5},{2,6},{3,7},{4,0},{5,1},{6,2},{7,3},{16,20},{17,21},{1... | collective-permute-start | bytes 7077896 | tf_op jit(solution)/shard_map/ppermute | solution.py:46
  94.6 3.8 %collective-permute-start.12 = (f32[2,8,128]{2,1,0:T(8,128)S(1)}, f32[2,8,128]{2,1,0:T(8,128)S(1)}, u32[]{:S(2)}, u32[]{:S(2)}) collective-permute-start(f32[2,8,128]{2,1,0:T(8,128)S(1)} %pad_maximum_fusion.6), channel_id=1, source_target_pairs={{0,96},{1,97},{2,98},{3,99},{4,100},{5,101},{6,102},{7,103},{16,11... | collective-permute-start | bytes 24584 | tf_op jit(solution)/shard_map/ppermute | solution.py:46
  94.7 4.3 %collective-permute-start.11 = (f32[2,8,128]{2,1,0:T(8,128)S(1)}, f32[2,8,128]{2,1,0:T(8,128)S(1)}, u32[]{:S(2)}, u32[]{:S(2)}) collective-permute-start(f32[2,8,128]{2,1,0:T(8,128)S(1)} %pad_maximum_fusion.6), channel_id=1, source_target_pairs={{0,64},{1,65},{2,66},{3,67},{4,68},{5,69},{6,70},{7,71},{16,80},{1... | collective-permute-start | bytes 24584 | tf_op jit(solution)/shard_map/ppermute | solution.py:46
  98.0 2.9 %collective-permute-start.10 = (f32[2,8,128]{2,1,0:T(8,128)S(1)}, f32[2,8,128]{2,1,0:T(8,128)S(1)}, u32[]{:S(2)}, u32[]{:S(2)}) collective-permute-start(f32[2,8,128]{2,1,0:T(8,128)S(1)} %pad_maximum_fusion.6), channel_id=1, source_target_pairs={{0,32},{1,33},{2,34},{3,35},{4,36},{5,37},{6,38},{7,39},{16,48},{1... | collective-permute-start | bytes 24584 | tf_op jit(solution)/shard_map/ppermute | solution.py:46
  110.4 33.3 %copy-start.3 = (bf16[4,384,768]{2,1,0:T(8,128)(2,1)S(1)}, bf16[4,384,768]{2,1,0:T(8,128)(2,1)}, u32[]{:S(2)}) copy-start(bf16[4,384,768]{2,1,0:T(8,128)(2,1)} %pad_maximum_fusion) | copy-start | bytes 7077892
  110.4 19.3 %collective-permute-start.15 = (bf16[1024,384]{1,0:T(8,128)(2,1)}, bf16[1024,384]{1,0:T(8,128)(2,1)S(1)}, u32[]{:S(2)}, u32[]{:S(2)}) collective-permute-start(bf16[1024,384]{1,0:T(8,128)(2,1)} %bitcast.159), channel_id=1, source_target_pairs={{0,32},{1,33},{2,34},{3,35},{4,36},{5,37},{6,38},{7,39},{16,48},{1... | collective-permute-start | bytes 2359304 | tf_op jit(solution)/shard_map/ppermute | solution.py:46
  111.1 20.5 %collective-permute-start.16 = (bf16[1024,384]{1,0:T(8,128)(2,1)}, bf16[1024,384]{1,0:T(8,128)(2,1)S(1)}, u32[]{:S(2)}, u32[]{:S(2)}) collective-permute-start(bf16[1024,384]{1,0:T(8,128)(2,1)} %bitcast.160), channel_id=1, source_target_pairs={{0,96},{1,97},{2,98},{3,99},{4,100},{5,101},{6,102},{7,103},{16,11... | collective-permute-start | bytes 2359304 | tf_op jit(solution)/shard_map/ppermute | solution.py:46
  129.6 2.0 %copy-start.9 = (bf16[1024,384]{1,0:T(8,128)(2,1)}, bf16[1024,384]{1,0:T(8,128)(2,1)S(1)}, u32[]{:S(2)}) copy-start(bf16[1024,384]{1,0:T(8,128)(2,1)S(1)} %collective-permute-done.15) | copy-start | bytes 2359300
  129.7 11.0 %collective-permute-start.20 = (bf16[512,384]{1,0:T(8,128)(2,1)S(1)}, bf16[512,384]{1,0:T(8,128)(2,1)S(1)}, u32[]{:S(2)}, u32[]{:S(2)}) collective-permute-start(bf16[512,384]{1,0:T(8,128)(2,1)S(1)} %slice.157), channel_id=1, source_target_pairs={{0,96},{1,97},{2,98},{3,99},{4,100},{5,101},{6,102},{7,103},{16,11... | collective-permute-start | bytes 1179656 | tf_op jit(solution)/shard_map/ppermute | solution.py:46
  131.7 10.9 %collective-permute-start.19 = (bf16[512,384]{1,0:T(8,128)(2,1)S(1)}, bf16[512,384]{1,0:T(8,128)(2,1)}, u32[]{:S(2)}, u32[]{:S(2)}) collective-permute-start(bf16[512,384]{1,0:T(8,128)(2,1)S(1)} %slice.156), channel_id=1, source_target_pairs={{0,32},{1,33},{2,34},{3,35},{4,36},{5,37},{6,38},{7,39},{16,48},{1... | collective-permute-start | bytes 1179656 | tf_op jit(solution)/shard_map/ppermute | solution.py:46
  140.7 4.9 %collective-permute-start.22 = (bf16[512,384]{1,0:T(8,128)(2,1)S(1)}, bf16[512,384]{1,0:T(8,128)(2,1)}, u32[]{:S(2)}, u32[]{:S(2)}) collective-permute-start(bf16[512,384]{1,0:T(8,128)(2,1)S(1)} %collective-permute-done.20), channel_id=1, source_target_pairs={{0,8},{1,9},{2,10},{3,11},{4,12},{5,13},{6,14},{7,15},{16,24},{17,... | collective-permute-start | bytes 1179656 | tf_op jit(solution)/shard_map/ppermute | solution.py:46
  142.5 3.7 %collective-permute-start.21 = (bf16[512,384]{1,0:T(8,128)(2,1)}, bf16[512,384]{1,0:T(8,128)(2,1)}, u32[]{:S(2)}, u32[]{:S(2)}) collective-permute-start(bf16[512,384]{1,0:T(8,128)(2,1)} %collective-permute-done.19), channel_id=1, source_target_pairs={{0,8},{1,9},{2,10},{3,11},{4,12},{5,13},{6,14},{7,15},{16,24},{17,... | collective-permute-start | bytes 1179656 | tf_op jit(solution)/shard_map/ppermute | solution.py:46
  143.4 1.1 copy-start.10
  143.4 9.8 %collective-permute-start.14 = (bf16[1024,384]{1,0:T(8,128)(2,1)}, bf16[1024,384]{1,0:T(8,128)(2,1)S(1)}, u32[]{:S(2)}, u32[]{:S(2)}) collective-permute-start(bf16[1024,384]{1,0:T(8,128)(2,1)} %bitcast.161), channel_id=1, source_target_pairs={{0,8},{1,9},{2,10},{3,11},{4,12},{5,13},{6,14},{7,15},{16,24},{17,... | collective-permute-start | bytes 2359304 | tf_op jit(solution)/shard_map/ppermute | solution.py:46
  144.5 12.5 %collective-permute-start.17 = (bf16[1024,384]{1,0:T(8,128)(2,1)S(1)}, bf16[1024,384]{1,0:T(8,128)(2,1)S(1)}, u32[]{:S(2)}, u32[]{:S(2)}) collective-permute-start(bf16[1024,384]{1,0:T(8,128)(2,1)S(1)} %copy-done.10), channel_id=1, source_target_pairs={{0,8},{1,9},{2,10},{3,11},{4,12},{5,13},{6,14},{7,15},{16,24},{17,... | collective-permute-start | bytes 2359304 | tf_op jit(solution)/shard_map/ppermute | solution.py:46
  145.6 12.3 %collective-permute-start.18 = (bf16[1024,384]{1,0:T(8,128)(2,1)S(1)}, bf16[1024,384]{1,0:T(8,128)(2,1)S(1)}, u32[]{:S(2)}, u32[]{:S(2)}) collective-permute-start(bf16[1024,384]{1,0:T(8,128)(2,1)S(1)} %collective-permute-done.16), channel_id=1, source_target_pairs={{0,8},{1,9},{2,10},{3,11},{4,12},{5,13},{6,14},{7,15},{16,24},{17,... | collective-permute-start | bytes 2359304 | tf_op jit(solution)/shard_map/ppermute | solution.py:46
  148.6 3.6 %copy-start.2 = (f32[8,128,768]{2,1,0:T(8,128)S(1)}, f32[8,128,768]{2,1,0:T(8,128)}, u32[]{:S(2)}) copy-start(f32[8,128,768]{2,1,0:T(8,128)} %copy-done.1) | copy-start | bytes 9437188
  148.6 3.6 %copy-start.5 = (bf16[8,128,384]{2,1,0:T(8,128)(2,1)S(1)}, bf16[8,128,384]{2,1,0:T(8,128)(2,1)}, u32[]{:S(2)}) copy-start(bf16[8,128,384]{2,1,0:T(8,128)(2,1)} %attend.1) | copy-start | bytes 2359300
  163.0 24.9 %all-to-all-start.2 = ((bf16[8,128,768]{2,1,0:T(8,128)(2,1)}), bf16[8,128,768]{2,1,0:T(8,128)(2,1)}, u32[]{:S(2)}, u32[]{:S(2)}) async-start(bf16[8,128,768]{2,1,0:T(8,128)(2,1)} %bitcast_convert_fusion), calls=%async_computation.2 | async-start | bytes 3145728 | tf_op jit(solution)/shard_map/all_to_all | solution.py:335
  167.5 8.0 %collective-permute-start.23 = (f32[128,384]{1,0:T(8,128)S(1)}, f32[128,384]{1,0:T(8,128)S(1)}, u32[]{:S(2)}, u32[]{:S(2)}) collective-permute-start(f32[128,384]{1,0:T(8,128)S(1)} %slice_select_fusion), channel_id=1, source_target_pairs={{0,16},{16,0},{1,17},{17,1},{2,18},{18,2},{3,19},{19,3},{4,20},{20... | collective-permute-start | bytes 589832 | tf_op jit(solution)/shard_map/ppermute | solution.py:333

commit v6 on v5

--- a/solution.py
+++ b/solution.py
@@ -48,6 +48,10 @@
 
 def x_partner(k):
     return lambda xc, yh, m: (xc ^ (2 * k), yh, m)
+
+
+def y_partner(xc, yh, m):
+    return xc, yh ^ (xc & 1), m ^ 4
 
 
 def core_partner(xc, yh, m):
@@ -95,7 +99,7 @@
 def join_weights(rows, gain, qkv):
     shares, _, cols = rows.shape
     width, group_cols = qkv.shape[1:]
-    per_step = 2
+    per_step = 4
     return pl.pallas_call(
         join_kernel,
         out_shape=jax.ShapeDtypeStruct((ROWS, 3 * group_cols), bf16),
@@ -126,7 +130,7 @@
 
 def attention_kernel(
     lhs_ref, query_w_ref, key_w_ref, value_w_ref, query_p_ref, key_p_ref, value_p_ref,
-    scale_ref, query_gain_ref, key_gain_ref, out_ref, proj_ref, scale_all,
+    scale_ref, query_gain_ref, key_gain_ref, first_ref, second_ref, proj_ref, scale_all,
 ):
     copies, patches, rows = lhs_ref.shape
 
@@ -154,7 +158,8 @@
         value = ((proj_ref[here, 2 * HEAD_DIM :] + value_p) * scale).astype(bf16)
         exp_scores = jnp.exp(dot(query, key_vec, ((1,), (1,))) * HEAD_DIM ** (-0.5)).astype(bf16)
         mixed = dot(exp_scores, jnp.concatenate([value, ones], axis=1), ((1,), (0,)))
-        out_ref[c] = (mixed[:, :HEAD_DIM] / mixed[:, HEAD_DIM:]).astype(bf16)
+        out_ref = first_ref if c < copies // 2 else second_ref
+        out_ref[c % (copies // 2)] = (mixed[:, :HEAD_DIM] / mixed[:, HEAD_DIM:]).astype(bf16)
 
 
 def attend(lhs, joined, scale, query_gain, key_gain):
@@ -168,7 +173,7 @@
 
     return pl.pallas_call(
         attention_kernel,
-        out_shape=jax.ShapeDtypeStruct((copies, patches, group_cols), bf16),
+        out_shape=[jax.ShapeDtypeStruct((copies // 2, patches, group_cols), bf16)] * 2,
         grid=(heads,),
         in_specs=[
             pl.BlockSpec((copies, patches, rows), lambda h: (0, 0, 0)),
@@ -178,7 +183,7 @@
             pl.BlockSpec((1, HEAD_DIM), lambda h: (0, 0)),
             pl.BlockSpec((1, HEAD_DIM), lambda h: (0, 0)),
         ],
-        out_specs=pl.BlockSpec((copies, patches, HEAD_DIM), lambda h: (0, 0, h)),
+        out_specs=[pl.BlockSpec((copies // 2, patches, HEAD_DIM), lambda h: (0, 0, h))] * 2,
         scratch_shapes=[
             pltpu.VMEM((copies * patches, 3 * HEAD_DIM), f32),
             pltpu.VMEM((copies, patches, HEAD_DIM), f32),
@@ -261,6 +266,7 @@
     piece = join_weights(rows, norm_gain[None], jnp.transpose(qkv_weight, (1, 0, 2)))
     lhs_own, own_weight, piece = lax.optimization_barrier((lhs_own, embed_weight, piece))
     piece = send(piece, lambda xc, yh, m: (m, yh, xc))
+    out_far_own = send(out_near[0], y_partner)
     other_weight = send(own_weight, lambda xc, yh, m: (xc, 1 - yh, m ^ 4))
     lhs_own = jnp.stack(lhs_own)
     joined = jnp.broadcast_to(piece[None], (PIECES, *piece.shape))
@@ -278,10 +284,17 @@
     weight_two = jnp.concatenate([first, second], axis=1)
     weight_two = padded(weight_two, LHS_ROWS)
     position_two = jnp.concatenate(my_columns(position_table), axis=1).astype(f32)
-    embedded = jnp.einsum("cpk,kd->cpd", lhs, weight_two, preferred_element_type=f32) + position_two
-
-    average = jnp.mean(embedded, axis=-1)
-    spread = jnp.mean(jnp.square(embedded - average[..., None]), axis=-1)
+    embedded = [
+        jnp.einsum("cpk,kd->cpd", lhs[start : start + 4], weight_two, preferred_element_type=f32)
+        + position_two
+        for start in (0, 4)
+    ]
+    averages = [jnp.mean(half, axis=-1) for half in embedded]
+    spreads = [
+        jnp.mean(jnp.square(half - average[..., None]), axis=-1)
+        for half, average in zip(embedded, averages)
+    ]
+    average, spread = jnp.concatenate(averages, axis=0), jnp.concatenate(spreads, axis=0)
     stat = jnp.stack([average, spread])
     for partners in ((1,), (2, 4, 6)):
         stats = [stat]
@@ -293,46 +306,57 @@
         stat = jnp.stack([average, spread])
     scale = lax.rsqrt(stat[1] + epsilon)
 
-    out_near, joined = lax.optimization_barrier((jnp.stack(out_near), joined))
-    out_far = send(out_near, lambda xc, yh, m: (xc, yh ^ (xc & 1), m ^ 4))
+    out_rest, joined = lax.optimization_barrier((jnp.stack(out_near[1:]), joined))
+    out_far = send(out_rest, y_partner)
 
     head_out = attend(lhs, joined, scale, query_gain, key_gain)
-    head_out = head_out.reshape(8 * patches, -1)
-
-    tokens = head_out.shape[0]
-    heads = [None] * 8
-    heads[0] = head_out
-    heads[1] = send(head_out, core_partner)
-    heads[2] = send(head_out, x_partner(1))
-    heads[6] = send(head_out, x_partner(3))
-    relayed = [
-        send(heads[6][: tokens // 2], x_partner(1)),
-        send(heads[2][tokens // 2 :], x_partner(3)),
-    ]
-    heads[3] = send(heads[2], core_partner)
-    heads[7] = send(heads[6], core_partner)
-    mates = [send(half, core_partner) for half in relayed]
-    heads[4] = lax.optimization_barrier(jnp.concatenate(relayed, axis=0))
-    heads[5] = lax.optimization_barrier(jnp.concatenate(mates, axis=0))
+    tokens = 4 * patches
+    top, bottom = (half.reshape(tokens, -1) for half in head_out)
+
+    heads = {(0, 0): top, (0, 1): bottom}
+    heads[6, 0] = send(top, x_partner(3))
+    heads[2, 1] = send(bottom, x_partner(1))
+    heads[2, 0] = send(top, x_partner(1))
+    heads[6, 1] = send(bottom, x_partner(3))
+    heads[1, 0] = send(top, core_partner)
+    heads[1, 1] = send(bottom, core_partner)
+    heads[4, 0] = send(heads[6, 0], x_partner(1))
+    heads[4, 1] = send(heads[2, 1], x_partner(3))
+    for k in (2, 6, 4):
+        for half in range(2):
+            heads[k + 1, half] = send(heads[k, half], core_partner)
 
     order = lax.axis_index(MP) ^ (2 * xi + ci)
-    out_all = jnp.zeros((8, *out_near.shape[1:]), bf16)
+    out_all = jnp.zeros((8, *out_near[0].shape), bf16)
     for k in range(4):
-        out_all = lax.dynamic_update_slice(out_all, out_near[k : k + 1], (order ^ k, 0, 0))
-        out_all = lax.dynamic_update_slice(out_all, out_far[k : k + 1], (order ^ (4 + k), 0, 0))
-    output = embedded.reshape(tokens, 2 * cols)
-    for k in (0, 1, 2, 6, 3, 7):
-        output = lax.optimization_barrier(output + dot(heads[k], out_all[k], ((1,), (0,))))
-    for k in (4, 5):
-        output = lax.optimization_barrier(output + dot(heads[k], out_all[k], ((1,), (0,))))
-    output = output.reshape(8, patches, 2 * cols)
-
-    summed = jnp.sum(output, axis=0) * (1.0 / 16)
+        far = out_far[k - 1] if k else out_far_own
+        out_all = lax.dynamic_update_slice(out_all, out_near[k][None], (order ^ k, 0, 0))
+        out_all = lax.dynamic_update_slice(out_all, far[None], (order ^ (4 + k), 0, 0))
+    output = [half.reshape(tokens, 2 * cols) for half in embedded]
+
+    def add(half, k):
+        grown = output[half] + dot(heads[k, half], out_all[k], ((1,), (0,)))
+        output[half] = lax.optimization_barrier(grown)
+
+    for half in range(2):
+        for k in (0, 1):
+            add(half, k)
+    for k in (6, 2):
+        for half in (0, 1) if k == 6 else (1, 0):
+            add(half, k)
+            add(half, k + 1)
+    for half in range(2):
+        for k in (4, 5):
+            add(half, k)
+    output = [half.reshape(4, patches, 2 * cols) for half in output]
+
+    summed = (jnp.sum(output[0], axis=0) + jnp.sum(output[1], axis=0)) * (1.0 / 16)
     kept = jnp.where(yhi == 0, summed[:, :cols], summed[:, cols:])
     sent = jnp.where(yhi == 0, summed[:, cols:], summed[:, :cols])
     smoothed = (kept + lax.ppermute(sent, "yh", [(0, 1), (1, 0)]))[:, None, :]
 
-    moved = lax.all_to_all(output.astype(bf16), GROUP, 0, 0, tiled=True)
+    rounded = jnp.concatenate([half.astype(bf16) for half in output], axis=0)
+    moved = lax.all_to_all(rounded, GROUP, 0, 0, tiled=True)
     features = assemble(moved).reshape(patches, 1, 1, width)
     return features, smoothed
 

time: 192 us -> 198 us (1.031)
  waiting for transfers between devices: 81.1 us -> 47.3 us
  matrix products: 9.35 us -> 29.2 us
  starting transfers between devices: 42 us -> 60.7 us
  local copies, waits for them, and re-layouts: 19.8 us -> 26 us
  other arithmetic: 15.7 us -> 12.4 us
  Pallas kernels: 21.4 us -> 19.3 us
    ppermute x23 -> x29, waiting for transfers between devices: 55.4 us -> 18.2 us  [send(): return lax.ppermute(array, AXES, pairs)]
    dot_general x8 -> x16, matrix products: 7.8 us -> 26.3 us  [dot(): lax.dot_general(left, right, (dims, ((), ())), preferred_element_type=f32)]
    ppermute x23 -> x29, starting transfers between devices: 25.4 us -> 40.2 us  [send(): return lax.ppermute(array, AXES, pairs)]
    all_to_all x1, waiting for transfers between devices: 1.52 us -> 10.8 us  [block(): lax.all_to_all(joined, AXES, 0, 0, axis_index_groups=HOLDERS, tiled=True)]
    dynamic_update_slice x8 -> x7, local copies, waits for them, and re-layouts: 4.79 us -> 10.3 us  [the longest x4 7.68 us: block(): lax.dynamic_update_slice(out_all, far[None], (order ^ 4 + k, 0, 0))]
    all_to_all x1, waiting for transfers between devices: 5.06 us -> 0.01 us  [block(): rows = lax.all_to_all(rows, AXES, 0, 0, axis_index_groups=NEAR, tiled=True)]
    all_to_all x1, starting transfers between devices: 3.71 us -> 6.76 us  [block(): lax.all_to_all(joined, AXES, 0, 0, axis_index_groups=HOLDERS, tiled=True)]
    another operation x2 -> x1, other arithmetic: 4.22 us -> 1.49 us  [block(): jnp.stack(out_near[1:])]
  transfers between devices with their start and end apart: 27 -> 33, of which waited for: 11 -> 9; matrix products, arithmetic and copies ran while one was open for 17% -> 29% of each run, Pallas kernels for 10% -> 8%
where the time goes in v6:
time: 198 us; the launch traced here: 196 us
  starting transfers between devices  60.7 us (31%)
  waiting for transfers between devices  47.3 us (24%)
  matrix products  29.2 us (15%)
  local copies, waits for them, and re-layouts  26 us (13%)
  Pallas kernels  19.3 us (10%)
  other arithmetic  12.4 us (6%)
    ppermute x29, starting transfers between devices, send(): return lax.ppermute(array, AXES, pairs)  40.2 us
    dot_general x16, matrix products, dot(): lax.dot_general(left, right, (dims, ((), ())), preferred_element_type=f32)  26.3 us
    ppermute x29, waiting for transfers between devices, send(): return lax.ppermute(array, AXES, pairs)  18.2 us
    all_to_all x1, waiting for transfers between devices, block(): moved = lax.all_to_all(rounded, GROUP, 0, 0, tiled=True)  11.5 us
    all_to_all x1, waiting for transfers between devices, block(): lax.all_to_all(joined, AXES, 0, 0, axis_index_groups=HOLDERS, tiled=True)  10.8 us
    pallas_call x1, Pallas kernels, attend(): pl.pallas_call(attention_kernel, out_shape=[jax.ShapeDtypeStruct((copies...  8.71 us
    all_to_all x1, starting transfers between devices, block(): rows = lax.all_to_all(rows, AXES, 0, 0, axis_index_groups=NEAR, tiled=True)  8.26 us
    pallas_call x1, Pallas kernels, join_weights(): pl.pallas_call(join_kernel, out_shape=jax.ShapeDtypeStruct((ROWS, 3 * gro...  7.93 us
  transfers between devices with their start and end apart: 33, of which 9 were waited for; matrix products, arithmetic and copies ran while one was open for 29% of the time, Pallas kernels for 8%

profile of v6, /device:TPU:1, one launch (start us, length us, event | category | flops | bytes accessed | tf_op | source)
XLA Modules:
  0.0 196.3 jit_solution(7727665386580198778)
XLA Ops:
  1.8 1.9 fusion.6
  3.6 8.3 %all-to-all-start = ((bf16[16,48,384]{2,1,0:T(8,128)(2,1)}), bf16[16,48,384]{2,1,0:T(8,128)(2,1)S(1)}, u32[]{:S(2)}, u32[]{:S(2)}) async-start(bf16[16,48,384]{2,1,0:T(8,128)(2,1)} %bitcast.3), calls=%async_computation | async-start | bytes 1179648 | tf_op jit(solution)/shard_map/all_to_all | solution.py:256
  16.5 1.6 collective-permute-start.5
  18.1 3.3 %collective-permute-start.6 = (bf16[384,768]{1,0:T(8,128)(2,1)}, bf16[384,768]{1,0:T(8,128)(2,1)S(1)}, u32[]{:S(2)}, u32[]{:S(2)}) collective-permute-start(bf16[384,768]{1,0:T(8,128)(2,1)} %pad_maximum_fusion.3), channel_id=1, source_target_pairs={{0,2},{1,3},{2,0},{3,1},{4,6},{5,7},{6,4},{7,5},{16,18},{17,19},{1... | collective-permute-start | bytes 1769480 | tf_op jit(solution)/shard_map/ppermute | solution.py:46
  21.4 2.4 %collective-permute-start.1 = (bf16[128,640]{1,0:T(8,128)(2,1)S(1)}, bf16[128,640]{1,0:T(8,128)(2,1)S(1)}, u32[]{:S(2)}, u32[]{:S(2)}) collective-permute-start(bf16[128,640]{1,0:T(8,128)(2,1)S(1)} %pad_bitcast_fusion), channel_id=1, source_target_pairs={{0,64},{1,65},{2,66},{3,67},{4,68},{5,69},{6,70},{7,71},{16,80},{1... | collective-permute-start | bytes 491528 | tf_op jit(solution)/shard_map/ppermute | solution.py:46
  24.0 1.7 collective-permute-start.2
  27.3 7.9 %join_weights.1 = bf16[48,1152]{1,0:T(8,128)(2,1)} custom-call(bf16[16,48,384]{2,1,0:T(8,128)(2,1)} %copy-done.9, f32[1,6144]{1,0:T(1,128)} %bitcast.210, bf16[3,6144,384]{2,1,0:T(8,128)(2,1)} %bitcast.193), custom_call_target="tpu_custom_call" | custom-call | flops 679477248 | bytes 14155776 | tf_op jit(solution)/shard_map/join_weights/pallas_call | solution.py:103
  35.3 2.5 %collective-permute-start.4 = (bf16[588,384]{1,0:T(8,128)(2,1)}, bf16[588,384]{1,0:T(8,128)(2,1)}, u32[]{:S(2)}, u32[]{:S(2)}) collective-permute-start(bf16[588,384]{1,0:T(8,128)(2,1)} %param.11), channel_id=1, source_target_pairs={{0,20},{1,21},{2,22},{3,23},{4,16},{5,17},{6,18},{7,19},{16,4},{17... | collective-permute-start | bytes 1354760 | tf_op jit(solution)/shard_map/ppermute | solution.py:46
  38.7 1.9 collective-permute-start.3
  40.8 3.6 %collective-permute-start.8 = (bf16[48,1152]{1,0:T(8,128)(2,1)S(1)}, bf16[48,1152]{1,0:T(8,128)(2,1)S(1)}, u32[]{:S(2)}, u32[]{:S(2)}) collective-permute-start(bf16[48,1152]{1,0:T(8,128)(2,1)S(1)} %copy-done.25), channel_id=1, source_target_pairs={{0,0},{1,8},{2,32},{3,40},{4,64},{5,72},{6,96},{7,104},{16,16},{17... | collective-permute-start | bytes 331784 | tf_op jit(solution)/shard_map/ppermute | solution.py:46
  44.4 2.6 %collective-permute-done.6 = bf16[384,768]{1,0:T(8,128)(2,1)S(1)} collective-permute-done((bf16[384,768]{1,0:T(8,128)(2,1)}, bf16[384,768]{1,0:T(8,128)(2,1)S(1)}, u32[]{:S(2)}, u32[]{:S(2)}) %collective-permute-start.6) | collective-permute-done | bytes 589856 | tf_op jit(solution)/shard_map/ppermute | solution.py:46
  47.1 2.2 %collective-permute-done.7 = bf16[384,768]{1,0:T(8,128)(2,1)S(1)} collective-permute-done((bf16[384,768]{1,0:T(8,128)(2,1)}, bf16[384,768]{1,0:T(8,128)(2,1)S(1)}, u32[]{:S(2)}, u32[]{:S(2)}) %collective-permute-start.7) | collective-permute-done | bytes 589856 | tf_op jit(solution)/shard_map/ppermute | solution.py:46
  52.1 6.8 %all-to-all-start.1 = ((bf16[16,48,1152]{2,1,0:T(8,128)(2,1)}), bf16[16,48,1152]{2,1,0:T(8,128)(2,1)S(1)}, u32[]{:S(2)}, u32[]{:S(2)}) async-start(bf16[16,48,1152]{2,1,0:T(8,128)(2,1)} %broadcast_in_dim.39), calls=%async_computation.1 | async-start | bytes 3538944 | tf_op jit(solution)/shard_map/all_to_all | solution.py:273
  65.3 2.0 %fusion.52 = (f32[4,128]{1,0:T(4,128)S(1)}, f32[4,128,768]{2,1,0:T(8,128)S(1)}) fusion(f32[128,768]{1,0:T(8,128)S(1)} %copy-done.20, bf16[8,128,640]{2,1,0:T(8,128)(2,1)} %copy-done.3, bf16[588,384]{1,0:T(8,128)(2,1)S(1)} %get-tuple-element.28, bf16[588,384]{1,0:T(8,128)(2,1)S(1)} %get-tuple-element.27), kind=kOutput, calls=%fused_computation.130 | convolution fusion | flops 507543040 | bytes 4182016 | tf_op jit(solution)/shard_map/cpk,kd->cpd/dot_general | solution.py:288
  70.6 10.8 %all-to-all-done.1 = bf16[16,48,1152]{2,1,0:T(8,128)(2,1)S(1)} async-done(((bf16[16,48,1152]{2,1,0:T(8,128)(2,1)}), bf16[16,48,1152]{2,1,0:T(8,128)(2,1)S(1)}, u32[]{:S(2)}, u32[]{:S(2)}) %all-to-all-start.1) | async-done | bytes 1769504 | tf_op jit(solution)/shard_map/all_to_all | solution.py:273
  81.4 2.3 %collective-permute-start.14 = (bf16[3,384,768]{2,1,0:T(8,128)(2,1)}, bf16[3,384,768]{2,1,0:T(8,128)(2,1)}, u32[]{:S(2)}, u32[]{:S(2)}) collective-permute-start(bf16[3,384,768]{2,1,0:T(8,128)(2,1)} %pad_maximum_fusion), channel_id=1, source_target_pairs={{0,4},{1,5},{2,6},{3,7},{4,0},{5,1},{6,2},{7,3},{16,20},{17,21},{1... | collective-permute-start | bytes 5308424 | tf_op jit(solution)/shard_map/ppermute | solution.py:46
  85.8 2.0 %collective-permute-start.11 = (f32[2,8,128]{2,1,0:T(8,128)S(1)}, f32[2,8,128]{2,1,0:T(8,128)S(1)}, u32[]{:S(2)}, u32[]{:S(2)}) collective-permute-start(f32[2,8,128]{2,1,0:T(8,128)S(1)} %pad_maximum_fusion.5), channel_id=1, source_target_pairs={{0,64},{1,65},{2,66},{3,67},{4,68},{5,69},{6,70},{7,71},{16,80},{1... | collective-permute-start | bytes 24584 | tf_op jit(solution)/shard_map/ppermute | solution.py:46
  87.8 1.8 collective-permute-start.12
  89.6 2.5 %broadcast_in_dim.42 = bf16[8,384,768]{2,1,0:T(8,128)(2,1)} broadcast(bf16[]{:T(256)} %constant.25.clone.1), dimensions={} | broadcast | bytes 4718594 | tf_op jit(solution)/shard_map/broadcast_in_dim | solution.py:330
  93.7 8.7 %attend.1 = (bf16[4,128,384]{2,1,0:T(8,128)(2,1)}, bf16[4,128,384]{2,1,0:T(8,128)(2,1)}) custom-call(bf16[8,128,640]{2,1,0:T(8,128)(2,1)} %copy-done.3, bf16[768,1152]{1,0:T(8,128)(2,1)} %bitcast.185, bf16[768,1152]{1,0:T(8,128)(2,1)} %bitcast.186, bf16[768,1152]{1,0:T(8,128)(2,1)} %bitcast.187, bf16[768,1152]{1,0:T(8,128)(2,1)} %bitcast.188, ...), custom_call_target="tpu_custom_call" | custom-call | flops 3019898880 | bytes 7864320 | tf_op jit(solution)/shard_map/attend/pallas_call | solution.py:174
  103.3 7.4 %collective-permute-done.13 = bf16[384,768]{1,0:T(8,128)(2,1)} collective-permute-done((bf16[384,768]{1,0:T(8,128)(2,1)}, bf16[384,768]{1,0:T(8,128)(2,1)}, u32[]{:S(2)}, u32[]{:S(2)}) %collective-permute-start.13) | collective-permute-done | bytes 589856 | tf_op jit(solution)/shard_map/ppermute | solution.py:46
  110.8 1.9 bitcast_dynamic-update-slice_fusion
  113.6 2.3 %collective-permute-start.15 = (bf16[512,384]{1,0:T(8,128)(2,1)S(1)}, bf16[512,384]{1,0:T(8,128)(2,1)S(1)}, u32[]{:S(2)}, u32[]{:S(2)}) collective-permute-start(bf16[512,384]{1,0:T(8,128)(2,1)S(1)} %bitcast.207), channel_id=1, source_target_pairs={{0,8},{1,9},{2,10},{3,11},{4,12},{5,13},{6,14},{7,15},{16,24},{17,... | collective-permute-start | bytes 1179656 | tf_op jit(solution)/shard_map/ppermute | solution.py:46
  119.1 1.9 slice_dynamic-update-slice_fusion.2
  121.9 1.9 slice_dynamic-update-slice_fusion.1
  124.6 1.9 slice_dynamic-update-slice_fusion
  126.6 1.8 bitcast_add_fusion.1
  128.3 1.6 bitcast_add_fusion
  130.1 1.6 convolution_add_fusion.9
  131.7 3.2 %collective-permute-done.25 = bf16[512,384]{1,0:T(8,128)(2,1)S(1)} collective-permute-done((bf16[512,384]{1,0:T(8,128)(2,1)S(1)}, bf16[512,384]{1,0:T(8,128)(2,1)S(1)}, u32[]{:S(2)}, u32[]{:S(2)}) %collective-permute-start.25) | collective-permute-done | bytes 393248 | tf_op jit(solution)/shard_map/ppermute | solution.py:46
  136.8 1.6 fusion.12
  138.6 1.6 convolution_add_fusion.8
  142.3 2.5 %collective-permute-done.20 = bf16[512,384]{1,0:T(8,128)(2,1)S(1)} collective-permute-done((bf16[512,384]{1,0:T(8,128)(2,1)S(1)}, bf16[512,384]{1,0:T(8,128)(2,1)S(1)}, u32[]{:S(2)}, u32[]{:S(2)}) %collective-permute-start.20) | collective-permute-done | bytes 393248 | tf_op jit(solution)/shard_map/ppermute | solution.py:46
  144.8 1.7 collective-permute-start.21
  148.0 1.6 convolution_add_fusion.5
  149.6 1.6 fusion.14
  151.3 1.6 fusion.11
  153.3 1.6 convolution_add_fusion.7
  155.0 1.6 convolution_add_fusion.4
  156.6 1.6 fusion.16
  158.3 1.6 fusion.13
  160.3 1.6 convolution_add_fusion.6
  162.0 1.6 convolution_add_fusion.3
  165.4 1.6 convolution_add_fusion.2
  168.5 4.3 %all-to-all-start.2 = ((bf16[8,128,768]{2,1,0:T(8,128)(2,1)}), bf16[8,128,768]{2,1,0:T(8,128)(2,1)}, u32[]{:S(2)}, u32[]{:S(2)}) async-start(bf16[8,128,768]{2,1,0:T(8,128)(2,1)} %pad_maximum_fusion.1), calls=%async_computation.2 | async-start | bytes 3145728 | tf_op jit(solution)/shard_map/all_to_all | solution.py:359
  174.3 6.8 %collective-permute-done.29 = f32[128,384]{1,0:T(8,128)S(1)} collective-permute-done((f32[128,384]{1,0:T(8,128)S(1)}, f32[128,384]{1,0:T(8,128)S(1)}, u32[]{:S(2)}, u32[]{:S(2)}) %collective-permute-start.29) | collective-permute-done | bytes 196640 | tf_op jit(solution)/shard_map/ppermute | solution.py:356
  182.0 11.5 %all-to-all-done.2.in_ref = bf16[8,128,768]{2,1,0:T(8,128)(2,1)} async-done(((bf16[8,128,768]{2,1,0:T(8,128)(2,1)}), bf16[8,128,768]{2,1,0:T(8,128)(2,1)}, u32[]{:S(2)}, u32[]{:S(2)}) %all-to-all-start.2) | async-done | bytes 1572896 | tf_op jit(solution)/shard_map/all_to_all | solution.py:359
  193.4 2.7 %assemble.1 = bf16[128,6144]{1,0:T(8,128)(2,1)} custom-call(bf16[8,128,768]{2,1,0:T(8,128)(2,1)} %all-to-all-done.2.in_ref), custom_call_target="tpu_custom_call" | custom-call | tf_op jit(solution)/shard_map/assemble/pallas_call | solution.py:222
  (148 shorter events, 43.2 us)
Async XLA Ops:
  0.6 11.3 %copy-start.23 = (bf16[1,588,128]{2,1,0:T(8,128)(2,1)S(1)}, bf16[1,588,128]{2,1,0:T(8,128)(2,1)}, u32[]{:S(2)}) copy-start(bf16[1,588,128]{2,1,0:T(8,128)(2,1)} %param.9) | copy-start | bytes 451588
  0.7 11.4 %copy-start.24 = (bf16[1,1,588,128]{3,2,1,0:T(8,128)(2,1)S(1)}, bf16[1,1,588,128]{3,2,1,0:T(8,128)(2,1)}, u32[]{:S(2)}) copy-start(bf16[1,1,588,128]{3,2,1,0:T(8,128)(2,1)} %param.10) | copy-start | bytes 451588
  3.6 22.9 %all-to-all-start = ((bf16[16,48,384]{2,1,0:T(8,128)(2,1)}), bf16[16,48,384]{2,1,0:T(8,128)(2,1)S(1)}, u32[]{:S(2)}, u32[]{:S(2)}) async-start(bf16[16,48,384]{2,1,0:T(8,128)(2,1)} %bitcast.3), calls=%async_computation | async-start | bytes 1179648 | tf_op jit(solution)/shard_map/all_to_all | solution.py:256
  12.3 11.7 %collective-permute-start = (bf16[128,640]{1,0:T(8,128)(2,1)S(1)}, bf16[128,640]{1,0:T(8,128)(2,1)S(1)}, u32[]{:S(2)}, u32[]{:S(2)}) collective-permute-start(bf16[128,640]{1,0:T(8,128)(2,1)S(1)} %pad_bitcast_fusion), channel_id=1, source_target_pairs={{0,32},{1,33},{2,34},{3,35},{4,36},{5,37},{6,38},{7,39},{16,48},{1... | collective-permute-start | bytes 491528 | tf_op jit(solution)/shard_map/ppermute | solution.py:46
  16.5 24.3 %collective-permute-start.5 = (bf16[384,768]{1,0:T(8,128)(2,1)}, bf16[384,768]{1,0:T(8,128)(2,1)S(1)}, u32[]{:S(2)}, u32[]{:S(2)}) collective-permute-start(bf16[384,768]{1,0:T(8,128)(2,1)} %pad_maximum_fusion.3), channel_id=1, source_target_pairs={{0,1},{1,0},{2,3},{3,2},{4,5},{5,4},{6,7},{7,6},{16,17},{17,16},{1... | collective-permute-start | bytes 1769480 | tf_op jit(solution)/shard_map/ppermute | solution.py:46
  18.1 28.9 %collective-permute-start.6 = (bf16[384,768]{1,0:T(8,128)(2,1)}, bf16[384,768]{1,0:T(8,128)(2,1)S(1)}, u32[]{:S(2)}, u32[]{:S(2)}) collective-permute-start(bf16[384,768]{1,0:T(8,128)(2,1)} %pad_maximum_fusion.3), channel_id=1, source_target_pairs={{0,2},{1,3},{2,0},{3,1},{4,6},{5,7},{6,4},{7,5},{16,18},{17,19},{1... | collective-permute-start | bytes 1769480 | tf_op jit(solution)/shard_map/ppermute | solution.py:46
  21.4 27.8 %collective-permute-start.7 = (bf16[384,768]{1,0:T(8,128)(2,1)}, bf16[384,768]{1,0:T(8,128)(2,1)S(1)}, u32[]{:S(2)}, u32[]{:S(2)}) collective-permute-start(bf16[384,768]{1,0:T(8,128)(2,1)} %pad_maximum_fusion.3), channel_id=1, source_target_pairs={{0,3},{1,2},{2,1},{3,0},{4,7},{5,6},{6,5},{7,4},{16,19},{17,18},{1... | collective-permute-start | bytes 1769480 | tf_op jit(solution)/shard_map/ppermute | solution.py:46
  21.4 13.8 %collective-permute-start.1 = (bf16[128,640]{1,0:T(8,128)(2,1)S(1)}, bf16[128,640]{1,0:T(8,128)(2,1)S(1)}, u32[]{:S(2)}, u32[]{:S(2)}) collective-permute-start(bf16[128,640]{1,0:T(8,128)(2,1)S(1)} %pad_bitcast_fusion), channel_id=1, source_target_pairs={{0,64},{1,65},{2,66},{3,67},{4,68},{5,69},{6,70},{7,71},{16,80},{1... | collective-permute-start | bytes 491528 | tf_op jit(solution)/shard_map/ppermute | solution.py:46
  24.0 11.3 %collective-permute-start.2 = (bf16[128,640]{1,0:T(8,128)(2,1)S(1)}, bf16[128,640]{1,0:T(8,128)(2,1)S(1)}, u32[]{:S(2)}, u32[]{:S(2)}) collective-permute-start(bf16[128,640]{1,0:T(8,128)(2,1)S(1)} %pad_bitcast_fusion), channel_id=1, source_target_pairs={{0,96},{1,97},{2,98},{3,99},{4,100},{5,101},{6,102},{7,103},{16,11... | collective-permute-start | bytes 491528 | tf_op jit(solution)/shard_map/ppermute | solution.py:46
  35.3 5.5 %copy-start.25 = (bf16[48,1152]{1,0:T(8,128)(2,1)S(1)}, bf16[48,1152]{1,0:T(8,128)(2,1)}, u32[]{:S(2)}) copy-start(bf16[48,1152]{1,0:T(8,128)(2,1)} %join_weights.1) | copy-start | bytes 331780
  35.3 23.6 %collective-permute-start.4 = (bf16[588,384]{1,0:T(8,128)(2,1)}, bf16[588,384]{1,0:T(8,128)(2,1)}, u32[]{:S(2)}, u32[]{:S(2)}) collective-permute-start(bf16[588,384]{1,0:T(8,128)(2,1)} %param.11), channel_id=1, source_target_pairs={{0,20},{1,21},{2,22},{3,23},{4,16},{5,17},{6,18},{7,19},{16,4},{17... | collective-permute-start | bytes 1354760 | tf_op jit(solution)/shard_map/ppermute | solution.py:46
  38.7 21.5 %collective-permute-start.3 = (bf16[4,128,640]{2,1,0:T(8,128)(2,1)}, bf16[4,128,640]{2,1,0:T(8,128)(2,1)}, u32[]{:S(2)}, u32[]{:S(2)}) collective-permute-start(bf16[4,128,640]{2,1,0:T(8,128)(2,1)} %pad_maximum_fusion.2), channel_id=1, source_target_pairs={{0,8},{1,9},{2,10},{3,11},{4,12},{5,13},{6,14},{7,15},{16,24},{17,... | collective-permute-start | bytes 1966088 | tf_op jit(solution)/shard_map/ppermute | solution.py:46
  40.8 9.9 %copy-start.14 = (bf16[384,768]{1,0:T(8,128)(2,1)}, bf16[384,768]{1,0:T(8,128)(2,1)S(1)}, u32[]{:S(2)}) copy-start(bf16[384,768]{1,0:T(8,128)(2,1)S(1)} %collective-permute-done.5) | copy-start | bytes 1769476
  40.8 9.9 %collective-permute-start.8 = (bf16[48,1152]{1,0:T(8,128)(2,1)S(1)}, bf16[48,1152]{1,0:T(8,128)(2,1)S(1)}, u32[]{:S(2)}, u32[]{:S(2)}) collective-permute-start(bf16[48,1152]{1,0:T(8,128)(2,1)S(1)} %copy-done.25), channel_id=1, source_target_pairs={{0,0},{1,8},{2,32},{3,40},{4,64},{5,72},{6,96},{7,104},{16,16},{17... | collective-permute-start | bytes 331784 | tf_op jit(solution)/shard_map/ppermute | solution.py:46
  47.1 3.7 %copy-start.12 = (bf16[384,768]{1,0:T(8,128)(2,1)}, bf16[384,768]{1,0:T(8,128)(2,1)S(1)}, u32[]{:S(2)}) copy-start(bf16[384,768]{1,0:T(8,128)(2,1)S(1)} %collective-permute-done.6) | copy-start | bytes 1769476
  52.1 29.2 %all-to-all-start.1 = ((bf16[16,48,1152]{2,1,0:T(8,128)(2,1)}), bf16[16,48,1152]{2,1,0:T(8,128)(2,1)S(1)}, u32[]{:S(2)}, u32[]{:S(2)}) async-start(bf16[16,48,1152]{2,1,0:T(8,128)(2,1)} %broadcast_in_dim.39), calls=%async_computation.1 | async-start | bytes 3538944 | tf_op jit(solution)/shard_map/all_to_all | solution.py:273
  58.9 4.3 %copy-start.19 = (bf16[128,640]{1,0:T(8,128)(2,1)S(1)}, bf16[128,640]{1,0:T(8,128)(2,1)}, u32[]{:S(2)}) copy-start(bf16[128,640]{1,0:T(8,128)(2,1)} %copy-done.18) | copy-start | bytes 491524
  60.2 5.0 %copy-start.20 = (f32[128,768]{1,0:T(8,128)S(1)}, f32[128,768]{1,0:T(8,128)}, u32[]{:S(2)}) copy-start(f32[128,768]{1,0:T(8,128)} %maximum_convert_fusion) | copy-start | bytes 1179652
  81.4 10.8 %copy-start = (bf16[16,48,1152]{2,1,0:T(8,128)(2,1)}, bf16[16,48,1152]{2,1,0:T(8,128)(2,1)S(1)}, u32[]{:S(2)}) copy-start(bf16[16,48,1152]{2,1,0:T(8,128)(2,1)S(1)} %all-to-all-done.1) | copy-start | bytes 5308420
  81.4 36.9 %collective-permute-start.14 = (bf16[3,384,768]{2,1,0:T(8,128)(2,1)}, bf16[3,384,768]{2,1,0:T(8,128)(2,1)}, u32[]{:S(2)}, u32[]{:S(2)}) collective-permute-start(bf16[3,384,768]{2,1,0:T(8,128)(2,1)} %pad_maximum_fusion), channel_id=1, source_target_pairs={{0,4},{1,5},{2,6},{3,7},{4,0},{5,1},{6,2},{7,3},{16,20},{17,21},{1... | collective-permute-start | bytes 5308424 | tf_op jit(solution)/shard_map/ppermute | solution.py:46
  83.7 2.0 %collective-permute-start.9 = (f32[2,8,128]{2,1,0:T(8,128)S(1)}, f32[2,8,128]{2,1,0:T(8,128)S(1)}, u32[]{:S(2)}, u32[]{:S(2)}) collective-permute-start(f32[2,8,128]{2,1,0:T(8,128)S(1)} %pad_maximum_fusion.4), channel_id=1, source_target_pairs={{0,8},{1,9},{2,10},{3,11},{4,12},{5,13},{6,14},{7,15},{16,24},{17,... | collective-permute-start | bytes 24584 | tf_op jit(solution)/shard_map/ppermute | solution.py:46
  84.5 26.3 %collective-permute-start.13 = (bf16[384,768]{1,0:T(8,128)(2,1)}, bf16[384,768]{1,0:T(8,128)(2,1)}, u32[]{:S(2)}, u32[]{:S(2)}) collective-permute-start(bf16[384,768]{1,0:T(8,128)(2,1)} %pad_maximum_fusion.3), channel_id=1, source_target_pairs={{0,4},{1,5},{2,6},{3,7},{4,0},{5,1},{6,2},{7,3},{16,20},{17,21},{1... | collective-permute-start | bytes 1769480 | tf_op jit(solution)/shard_map/ppermute | solution.py:46
  85.7 6.4 %copy-start.6 = (bf16[384,384]{1,0:T(8,128)(2,1)S(1)}, bf16[384,384]{1,0:T(8,128)(2,1)}, u32[]{:S(2)}) copy-start(bf16[384,384]{1,0:T(8,128)(2,1)} %copy-done.5) | copy-start | bytes 884740
  85.7 6.4 %copy-start.8 = (bf16[384,384]{1,0:T(8,128)(2,1)S(1)}, bf16[384,384]{1,0:T(8,128)(2,1)}, u32[]{:S(2)}) copy-start(bf16[384,384]{1,0:T(8,128)(2,1)} %copy-done.7) | copy-start | bytes 884740
  85.7 7.3 %collective-permute-start.10 = (f32[2,8,128]{2,1,0:T(8,128)S(1)}, f32[2,8,128]{2,1,0:T(8,128)S(1)}, u32[]{:S(2)}, u32[]{:S(2)}) collective-permute-start(f32[2,8,128]{2,1,0:T(8,128)S(1)} %pad_maximum_fusion.5), channel_id=1, source_target_pairs={{0,32},{1,33},{2,34},{3,35},{4,36},{5,37},{6,38},{7,39},{16,48},{1... | collective-permute-start | bytes 24584 | tf_op jit(solution)/shard_map/ppermute | solution.py:46
  85.8 7.2 %collective-permute-start.11 = (f32[2,8,128]{2,1,0:T(8,128)S(1)}, f32[2,8,128]{2,1,0:T(8,128)S(1)}, u32[]{:S(2)}, u32[]{:S(2)}) collective-permute-start(f32[2,8,128]{2,1,0:T(8,128)S(1)} %pad_maximum_fusion.5), channel_id=1, source_target_pairs={{0,64},{1,65},{2,66},{3,67},{4,68},{5,69},{6,70},{7,71},{16,80},{1... | collective-permute-start | bytes 24584 | tf_op jit(solution)/shard_map/ppermute | solution.py:46
  87.8 5.2 %collective-permute-start.12 = (f32[2,8,128]{2,1,0:T(8,128)S(1)}, f32[2,8,128]{2,1,0:T(8,128)S(1)}, u32[]{:S(2)}, u32[]{:S(2)}) collective-permute-start(f32[2,8,128]{2,1,0:T(8,128)S(1)} %pad_maximum_fusion.5), channel_id=1, source_target_pairs={{0,96},{1,97},{2,98},{3,99},{4,100},{5,101},{6,102},{7,103},{16,11... | collective-permute-start | bytes 24584 | tf_op jit(solution)/shard_map/ppermute | solution.py:46
  102.4 10.3 %copy-start.15 = (bf16[384,768]{1,0:T(8,128)(2,1)S(1)}, bf16[384,768]{1,0:T(8,128)(2,1)}, u32[]{:S(2)}) copy-start(bf16[384,768]{1,0:T(8,128)(2,1)} %copy-done.14) | copy-start | bytes 1769476
  102.4 11.2 %copy-start.22 = (bf16[4,128,384]{2,1,0:T(8,128)(2,1)S(1)}, bf16[4,128,384]{2,1,0:T(8,128)(2,1)}, u32[]{:S(2)}) copy-start(bf16[4,128,384]{2,1,0:T(8,128)(2,1)} %get-tuple-element.19) | copy-start | bytes 1179652
  102.4 13.5 %copy-start.21 = (bf16[4,128,384]{2,1,0:T(8,128)(2,1)S(1)}, bf16[4,128,384]{2,1,0:T(8,128)(2,1)}, u32[]{:S(2)}) copy-start(bf16[4,128,384]{2,1,0:T(8,128)(2,1)} %get-tuple-element.21) | copy-start | bytes 1179652
  102.4 18.6 %copy-start.13 = (bf16[384,768]{1,0:T(8,128)(2,1)S(1)}, bf16[384,768]{1,0:T(8,128)(2,1)}, u32[]{:S(2)}) copy-start(bf16[384,768]{1,0:T(8,128)(2,1)} %copy-done.12) | copy-start | bytes 1769476
  102.4 14.9 %collective-permute-start.16 = (bf16[512,384]{1,0:T(8,128)(2,1)}, bf16[512,384]{1,0:T(8,128)(2,1)S(1)}, u32[]{:S(2)}, u32[]{:S(2)}) collective-permute-start(bf16[512,384]{1,0:T(8,128)(2,1)} %bitcast.206), channel_id=1, source_target_pairs={{0,96},{1,97},{2,98},{3,99},{4,100},{5,101},{6,102},{7,103},{16,11... | collective-permute-start | bytes 1179656 | tf_op jit(solution)/shard_map/ppermute | solution.py:46
  113.6 16.4 %collective-permute-start.15 = (bf16[512,384]{1,0:T(8,128)(2,1)S(1)}, bf16[512,384]{1,0:T(8,128)(2,1)S(1)}, u32[]{:S(2)}, u32[]{:S(2)}) collective-permute-start(bf16[512,384]{1,0:T(8,128)(2,1)S(1)} %bitcast.207), channel_id=1, source_target_pairs={{0,8},{1,9},{2,10},{3,11},{4,12},{5,13},{6,14},{7,15},{16,24},{17,... | collective-permute-start | bytes 1179656 | tf_op jit(solution)/shard_map/ppermute | solution.py:46
  115.9 24.4 %collective-permute-start.18 = (bf16[512,384]{1,0:T(8,128)(2,1)S(1)}, bf16[512,384]{1,0:T(8,128)(2,1)S(1)}, u32[]{:S(2)}, u32[]{:S(2)}) collective-permute-start(bf16[512,384]{1,0:T(8,128)(2,1)S(1)} %bitcast.208), channel_id=1, source_target_pairs={{0,32},{1,33},{2,34},{3,35},{4,36},{5,37},{6,38},{7,39},{16,48},{1... | collective-permute-start | bytes 1179656 | tf_op jit(solution)/shard_map/ppermute | solution.py:46
  115.9 7.9 %copy-start.11 = (bf16[384,768]{1,0:T(8,128)(2,1)S(1)}, bf16[384,768]{1,0:T(8,128)(2,1)}, u32[]{:S(2)}) copy-start(bf16[384,768]{1,0:T(8,128)(2,1)} %copy-done.10) | copy-start | bytes 1769476
  115.9 19.1 %collective-permute-start.25 = (bf16[512,384]{1,0:T(8,128)(2,1)S(1)}, bf16[512,384]{1,0:T(8,128)(2,1)S(1)}, u32[]{:S(2)}, u32[]{:S(2)}) collective-permute-start(bf16[512,384]{1,0:T(8,128)(2,1)S(1)} %bitcast.202), channel_id=1, source_target_pairs={{0,32},{1,33},{2,34},{3,35},{4,36},{5,37},{6,38},{7,39},{16,48},{1... | collective-permute-start | bytes 1179656 | tf_op jit(solution)/shard_map/ppermute | solution.py:46
  117.3 24.4 %collective-permute-start.23 = (bf16[512,384]{1,0:T(8,128)(2,1)S(1)}, bf16[512,384]{1,0:T(8,128)(2,1)S(1)}, u32[]{:S(2)}, u32[]{:S(2)}) collective-permute-start(bf16[512,384]{1,0:T(8,128)(2,1)S(1)} %bitcast.203), channel_id=1, source_target_pairs={{0,96},{1,97},{2,98},{3,99},{4,100},{5,101},{6,102},{7,103},{16,11... | collective-permute-start | bytes 1179656 | tf_op jit(solution)/shard_map/ppermute | solution.py:46
  118.2 17.0 %collective-permute-start.17 = (bf16[512,384]{1,0:T(8,128)(2,1)S(1)}, bf16[512,384]{1,0:T(8,128)(2,1)S(1)}, u32[]{:S(2)}, u32[]{:S(2)}) collective-permute-start(bf16[512,384]{1,0:T(8,128)(2,1)S(1)} %collective-permute-done.16), channel_id=1, source_target_pairs={{0,8},{1,9},{2,10},{3,11},{4,12},{5,13},{6,14},{7,15},{16,24},{17,... | collective-permute-start | bytes 1179656 | tf_op jit(solution)/shard_map/ppermute | solution.py:46
  130.0 11.9 %collective-permute-start.22 = (bf16[512,384]{1,0:T(8,128)(2,1)S(1)}, bf16[512,384]{1,0:T(8,128)(2,1)S(1)}, u32[]{:S(2)}, u32[]{:S(2)}) collective-permute-start(bf16[512,384]{1,0:T(8,128)(2,1)S(1)} %bitcast.205), channel_id=1, source_target_pairs={{0,8},{1,9},{2,10},{3,11},{4,12},{5,13},{6,14},{7,15},{16,24},{17,... | collective-permute-start | bytes 1179656 | tf_op jit(solution)/shard_map/ppermute | solution.py:46
  135.0 9.8 %collective-permute-start.20 = (bf16[512,384]{1,0:T(8,128)(2,1)S(1)}, bf16[512,384]{1,0:T(8,128)(2,1)S(1)}, u32[]{:S(2)}, u32[]{:S(2)}) collective-permute-start(bf16[512,384]{1,0:T(8,128)(2,1)S(1)} %collective-permute-done.16), channel_id=1, source_target_pairs={{0,32},{1,33},{2,34},{3,35},{4,36},{5,37},{6,38},{7,39},{16,48},{1... | collective-permute-start | bytes 1179656 | tf_op jit(solution)/shard_map/ppermute | solution.py:46
  135.3 11.2 %collective-permute-start.27 = (bf16[512,384]{1,0:T(8,128)(2,1)S(1)}, bf16[512,384]{1,0:T(8,128)(2,1)S(1)}, u32[]{:S(2)}, u32[]{:S(2)}) collective-permute-start(bf16[512,384]{1,0:T(8,128)(2,1)S(1)} %collective-permute-done.25), channel_id=1, source_target_pairs={{0,96},{1,97},{2,98},{3,99},{4,100},{5,101},{6,102},{7,103},{16,11... | collective-permute-start | bytes 1179656 | tf_op jit(solution)/shard_map/ppermute | solution.py:46
  140.3 21.7 %collective-permute-start.26 = (bf16[512,384]{1,0:T(8,128)(2,1)S(1)}, bf16[512,384]{1,0:T(8,128)(2,1)S(1)}, u32[]{:S(2)}, u32[]{:S(2)}) collective-permute-start(bf16[512,384]{1,0:T(8,128)(2,1)S(1)} %collective-permute-done.25), channel_id=1, source_target_pairs={{0,8},{1,9},{2,10},{3,11},{4,12},{5,13},{6,14},{7,15},{16,24},{17,... | collective-permute-start | bytes 1179656 | tf_op jit(solution)/shard_map/ppermute | solution.py:46
  141.8 11.5 %collective-permute-start.19 = (bf16[512,384]{1,0:T(8,128)(2,1)S(1)}, bf16[512,384]{1,0:T(8,128)(2,1)S(1)}, u32[]{:S(2)}, u32[]{:S(2)}) collective-permute-start(bf16[512,384]{1,0:T(8,128)(2,1)S(1)} %collective-permute-done.18), channel_id=1, source_target_pairs={{0,8},{1,9},{2,10},{3,11},{4,12},{5,13},{6,14},{7,15},{16,24},{17,... | collective-permute-start | bytes 1179656 | tf_op jit(solution)/shard_map/ppermute | solution.py:46
  141.9 13.1 %collective-permute-start.24 = (bf16[512,384]{1,0:T(8,128)(2,1)S(1)}, bf16[512,384]{1,0:T(8,128)(2,1)S(1)}, u32[]{:S(2)}, u32[]{:S(2)}) collective-permute-start(bf16[512,384]{1,0:T(8,128)(2,1)S(1)} %collective-permute-done.23), channel_id=1, source_target_pairs={{0,8},{1,9},{2,10},{3,11},{4,12},{5,13},{6,14},{7,15},{16,24},{17,... | collective-permute-start | bytes 1179656 | tf_op jit(solution)/shard_map/ppermute | solution.py:46
  144.8 15.5 %collective-permute-start.21 = (bf16[512,384]{1,0:T(8,128)(2,1)S(1)}, bf16[512,384]{1,0:T(8,128)(2,1)S(1)}, u32[]{:S(2)}, u32[]{:S(2)}) collective-permute-start(bf16[512,384]{1,0:T(8,128)(2,1)S(1)} %collective-permute-done.20), channel_id=1, source_target_pairs={{0,8},{1,9},{2,10},{3,11},{4,12},{5,13},{6,14},{7,15},{16,24},{17,... | collective-permute-start | bytes 1179656 | tf_op jit(solution)/shard_map/ppermute | solution.py:46
  146.5 18.9 %collective-permute-start.28 = (bf16[512,384]{1,0:T(8,128)(2,1)S(1)}, bf16[512,384]{1,0:T(8,128)(2,1)S(1)}, u32[]{:S(2)}, u32[]{:S(2)}) collective-permute-start(bf16[512,384]{1,0:T(8,128)(2,1)S(1)} %collective-permute-done.27), channel_id=1, source_target_pairs={{0,8},{1,9},{2,10},{3,11},{4,12},{5,13},{6,14},{7,15},{16,24},{17,... | collective-permute-start | bytes 1179656 | tf_op jit(solution)/shard_map/ppermute | solution.py:46
  168.5 24.9 %all-to-all-start.2 = ((bf16[8,128,768]{2,1,0:T(8,128)(2,1)}), bf16[8,128,768]{2,1,0:T(8,128)(2,1)}, u32[]{:S(2)}, u32[]{:S(2)}) async-start(bf16[8,128,768]{2,1,0:T(8,128)(2,1)} %pad_maximum_fusion.1), calls=%async_computation.2 | async-start | bytes 3145728 | tf_op jit(solution)/shard_map/all_to_all | solution.py:359
  173.1 8.0 %collective-permute-start.29 = (f32[128,384]{1,0:T(8,128)S(1)}, f32[128,384]{1,0:T(8,128)S(1)}, u32[]{:S(2)}, u32[]{:S(2)}) collective-permute-start(f32[128,384]{1,0:T(8,128)S(1)} %slice_select_fusion), channel_id=1, source_target_pairs={{0,16},{16,0},{1,17},{17,1},{2,18},{18,2},{3,19},{19,3},{4,20},{20... | collective-permute-start | bytes 589832 | tf_op jit(solution)/shard_map/ppermute | solution.py:356
  (11 other events, 20.1 us)
